TPU v7x, 32 devices: a whole 2x2x4 slice. The times are simulated.
32 devices in a mesh: dp: 8 (over z, x), fsdp: 4 (over y, core).
Axes of the slice: x: 2, y: 2, z: 4, core: 2. Of those that a mesh axis runs over, the one named last changes fastest.
Arguments:
- tokens: bfloat16 [32768, 768], P(('dp', 'fsdp')), may hold values from -6 to 6
- lengths: int32 [64, 4], P(('dp', 'fsdp')), may hold values from 1 to 192, 512 in all within a row
- exit_layers: int32 [64, 4], P(('dp', 'fsdp')), may hold values from 3 to 6
- destination: int32 [32, 8], P(('dp', 'fsdp')), may hold values from 0 to 7, each once within a row
- carried_grad: bfloat16 [49152, 768], P(('dp', 'fsdp')), may hold values from -6 to 6
- logits_grad: float32 [256, 14], P(('dp', 'fsdp')), may hold values from -6 to 6
- qkv_weight: bfloat16 [768, 2304], P(('dp', 'fsdp')), may hold values from -0.21875 to 0.21875
- query_bias: bfloat16 [768], P(('dp', 'fsdp')), may hold values from -3 to 3
- value_bias: bfloat16 [768], P(('dp', 'fsdp')), may hold values from -3 to 3
- out_weight: bfloat16 [768, 768], P(('dp', 'fsdp')), may hold values from -1 to 1
- out_bias: bfloat16 [768], P(('dp', 'fsdp')), may hold values from -1.75 to 1.75
- norm1_gain: bfloat16 [768], P(('dp', 'fsdp')), may hold values from 0.5 to 1.5
- norm1_bias: bfloat16 [768], P(('dp', 'fsdp')), may hold values from -1.75 to 1.75
- up_weight: bfloat16 [768, 3072], P(('dp', 'fsdp')), may hold values from -0.21875 to 0.21875
- up_bias: bfloat16 [3072], P(('dp', 'fsdp')), may hold values from -3 to 3
- down_weight: bfloat16 [3072, 768], P(('dp', 'fsdp')), may hold values from -0.109375 to 0.109375
- down_bias: bfloat16 [768], P(('dp', 'fsdp')), may hold values from -1.75 to 1.75
- norm2_gain: bfloat16 [768], P(('dp', 'fsdp')), may hold values from 0.5 to 1.5
- norm2_bias: bfloat16 [768], P(('dp', 'fsdp')), may hold values from -1.75 to 1.75
- student_weight: bfloat16 [768, 128], P(('dp', 'fsdp')), may hold values from -0.21875 to 0.21875
- student_bias: float32 [128], replicated, may hold values from -3 to 3
- pool_query: float32 [128], replicated, may hold values from -12 to 12
- dense_weight: float32 [128, 128], replicated, may hold values from -1 to 1
- dense_bias: float32 [128], replicated, may hold values from -1.75 to 1.75
- class_weight: float32 [128, 14], replicated, may hold values from -0.5 to 0.5
- class_bias: float32 [14], replicated, may hold values from -6 to 6
Outputs:
- carried: bfloat16 [49152, 768], P(('dp', 'fsdp'))
- logits: float32 [256, 14], P(('dp', 'fsdp'))
- tokens_grad: bfloat16 [32768, 768], P(('dp', 'fsdp'))
- qkv_weight_grad: float32 [768, 2304], P(('dp', 'fsdp'))
- query_bias_grad: float32 [768], P(('dp', 'fsdp'))
- value_bias_grad: float32 [768], P(('dp', 'fsdp'))
- out_weight_grad: float32 [768, 768], P(('dp', 'fsdp'))
- out_bias_grad: float32 [768], P(('dp', 'fsdp'))
- norm1_gain_grad: float32 [768], P(('dp', 'fsdp'))
- norm1_bias_grad: float32 [768], P(('dp', 'fsdp'))
- up_weight_grad: float32 [768, 3072], P(('dp', 'fsdp'))
- up_bias_grad: float32 [3072], P(('dp', 'fsdp'))
- down_weight_grad: float32 [3072, 768], P(('dp', 'fsdp'))
- down_bias_grad: float32 [768], P(('dp', 'fsdp'))
- norm2_gain_grad: float32 [768], P(('dp', 'fsdp'))
- norm2_bias_grad: float32 [768], P(('dp', 'fsdp'))
- student_weight_grad: float32 [768, 128], P(('dp', 'fsdp'))
- student_bias_grad: float32 [128], replicated
- pool_query_grad: float32 [128], replicated
- dense_weight_grad: float32 [128, 128], replicated
- dense_bias_grad: float32 [128], replicated
- class_weight_grad: float32 [128, 14], replicated
- class_bias_grad: float32 [14], replicated
Inputs may be any that keep to these rules, and one draw needn't show every extreme that they name: In every row the 4 lengths sum to 512 and one of them is exactly 192. Each device's row names every dp index once; its entry r * 4 + k is the destination of pair k of the device's row r.
All inputs are finite; a program needn't handle non-finite values.
Results may differ from a plain program's by a relative error of at most 0.02.
The roundings to bfloat16 on the way count: a program that leaves them out, or rounds other values in their place, can miss the bound.
Values may be sent and summed in bfloat16 or wider, within the bound.
No kernel may reach another device: no remote copies, remote signals or barrier semaphores. Data moves between devices by JAX's collectives and lax.ppermute only.
A program may use at most 256 MiB of HBM per device.

v0:
```python
import math

import jax
import jax.numpy as jnp
from jax import lax
from jax.sharding import PartitionSpec as P

HD = 64
SD = 128
SH = 2
LAYER = 3
ROW = 512
MICRO = 2


highest = lax.Precision.HIGHEST
norm_eps = 1e-12
masked_value = -1e30


def narrow(value):
    return value.astype(jnp.bfloat16)


def widen(value):
    return value.astype(jnp.float32)


def matmul(left, right):
    return jnp.dot(left, right, preferred_element_type=jnp.float32)


def left_inner(left, right):
    return lax.dot_general(
        left, right, (((0,), (0,)), ((), ())), preferred_element_type=jnp.float32
    )


def right_inner(left, right):
    return lax.dot_general(
        left, right, (((1,), (1,)), ((), ())), preferred_element_type=jnp.float32
    )


def layer_norm(values, gain, shift):
    average = jnp.mean(values, axis=-1, keepdims=True)
    centered = values - average
    spread = jnp.mean(centered * centered, axis=-1, keepdims=True)
    return centered * lax.rsqrt(spread + norm_eps) * gain + shift


def gelu_exact(values):
    return jax.nn.gelu(values, approximate=False)


def student_head(
    student_rows,
    segment,
    pair_count,
    pool_query,
    dense_weight,
    dense_bias,
    class_weight,
    class_bias,
):
    token_count = student_rows.shape[0]
    head_width = SD // SH
    split_rows = student_rows.reshape(token_count, SH, head_width)
    pool_heads = pool_query.reshape(SH, head_width)
    pool_scores = jnp.einsum("tad,ad->at", split_rows, pool_heads, precision=highest) / math.sqrt(
        head_width
    )
    member = segment[None, :] == jnp.arange(pair_count, dtype=jnp.int32)[:, None]
    pool_weight = jax.nn.softmax(
        jnp.where(member[None], pool_scores[:, None, :], masked_value), axis=-1
    )
    pooled = jnp.einsum("apt,tad->pad", pool_weight, split_rows, precision=highest).reshape(
        pair_count, SD
    )
    dense = jnp.tanh(jnp.dot(pooled, dense_weight, precision=highest) + dense_bias)
    return jnp.dot(dense, class_weight, precision=highest) + class_bias


def row_pass(
    row_tokens, segment, row_cotangent, row_logit_grad, full_weights, head_weights, pair_count
):
    (
        qkv_matrix,
        out_matrix,
        up_matrix,
        down_matrix,
        student_matrix,
        query_shift,
        value_shift,
        out_shift,
        first_gain,
        first_shift,
        up_shift,
        down_shift,
        second_gain,
        second_shift,
    ) = full_weights
    student_shift, pool_query, dense_weight, dense_bias, class_weight, class_bias = head_weights
    hidden_dim = row_tokens.shape[1]
    token_count = row_tokens.shape[0]
    head_count = hidden_dim // HD
    scale = 1.0 / math.sqrt(HD)
    same_pair = segment[:, None] == segment[None, :]
    projected = matmul(row_tokens, qkv_matrix)
    query_rows = narrow(projected[:, :hidden_dim] + widen(query_shift)).reshape(
        token_count, head_count, HD
    )
    key_rows = narrow(projected[:, hidden_dim : 2 * hidden_dim]).reshape(
        token_count, head_count, HD
    )
    value_rows = narrow(projected[:, 2 * hidden_dim :] + widen(value_shift)).reshape(
        token_count, head_count, HD
    )
    scores = (
        jnp.einsum("qhd,khd->hqk", query_rows, key_rows, preferred_element_type=jnp.float32) * scale
    )
    masked = jnp.where(same_pair[None], scores, masked_value)
    top_score = jnp.max(masked, axis=-1, keepdims=True)
    exponent = jnp.exp(masked - top_score)
    totals = jnp.sum(exponent, axis=-1, keepdims=True)
    log_total = top_score + jnp.log(totals)
    probs = exponent / totals
    context = jnp.einsum(
        "hqk,khd->qhd", narrow(probs), value_rows, preferred_element_type=jnp.float32
    )
    context = narrow(context.reshape(token_count, hidden_dim))
    pre_first = widen(row_tokens) + matmul(context, out_matrix) + widen(out_shift)
    first_norm, first_pull = jax.vjp(layer_norm, pre_first, widen(first_gain), widen(first_shift))
    normed = narrow(first_norm)
    inner = matmul(normed, up_matrix) + widen(up_shift)
    activated_wide, gelu_pull = jax.vjp(gelu_exact, inner)
    activated = narrow(activated_wide)
    pre_second = widen(normed) + matmul(activated, down_matrix) + widen(down_shift)
    second_norm, second_pull = jax.vjp(
        layer_norm, pre_second, widen(second_gain), widen(second_shift)
    )
    output_rows = narrow(second_norm)
    student_rows = matmul(output_rows, student_matrix) + student_shift

    def head_logits(rows_in, query_in, dense_in, dense_shift, class_in, class_shift):
        return student_head(
            rows_in, segment, pair_count, query_in, dense_in, dense_shift, class_in, class_shift
        )

    logits, head_pull = jax.vjp(
        head_logits, student_rows, pool_query, dense_weight, dense_bias, class_weight, class_bias
    )
    head_grads = head_pull(row_logit_grad)
    student_grad = narrow(head_grads[0])
    grad_rows = row_cotangent + right_inner(student_grad, student_matrix)
    grad_second, second_gain_grad, second_shift_grad = second_pull(grad_rows)
    grad_down = narrow(grad_second)
    grad_act = right_inner(grad_down, down_matrix)
    grad_inner = narrow(gelu_pull(grad_act)[0])
    grad_normed = right_inner(grad_inner, up_matrix) + grad_second
    grad_first, first_gain_grad, first_shift_grad = first_pull(grad_normed)
    grad_branch = narrow(grad_first)
    grad_context = narrow(right_inner(grad_branch, out_matrix)).reshape(token_count, head_count, HD)
    scores_again = (
        jnp.einsum("qhd,khd->hqk", query_rows, key_rows, preferred_element_type=jnp.float32) * scale
    )
    probs_again = jnp.exp(jnp.where(same_pair[None], scores_again, masked_value) - log_total)
    grad_probs = jnp.einsum(
        "qhd,khd->hqk", grad_context, value_rows, preferred_element_type=jnp.float32
    )
    grad_value = jnp.einsum(
        "hqk,qhd->khd", narrow(probs_again), grad_context, preferred_element_type=jnp.float32
    )
    grad_scores = narrow(
        probs_again * (grad_probs - jnp.sum(probs_again * grad_probs, axis=-1, keepdims=True))
    )
    grad_query = (
        jnp.einsum("hqk,khd->qhd", grad_scores, key_rows, preferred_element_type=jnp.float32)
        * scale
    )
    grad_key = (
        jnp.einsum("hqk,qhd->khd", grad_scores, query_rows, preferred_element_type=jnp.float32)
        * scale
    )
    grad_projected = narrow(
        jnp.concatenate(
            [
                grad_query.reshape(token_count, hidden_dim),
                grad_key.reshape(token_count, hidden_dim),
                grad_value.reshape(token_count, hidden_dim),
            ],
            axis=1,
        )
    )
    grad_tokens = narrow(right_inner(grad_projected, qkv_matrix) + grad_first)
    weight_grads = (
        left_inner(row_tokens, grad_projected),
        left_inner(context, grad_branch),
        left_inner(normed, grad_inner),
        left_inner(activated, grad_down),
        left_inner(output_rows, student_grad),
        jnp.sum(widen(grad_projected[:, :hidden_dim]), axis=0),
        jnp.sum(widen(grad_projected[:, 2 * hidden_dim :]), axis=0),
        jnp.sum(widen(grad_branch), axis=0),
        first_gain_grad,
        first_shift_grad,
        jnp.sum(widen(grad_inner), axis=0),
        jnp.sum(widen(grad_down), axis=0),
        second_gain_grad,
        second_shift_grad,
    )
    head_out = (
        jnp.sum(widen(student_grad), axis=0),
        head_grads[1],
        head_grads[2],
        head_grads[3],
        head_grads[4],
        head_grads[5],
    )
    return (output_rows, logits, grad_tokens, weight_grads, head_out)


def local(
    tokens,
    lengths,
    exit_layers,
    destination,
    carried_grad,
    logits_grad,
    qkv_weight,
    query_bias,
    value_bias,
    out_weight,
    out_bias,
    norm1_gain,
    norm1_bias,
    up_weight,
    up_bias,
    down_weight,
    down_bias,
    norm2_gain,
    norm2_bias,
    student_weight,
    student_bias,
    pool_query,
    dense_weight,
    dense_bias,
    class_weight,
    class_bias,
):
    dp_count = lax.axis_size("dp")
    pair_count = lengths.shape[1]
    slot_width = carried_grad.shape[0] // dp_count
    place = jnp.arange(ROW, dtype=jnp.int32)
    pair_ids = jnp.arange(pair_count, dtype=jnp.int32)
    ends = jnp.cumsum(lengths, axis=1)
    starts = ends - lengths
    alive = (exit_layers > LAYER).astype(jnp.int32)
    targets = destination.reshape(MICRO, pair_count)
    returned = lax.all_to_all(carried_grad, "dp", split_axis=0, concat_axis=0, tiled=True)
    head_weights = (student_bias, pool_query, dense_weight, dense_bias, class_weight, class_bias)
    totals = None
    head_totals = None
    output_parts = []
    logit_parts = []
    token_grad_parts = []
    for batch_index in range(MICRO):
        full_weights = (
            lax.all_gather(qkv_weight, ("dp", "fsdp"), axis=0, tiled=True),
            lax.all_gather(out_weight, ("dp", "fsdp"), axis=0, tiled=True),
            lax.all_gather(up_weight, ("dp", "fsdp"), axis=0, tiled=True),
            lax.all_gather(down_weight, ("dp", "fsdp"), axis=0, tiled=True),
            lax.all_gather(student_weight, ("dp", "fsdp"), axis=0, tiled=True),
            lax.all_gather(query_bias, ("dp", "fsdp"), axis=0, tiled=True),
            lax.all_gather(value_bias, ("dp", "fsdp"), axis=0, tiled=True),
            lax.all_gather(out_bias, ("dp", "fsdp"), axis=0, tiled=True),
            lax.all_gather(norm1_gain, ("dp", "fsdp"), axis=0, tiled=True),
            lax.all_gather(norm1_bias, ("dp", "fsdp"), axis=0, tiled=True),
            lax.all_gather(up_bias, ("dp", "fsdp"), axis=0, tiled=True),
            lax.all_gather(down_bias, ("dp", "fsdp"), axis=0, tiled=True),
            lax.all_gather(norm2_gain, ("dp", "fsdp"), axis=0, tiled=True),
            lax.all_gather(norm2_bias, ("dp", "fsdp"), axis=0, tiled=True),
        )
        row_tokens = tokens[batch_index * ROW : (batch_index + 1) * ROW]
        segment = jnp.sum((place[:, None] >= ends[batch_index][None, :]).astype(jnp.int32), axis=1)
        member = (segment[:, None] == pair_ids[None, :]).astype(jnp.int32)
        token_start = jnp.sum(member * starts[batch_index][None, :], axis=1)
        token_target = jnp.sum(member * targets[batch_index][None, :], axis=1)
        token_alive = jnp.sum(member * alive[batch_index][None, :], axis=1)
        slot_index = token_target * slot_width + place - token_start
        row_cotangent = jnp.where(token_alive[:, None] > 0, widen(returned[slot_index]), 0.0)
        row_logit_grad = logits_grad[batch_index * pair_count : (batch_index + 1) * pair_count]
        output_rows, logits, grad_tokens, weight_grads, head_grads = row_pass(
            row_tokens,
            segment,
            row_cotangent,
            row_logit_grad,
            full_weights,
            head_weights,
            pair_count,
        )
        totals = (
            tuple(weight_grads)
            if totals is None
            else tuple((left + right for left, right in zip(totals, weight_grads)))
        )
        head_totals = (
            head_grads
            if head_totals is None
            else tuple((left + right for left, right in zip(head_totals, head_grads)))
        )
        output_parts.append(output_rows)
        logit_parts.append(logits)
        token_grad_parts.append(grad_tokens)
    totals = (
        lax.psum_scatter(totals[0], ("dp", "fsdp"), scatter_dimension=0, tiled=True),
        lax.psum_scatter(totals[1], ("dp", "fsdp"), scatter_dimension=0, tiled=True),
        lax.psum_scatter(totals[2], ("dp", "fsdp"), scatter_dimension=0, tiled=True),
        lax.psum_scatter(totals[3], ("dp", "fsdp"), scatter_dimension=0, tiled=True),
        lax.psum_scatter(totals[4], ("dp", "fsdp"), scatter_dimension=0, tiled=True),
        lax.psum_scatter(totals[5], ("dp", "fsdp"), scatter_dimension=0, tiled=True),
        lax.psum_scatter(totals[6], ("dp", "fsdp"), scatter_dimension=0, tiled=True),
        lax.psum_scatter(totals[7], ("dp", "fsdp"), scatter_dimension=0, tiled=True),
        lax.psum_scatter(totals[8], ("dp", "fsdp"), scatter_dimension=0, tiled=True),
        lax.psum_scatter(totals[9], ("dp", "fsdp"), scatter_dimension=0, tiled=True),
        lax.psum_scatter(totals[10], ("dp", "fsdp"), scatter_dimension=0, tiled=True),
        lax.psum_scatter(totals[11], ("dp", "fsdp"), scatter_dimension=0, tiled=True),
        lax.psum_scatter(totals[12], ("dp", "fsdp"), scatter_dimension=0, tiled=True),
        lax.psum_scatter(totals[13], ("dp", "fsdp"), scatter_dimension=0, tiled=True),
    )
    head_sums = lax.psum(
        (
            head_totals[0],
            head_totals[1],
            head_totals[2],
            head_totals[3],
            head_totals[4],
            head_totals[5],
        ),
        ("dp", "fsdp"),
    )
    all_outputs = jnp.concatenate(output_parts, axis=0)
    flat_targets = destination.reshape(-1)
    dp_ids = jnp.arange(dp_count, dtype=jnp.int32)
    chosen = (flat_targets[None, :] == dp_ids[:, None]).astype(jnp.int32)
    flat_starts = (starts + ROW * jnp.arange(MICRO, dtype=jnp.int32)[:, None]).reshape(-1)
    send_start = jnp.sum(chosen * flat_starts[None, :], axis=1)
    send_length = jnp.sum(chosen * lengths.reshape(-1)[None, :], axis=1)
    send_alive = jnp.sum(chosen * alive.reshape(-1)[None, :], axis=1)
    slot_place = jnp.arange(slot_width, dtype=jnp.int32)
    valid = (slot_place[None, :] < send_length[:, None]) & (send_alive[:, None] > 0)
    source_index = jnp.where(valid, send_start[:, None] + slot_place[None, :], 0).reshape(-1)
    outgoing = jnp.where(
        valid.reshape(-1)[:, None], all_outputs[source_index], jnp.zeros((), jnp.bfloat16)
    )
    carried = lax.all_to_all(outgoing, "dp", split_axis=0, concat_axis=0, tiled=True)
    logits_all = jnp.concatenate(logit_parts, axis=0)
    tokens_grad = jnp.concatenate(token_grad_parts, axis=0)
    return (
        carried,
        logits_all,
        tokens_grad,
        totals[0],
        totals[5],
        totals[6],
        totals[1],
        totals[7],
        totals[8],
        totals[9],
        totals[2],
        totals[10],
        totals[3],
        totals[11],
        totals[12],
        totals[13],
        totals[4],
        head_sums[0],
        head_sums[1],
        head_sums[2],
        head_sums[3],
        head_sums[4],
        head_sums[5],
    )


def solution(mesh):
    return jax.shard_map(
        local,
        mesh=mesh,
        in_specs=(
            P(("dp", "fsdp"), None),
            P(("dp", "fsdp"), None),
            P(("dp", "fsdp"), None),
            P(("dp", "fsdp"), None),
            P(("dp", "fsdp"), None),
            P(("dp", "fsdp"), None),
            P(("dp", "fsdp"), None),
            P(("dp", "fsdp")),
            P(("dp", "fsdp")),
            P(("dp", "fsdp"), None),
            P(("dp", "fsdp")),
            P(("dp", "fsdp")),
            P(("dp", "fsdp")),
            P(("dp", "fsdp"), None),
            P(("dp", "fsdp")),
            P(("dp", "fsdp"), None),
            P(("dp", "fsdp")),
            P(("dp", "fsdp")),
            P(("dp", "fsdp")),
            P(("dp", "fsdp"), None),
            P(),
            P(),
            P(),
            P(),
            P(),
            P(),
        ),
        out_specs=(
            P(("dp", "fsdp"), None),
            P(("dp", "fsdp"), None),
            P(("dp", "fsdp"), None),
            P(("dp", "fsdp"), None),
            P(("dp", "fsdp")),
            P(("dp", "fsdp")),
            P(("dp", "fsdp"), None),
            P(("dp", "fsdp")),
            P(("dp", "fsdp")),
            P(("dp", "fsdp")),
            P(("dp", "fsdp"), None),
            P(("dp", "fsdp")),
            P(("dp", "fsdp"), None),
            P(("dp", "fsdp")),
            P(("dp", "fsdp")),
            P(("dp", "fsdp")),
            P(("dp", "fsdp"), None),
            P(),
            P(),
            P(),
            P(),
            P(),
            P(),
        ),
        check_vma=False,
    )
```

profile of v0, /device:TPU:0, one launch (start us, length us, event | category | flops | bytes accessed | tf_op | source)
XLA Modules:
  0.0 1140.7 jit_solution(3663396438205528054)
XLA Ops:
  9.6 7.3 all-to-all-start.1
  20.9 77.3 %all-reduce.20 = (bf16[768]{0:T(1024)(128)(2,1)S(1)}, bf16[768]{0:T(1024)(128)(2,1)S(1)}, bf16[768]{0:T(1024)(128)(2,1)S(1)}, bf16[768]{0:T(1024)(128)(2,1)S(1)}...) all-reduce(bf16[768]{0:T(1024)(128)(2,1)S(1)} %dynamic-update-slice, ...), channel_id=1, replica_groups=mesh['dp'=8,'fsdp'=4] {'dp','fsdp'}, use_global_device_ids=true, to_apply=%add | all-reduce | flops 9216 | bytes 36864
  100.3 44.0 %all_gather.69 = bf16[768,128]{1,0:T(8,128)(2,1)} all-gather(bf16[24,128]{1,0:T(8,128)(2,1)S(1)} %copy-done.125), channel_id=1, replica_groups=mesh['dp'=8,'fsdp'=4] {'dp','fsdp'}, dimensions={0}, use_global_device_ids=true | all-gather | bytes 202752 | tf_op jit(solution)/shard_map/all_gather | solution.py:273
  197.9 23.6 %all-gather.9.cloned.1.call-done = bf16[768,3072]{1,0:T(8,128)(2,1)} async-done(((bf16[24,3072]{1,0:T(8,128)(2,1)}), bf16[768,3072]{1,0:T(8,128)(2,1)}) %all-gather.9.cloned.1.call-update) | async-done | bytes 4718608 | tf_op jit(solution)/shard_map/all_gather | solution.py:271
  228.8 33.9 %multiply_convert_fusion.3 = (bf16[512,3072]{1,0:T(8,128)(2,1)}, f32[512,3072]{1,0:T(8,128)}, bf16[512,3072]{1,0:T(8,128)(2,1)}, f32[512,3072]{1,0:T(8,128)}, f32[512,3072]{1,0:T(8,128)}) fusion(f32[3072]{0:T(1024)S(1)} %convert_element_type.234, f32[512,3072]{1,0:T(8,128)S(1)} %fusion.126, bf16[512,768]{1,0:T(8,128)(2,1)S(1)} %get-tuple-element.199, ...), kind=kOutput, calls=%fused_computation.45 | convolution fusion | flops 2623537152 | bytes 36974592 | tf_op jit(solution)/shard_map/dot_general | solution.py:30
  262.7 24.0 %all-gather.11.cloned.1.call-done = bf16[3072,768]{1,0:T(8,128)(2,1)} async-done(((bf16[96,768]{1,0:T(8,128)(2,1)}), bf16[3072,768]{1,0:T(8,128)(2,1)}) %all-gather.11.cloned.1.call-update) | async-done | bytes 4718608 | tf_op jit(solution)/shard_map/all_gather | solution.py:272
  286.7 6.1 fusion.123
  343.7 17.9 %convert_reduce_fusion.1 = (f32[3072]{0:T(1024)S(1)}, bf16[512,3072]{1,0:T(8,128)(2,1)}, f32[3072]{0:T(1024)}, bf16[512,3072]{1,0:T(8,128)(2,1)}) fusion(f32[512,3072]{1,0:T(8,128)} %get-tuple-element.184, f32[512,3072]{1,0:T(8,128)} %get-tuple-element.231, f32[3072]{0:T(1024)S(1)} %copy-done.121, f32[512,3072]{1,0:T(8,128)} %fusion.131, ...), kind=kOutput, calls=%fused_computation.27 | convolution fusion | flops 2469390336 | bytes 43290624 | tf_op jit(solution)/shard_map/dot_general | solution.py:40
  361.6 6.1 add_add_fusion.8
  367.8 6.4 multiply_reduce_fusion.5
  382.9 7.6 fusion.30
  390.5 9.9 multiply_reduce_fusion.1
  410.3 13.2 %multiply_convert_fusion.1 = bf16[12,512,512]{1,2,0:T(8,128)(2,1)} fusion(f32[12,512,512]{1,2,0:T(8,128)} %get-tuple-element.245, f32[12,512]{1,0:T(8,128)S(1)} %get-tuple-element.244, f32[12,512]{1,0:T(8,128)S(1)} %copy-done.69, f32[12,512,512]{1,2,0:T(8,128)} %copy-done.3, pred[512,512]{0,1:T(8,128)(4,1)S(1)} %copy-done.26), kind=kLoop, calls=%fused_computation.6 | loop fusion | flops 18874368 | bytes 31768576 | tf_op jit(solution)/shard_map/convert_element_type | solution.py:22
  429.6 13.7 %multiply_reduce_fusion = (f32[12,512]{1,0:T(8,128)S(1)}, f32[12,512,512]{1,2,0:T(8,128)}) fusion(f32[12,512]{1,0:T(8,128)S(1)} %copy-done.68, f32[12,512,512]{1,2,0:T(8,128)} %copy-done.2, pred[512,512]{0,1:T(8,128)(4,1)S(1)} %copy-done.24, bf16[512,12,64]{0,2,1:T(8,128)(2,1)} %bitcast.257, bf16[512,12,64]{0,2,1:T(8,128)(2,1)} %bitcast.254), kind=kOutput, calls=%fused_computation.4 | convolution fusion | flops 418375680 | bytes 27049984 | tf_op jit(solution)/shard_map/qhd,khd->hqk/dot_general | solution.py:168
  443.4 10.2 multiply_convert_fusion
  465.2 6.1 add_bitcast_fusion
  471.3 8.1 copy.154
  503.4 5.6 gather_fusion
  523.6 68.2 %all-reduce.19 = (f32[768]{0:T(1024)S(1)}, f32[768]{0:T(1024)S(1)}, f32[768]{0:T(1024)S(1)}, f32[768]{0:T(1024)S(1)}, f32[768]{0:T(1024)S(1)}, /*index=5*/f32[30...) all-reduce(f32[768]{0:T(1024)S(1)} %add.482, ...), channel_id=3, replica_groups=mesh['dp'=8,'fsdp'=4] {'dp','fsdp'}, use_global_device_ids=true, to_apply=%region_45.46.clone | all-reduce | flops 11406 | bytes 91248
  606.7 12.3 %reduce-scatter.18.cloned.1.call-done = f32[24,128]{1,0:T(8,128)} async-done(((f32[768,128]{1,0:T(8,128)}), f32[24,128]{1,0:T(8,128)}) %reduce-scatter.18.cloned.1.call-update) | async-done | bytes 12304
  619.0 104.9 %reduce-scatter.10.cloned.1.call-done = f32[24,768]{1,0:T(8,128)} async-done(((f32[768,768]{1,0:T(8,128)}), f32[24,768]{1,0:T(8,128)}) %reduce-scatter.10.cloned.1.call-update) | async-done | bytes 73744 | tf_op jit(solution)/shard_map/reduce_scatter | solution.py:317
  723.9 124.4 %reduce-scatter.16.cloned.1.call-done = f32[24,2304]{1,0:T(8,128)} async-done(((f32[768,2304]{1,0:T(8,128)}), f32[24,2304]{1,0:T(8,128)}) %reduce-scatter.16.cloned.1.call-update) | async-done | bytes 221200
  848.2 142.2 %reduce-scatter.14.cloned.1.call-done = f32[96,768]{1,0:T(8,128)} async-done(((f32[3072,768]{1,0:T(8,128)}), f32[96,768]{1,0:T(8,128)}) %reduce-scatter.14.cloned.1.call-update) | async-done | bytes 294928 | tf_op jit(solution)/shard_map/reduce_scatter | solution.py:319
  990.4 141.1 %reduce-scatter.12.cloned.1.call-done = f32[24,3072]{1,0:T(8,128)} async-done(((f32[768,3072]{1,0:T(8,128)}), f32[24,3072]{1,0:T(8,128)}) %reduce-scatter.12.cloned.1.call-update) | async-done | bytes 294928 | tf_op jit(solution)/shard_map/reduce_scatter | solution.py:318
  (600 shorter events, 210.0 us)
Async XLA Ops:
  7.2 293.0 %copy-start = (f32[128,128]{1,0:T(8,128)S(1)}, f32[128,128]{1,0:T(8,128)}, u32[]{:S(2)}) copy-start(f32[128,128]{1,0:T(8,128)} %param.48) | copy-start | bytes 196612
  7.3 92.8 %copy-start.140 = (s32[2,4]{1,0:T(2,128)S(1)}, s32[2,4]{1,0:T(2,128)}, u32[]{:S(2)}) copy-start(s32[2,4]{1,0:T(2,128)} %param.27) | copy-start | bytes 100
  7.3 92.9 %copy-start.125 = (bf16[24,128]{1,0:T(8,128)(2,1)S(1)}, bf16[24,128]{1,0:T(8,128)(2,1)}, u32[]{:S(2)}) copy-start(bf16[24,128]{1,0:T(8,128)(2,1)} %param.45) | copy-start | bytes 18436
  7.3 137.0 %copy-start.147 = (s32[2,4]{1,0:T(2,128)S(1)}, s32[2,4]{1,0:T(2,128)}, u32[]{:S(2)}) copy-start(s32[2,4]{1,0:T(2,128)} %param.28) | copy-start | bytes 100
  7.3 137.6 %copy-start.126 = (s32[1,8]{1,0:T(1,128)S(1)}, s32[1,8]{1,0:T(1,128)}, u32[]{:S(2)}) copy-start(s32[1,8]{1,0:T(1,128)} %param.29) | copy-start | bytes 100
  7.4 146.0 %all-gather.5.cloned.1.call-start = ((), (), s32[]{:S(2)}) async-start(), calls=%async_computation.7 | async-start | bytes 3649536 | tf_op jit(solution)/shard_map/all_gather | solution.py:269
  8.1 168.3 %all-gather.7.cloned.1.call-start = ((), (), s32[]{:S(2)}) async-start(), calls=%async_computation.8 | async-start | bytes 1216512 | tf_op jit(solution)/shard_map/all_gather | solution.py:270
  8.8 212.6 %all-gather.9.cloned.1.call-start = ((), (), s32[]{:S(2)}) async-start(), calls=%async_computation.9 | async-start | bytes 4866048 | tf_op jit(solution)/shard_map/all_gather | solution.py:271
  9.6 138.4 %all-to-all-start.1 = ((bf16[8,192,768]{2,1,0:T(8,128)(2,1)}), bf16[8,192,768]{2,1,0:T(8,128)(2,1)S(1)}, u32[]{:S(2)}, u32[]{:S(2)}) async-start(bf16[8,192,768]{2,1,0:T(8,128)(2,1)} %bitcast.265), calls=%async_computation.1 | async-start | bytes 4718592 | tf_op jit(solution)/shard_map/all_to_all | solution.py:260
  16.8 269.8 %all-gather.11.cloned.1.call-start = ((), (), s32[]{:S(2)}) async-start(), calls=%async_computation.10 | async-start | bytes 4866048 | tf_op jit(solution)/shard_map/all_gather | solution.py:272
  17.4 589.3 %all-reduce.23.cloned.1.call-start = ((), (), s32[]{:S(2)}) async-start(), calls=%async_computation.14 | async-start | bytes 131072 | tf_op jit(solution)/shard_map/psum | solution.py:331
  98.2 98.3 %copy-start.75 = (f32[768]{0:T(1024)}, f32[768]{0:T(1024)S(1)}, u32[]{:S(2)}) copy-start(f32[768]{0:T(1024)S(1)} %convert_element_type.230) | copy-start | bytes 9220
  98.3 127.9 %copy-start.120 = (f32[3072]{0:T(1024)}, f32[3072]{0:T(1024)S(1)}, u32[]{:S(2)}) copy-start(f32[3072]{0:T(1024)S(1)} %convert_element_type.234) | copy-start | bytes 36868
  197.9 88.8 %copy-start.17 = (bf16[512,768]{1,0:T(8,128)(2,1)}, bf16[512,768]{1,0:T(8,128)(2,1)S(1)}, u32[]{:S(2)}) copy-start(bf16[512,768]{1,0:T(8,128)(2,1)S(1)} %get-tuple-element.200) | copy-start | bytes 2359300
  401.4 217.7 %reduce-scatter.18.cloned.1.call-start = ((), (), s32[]{:S(2)}) async-start(), calls=%async_computation.16 | async-start | bytes 405504
  404.4 319.5 %reduce-scatter.10.cloned.1.call-start = ((), (), s32[]{:S(2)}) async-start(), calls=%async_computation.11 | async-start | bytes 2433024 | tf_op jit(solution)/shard_map/reduce_scatter | solution.py:317
  429.5 418.7 %reduce-scatter.16.cloned.1.call-start = ((), (), s32[]{:S(2)}) async-start(), calls=%async_computation.15 | async-start | bytes 7299072
  479.4 511.0 %reduce-scatter.14.cloned.1.call-start = ((), (), s32[]{:S(2)}) async-start(), calls=%async_computation.13 | async-start | bytes 9732096 | tf_op jit(solution)/shard_map/reduce_scatter | solution.py:319
  490.7 640.8 %reduce-scatter.12.cloned.1.call-start = ((), (), s32[]{:S(2)}) async-start(), calls=%async_computation.12 | async-start | bytes 9732096 | tf_op jit(solution)/shard_map/reduce_scatter | solution.py:318
  512.5 84.5 %copy-start.72 = (f32[128,14]{0,1:T(8,128)S(1)}, f32[128,14]{0,1:T(8,128)}, u32[]{:S(2)}) copy-start(f32[128,14]{0,1:T(8,128)} %param.50) | copy-start | bytes 21508
  512.5 85.3 %copy-start.124 = (f32[512]{0:T(512)S(1)}, f32[512]{0:T(512)}, u32[]{:S(2)}) copy-start(f32[512]{0:T(512)} %copy-done.123) | copy-start | bytes 6148
  512.5 94.2 %all-to-all-start = ((bf16[8,192,768]{2,1,0:T(8,128)(2,1)}), bf16[8,192,768]{2,1,0:T(8,128)(2,1)S(1)}, u32[]{:S(2)}, u32[]{:S(2)}) async-start(bf16[8,192,768]{2,1,0:T(8,128)(2,1)} %broadcast_select_fusion), calls=%async_computation | async-start | bytes 4718592 | tf_op jit(solution)/shard_map/all_to_all | solution.py:356
  603.3 530.2 %copy-start.1 = (f32[128,128]{1,0:T(8,128)S(1)}, f32[128,128]{1,0:T(8,128)}, u32[]{:S(2)}) copy-start(f32[128,128]{1,0:T(8,128)} %param.48) | copy-start | bytes 196612
  606.7 526.2 %copy-start.74 = (f32[128,128]{1,0:T(8,128)S(1)}, f32[128,128]{1,0:T(8,128)}, u32[]{:S(2)}) copy-start(f32[128,128]{1,0:T(8,128)} %all-reduce.23.cloned.1.call-done) | copy-start | bytes 196612
  (165 other events, 1361.1 us)
Sparse Core Ops, SparseCore 0:
  11.1 89.0 all-gather.4
  103.1 52.8 all-gather.6
  158.9 62.5 all-gather.8
  224.2 62.3 all-gather.10
  401.5 116.3 all-reduce.22
  523.3 95.7 reduce-scatter.17
  625.7 98.1 reduce-scatter.9
  730.1 118.0 reduce-scatter.15
  855.7 134.6 reduce-scatter.13
  996.8 134.7 reduce-scatter.11
where the time goes:
time: 1150 us; the launch traced here: 1140 us
  waiting for transfers between devices  575 us (50%)
  matrix products  220 us (19%)
  blocking collectives  189 us (16%)
  other arithmetic  66.1 us (6%)
  local copies, waits for them, and re-layouts  60.6 us (5%)
  between operations  16.8 us (1%)
  starting transfers between devices  12.3 us (1%)
    unnamed x2, blocking collectives  145 us
    reduce_scatter x1, waiting for transfers between devices, local(): lax.psum_scatter(totals[3], ('dp', 'fsdp'), scatter_dimension=0, tiled=True)  142 us
    reduce_scatter x1, waiting for transfers between devices, local(): lax.psum_scatter(totals[2], ('dp', 'fsdp'), scatter_dimension=0, tiled=True)  141 us
    unnamed x12, waiting for transfers between devices  139 us
    reduce_scatter x1, waiting for transfers between devices, local(): lax.psum_scatter(totals[1], ('dp', 'fsdp'), scatter_dimension=0, tiled=True)  105 us
    dot_general x10, matrix products, matmul(): return jnp.dot(left, right, preferred_element_type=jnp.float32)  59.5 us
    dot_general x10, matrix products, right_inner(): lax.dot_general(left, right, (((1,), (1,)), ((), ())), preferred_element_...  50.2 us
    all_gather x1, blocking collectives, local(): lax.all_gather(student_weight, ('dp', 'fsdp'), axis=0, tiled=True)  44 us
  transfers between devices with their start and end apart: 12, of which 7 were waited for; matrix products, arithmetic and copies ran while one was open for 19% of the time, Pallas kernels for 0%

commit v1 on v0

v1 whole, which is shorter than its diff:
```python
import functools
import math

import jax
import jax.numpy as jnp
from jax import lax
from jax.experimental import pallas as pl
from jax.experimental.pallas import tpu as pltpu
from jax.sharding import Mesh
from jax.sharding import PartitionSpec as P

HD = 64
SD = 128
SH = 2
LAYER = 3
ROW = 512
MICRO = 2
LANES = 128

BF16 = jnp.bfloat16
F32 = jnp.float32
highest = lax.Precision.HIGHEST
norm_eps = 1e-12
masked_value = -1e30

tail_scale = 0.425
tail_terms = (
    0.2397720031195156,
    0.2404005560164679,
    0.20920268278012027,
    0.22961437095935636,
    -0.06054995293320506,
    0.3670545366443018,
    -0.292749557721544,
    0.06725537014453116,
)

QUERY_BIAS, VALUE_BIAS, OUT_BIAS, GAIN1, BIAS1, DOWN_BIAS, GAIN2, BIAS2, UP_BIAS = range(9)


def narrow(value):
    return value.astype(BF16)


def widen(value):
    return value.astype(F32)


def matmul(left, right, precision=None):
    return lax.dot_general(
        left, right, (((1,), (0,)), ((), ())), preferred_element_type=F32, precision=precision
    )


def left_inner(left, right, precision=None):
    return lax.dot_general(
        left, right, (((0,), (0,)), ((), ())), preferred_element_type=F32, precision=precision
    )


def right_inner(left, right, precision=None):
    return lax.dot_general(
        left, right, (((1,), (1,)), ((), ())), preferred_element_type=F32, precision=precision
    )


def params(*semantics, limit=58):
    return pltpu.CompilerParams(
        dimension_semantics=semantics or None, vmem_limit_bytes=limit * 1024 * 1024
    )


def cost(flops, nbytes, transcendentals=0):
    return pl.CostEstimate(
        flops=int(flops), bytes_accessed=int(nbytes), transcendentals=int(transcendentals)
    )


def fixed(shape, *at):
    where = at or (0,) * len(shape)
    return pl.BlockSpec(shape, lambda *_: where)


class Layout:
    def __init__(self, mesh):
        dp, fsdp = mesh.shape["dp"], mesh.shape["fsdp"]
        devices = mesh.devices
        if (dp, fsdp) == (8, 4):
            self.mesh = Mesh(devices.reshape(4, 2, 2, 2), ("z", "x", "y", "core"))
            self.dp = ("z", "x")
            self.stages = (("core",), ("x", "y"), ("z",))
        elif (dp, fsdp) == (64, 4):
            self.mesh = Mesh(devices.reshape(8, 4, 2, 4), ("z", "x", "core", "y"))
            self.dp = ("z", "x", "core")
            self.stages = (("core",), ("x", "y"), ("z",))
        else:
            self.mesh = mesh
            self.dp = ("dp",)
            self.stages = (("fsdp",), ("dp",))
        self.axes = tuple(self.mesh.axis_names)
        self.sizes = tuple(self.mesh.shape[name] for name in self.axes)
        self.count = math.prod(self.sizes)
        self.dp_count = dp
        self.extents = tuple(math.prod(self.mesh.shape[n] for n in stage) for stage in self.stages)
        order = [self.axes.index(name) for stage in self.stages for name in stage]
        self.place = []
        for device in range(self.count):
            at, rest = [], device
            for size in reversed(self.sizes):
                at.append(rest % size)
                rest //= size
            at = at[::-1]
            position = 0
            for axis in order:
                position = position * self.sizes[axis] + at[axis]
            self.place.append(position)
        self.device_at = [self.place.index(i) for i in range(self.count)]

    def exchange(self, value, stage):
        extent = self.extents[stage]
        value = value.reshape((extent, value.shape[0] // extent) + value.shape[1:])
        return lax.all_to_all(
            value, self.stages[stage], split_axis=0, concat_axis=0, tiled=True
        )

    def scatter_sum(self, value):
        for stage in range(len(self.stages)):
            value = jnp.sum(widen(self.exchange(narrow(value), stage)), axis=0)
        return value[0]


def store_parts(ref, value, place, column):
    count, part, _ = ref.shape
    width = value.shape[1]
    value = value.astype(ref.dtype) if part % 16 == 0 else value
    for device in range(count):
        ref[place[device], :, pl.ds(column, width)] = value[
            device * part : (device + 1) * part
        ].astype(ref.dtype)


class Sums:
    def __init__(self, layout, rows):
        self.layout = layout
        self.count, self.part = layout.count, rows // layout.count
        self.split = self.part % 8 == 0

    def shape(self, columns):
        if self.split:
            return jax.ShapeDtypeStruct((self.count, self.part, columns), BF16)
        return jax.ShapeDtypeStruct((self.count * self.part, columns), BF16)

    def spec(self, columns):
        return fixed(self.shape(columns).shape)

    def store(self, ref, value, column):
        if self.split:
            store_parts(ref, value, self.layout.place, column)
        else:
            ref[:, pl.ds(column, value.shape[1])] = value.astype(ref.dtype)

    def parts(self, value):
        if self.split:
            return value
        value = value.reshape(self.count, self.part, value.shape[1])
        return value[jnp.asarray(self.layout.device_at)]


def interleave(width, ratio, dtype):
    size = width * ratio
    source = lax.broadcasted_iota(jnp.int32, (size, size), 0)
    target = lax.broadcasted_iota(jnp.int32, (size, size), 1)
    return (source == (target % width) * ratio + target // width).astype(dtype)


def pack_body(qkv, out, up, down, student, columns, packed, *, ratio, hidden):
    part = qkv.shape[0]
    packed[:, : 3 * hidden] = qkv[...]
    packed[:, 3 * hidden : 4 * hidden] = out[...]
    base = 4 * hidden
    mix = interleave(LANES, ratio, BF16)
    for chunk in range(hidden // LANES):
        piece = narrow(
            matmul(up[:, chunk * ratio * LANES : (chunk + 1) * ratio * LANES], mix)
        )
        for j in range(ratio):
            at = base + j * hidden + chunk * LANES
            packed[:, at : at + LANES] = piece[:, j * LANES : (j + 1) * LANES]
    base += ratio * hidden
    row = lax.broadcasted_iota(jnp.int32, (part, part * ratio), 0)
    column = lax.broadcasted_iota(jnp.int32, (part, part * ratio), 1)
    for j in range(ratio):
        pick = (column == row * ratio + j).astype(BF16)
        packed[:, base + j * hidden : base + (j + 1) * hidden] = narrow(matmul(pick, down[...]))
    base += ratio * hidden
    packed[:, base : base + SD] = student[...]
    packed[:, base + SD :] = columns[...]


def turned(vectors):
    return widen(vectors).T


def attention_body(
    tokens, seg_column, seg_row, wq, wk, wv, vectors, query, key, value, context, mask, rows
):
    step = pl.program_id(1)
    width = wq.shape[1]

    @pl.when((step == 0) & (pl.program_id(0) == 0))
    def _():
        rows[...] = turned(vectors[...])

    @pl.when(step == 0)
    def _():
        mask[...] = jnp.where(seg_column[0] == seg_row[0], 0.0, masked_value)

    here = pl.ds(pl.multiple_of(step * width, width), width)
    x = tokens[...]
    q = narrow(matmul(x, wq[...]) + rows[QUERY_BIAS : QUERY_BIAS + 1, here])
    k = narrow(matmul(x, wk[...]))
    v = narrow(matmul(x, wv[...]) + rows[VALUE_BIAS : VALUE_BIAS + 1, here])
    query[...] = q
    key[...] = k
    value[...] = v
    lane = lax.broadcasted_iota(jnp.int32, (x.shape[0], LANES), 1)
    scale = BF16(1.0 / math.sqrt(HD))
    for block in range(width // LANES):
        cut = slice(block * LANES, (block + 1) * LANES)
        q_block, k_block, v_turned = q[:, cut] * scale, k[:, cut], v[:, cut].T
        parts = []
        for head in range(LANES // HD):
            mine = (lane >= head * HD) & (lane < (head + 1) * HD)
            scores = right_inner(k_block, jnp.where(mine, q_block, BF16(0))) + mask[...]
            exponent = jnp.exp(scores - jnp.max(scores, axis=0, keepdims=True))
            total = jnp.sum(exponent, axis=0, keepdims=True)
            probs = narrow(exponent * (1.0 / total))
            parts.append(matmul(v_turned[head * HD : (head + 1) * HD], probs))
        context[:, cut] = narrow(jnp.concatenate(parts, axis=0)).T


def attention_grad_body(
    branch, seg_column, seg_row, query, key, value, out_weight, grads, mask
):
    width = query.shape[1]

    @pl.when(pl.program_id(1) == 0)
    def _():
        mask[...] = jnp.where(seg_column[0] == seg_row[0], 0.0, masked_value)

    grad_context = narrow(right_inner(branch[...], out_weight[...]))
    lane = lax.broadcasted_iota(jnp.int32, (branch.shape[0], LANES), 1)
    scale = 1.0 / math.sqrt(HD)
    for block in range(width // LANES):
        cut = slice(block * LANES, (block + 1) * LANES)
        q_block, k_block, v_block = query[:, cut] * BF16(scale), key[:, cut], value[:, cut]
        g_block, k_turned = grad_context[:, cut], k_block.T
        grad_q, grad_k, grad_v = [], 0.0, 0.0
        for head in range(LANES // HD):
            mine = (lane >= head * HD) & (lane < (head + 1) * HD)
            q_head = jnp.where(mine, q_block, BF16(0))
            g_head = jnp.where(mine, g_block, BF16(0))
            scores = right_inner(k_block, q_head) + mask[...]
            exponent = jnp.exp(scores - jnp.max(scores, axis=0, keepdims=True))
            total = jnp.sum(exponent, axis=0, keepdims=True)
            probs = exponent * (1.0 / total)
            grad_probs = right_inner(v_block, g_head)
            inner = jnp.sum(probs * grad_probs, axis=0, keepdims=True)
            grad_scores = narrow(probs * (grad_probs - inner))
            grad_v += matmul(narrow(probs), g_head)
            grad_k += matmul(grad_scores, q_head)
            grad_q.append(matmul(k_turned[head * HD : (head + 1) * HD], grad_scores))
        grads[0, :, cut] = narrow(jnp.concatenate(grad_q, axis=0) * scale).T
        grads[1, :, cut] = narrow(grad_k)
        grads[2, :, cut] = narrow(grad_v)


def normalize(values):
    average = jnp.mean(values, axis=-1, keepdims=True)
    centered = values - average
    spread = jnp.mean(centered * centered, axis=-1, keepdims=True)
    scale = lax.rsqrt(spread + norm_eps)
    return centered * scale, scale


def gelu_and_slope(x):
    t = 1.0 / (1.0 + (tail_scale / math.sqrt(2.0)) * jnp.abs(x))
    bell = jnp.exp(-0.5 * (x * x))
    tail = F32(0.5 * tail_terms[-1])
    for term in tail_terms[-2::-1]:
        tail = tail * t + 0.5 * term
    tail = tail * t * bell
    phi = jnp.where(x < 0.0, tail, 1.0 - tail)
    return x * phi, phi + x * (bell * (1.0 / math.sqrt(2.0 * math.pi)))


CHUNK = 256


def forward_body(
    tokens, context, out_weight, up, down, student, vectors, student_bias,
    pre_first, normed, activated, slope, pre_second, outputs, student_rows, total, rows,
):
    step = pl.program_id(0)
    count = tokens.shape[0]

    @pl.when(step == 0)
    def _():
        rows[...] = turned(vectors[...])
        for low in range(0, count, CHUNK):
            cut = slice(low, low + CHUNK)
            pre = (
                widen(tokens[cut])
                + matmul(context[cut], out_weight[...])
                + rows[OUT_BIAS : OUT_BIAS + 1]
            )
            pre_first[cut] = pre
            hat, _ = normalize(pre)
            value = narrow(hat * rows[GAIN1 : GAIN1 + 1] + rows[BIAS1 : BIAS1 + 1])
            normed[cut] = value
            total[cut] = widen(value) + rows[DOWN_BIAS : DOWN_BIAS + 1]

    bias = rows[pl.ds(UP_BIAS + step, 1)]
    for low in range(0, count, CHUNK):
        cut = slice(low, low + CHUNK)
        value, grad = gelu_and_slope(matmul(normed[cut], up[...]) + bias)
        value = narrow(value)
        activated[cut] = value
        slope[cut] = narrow(grad)
        total[cut] += matmul(value, down[...])

    @pl.when(step == pl.num_programs(0) - 1)
    def _():
        for low in range(0, count, CHUNK):
            cut = slice(low, low + CHUNK)
            pre = total[cut]
            pre_second[cut] = pre
            hat, _ = normalize(pre)
            value = narrow(hat * rows[GAIN2 : GAIN2 + 1] + rows[BIAS2 : BIAS2 + 1])
            outputs[cut] = value
            student_rows[cut] = matmul(value, student[...]) + student_bias[...]


def select_body(index, source, target):
    place = lax.broadcasted_iota(jnp.int32, (index.shape[0], source.shape[0]), 1)
    target[...] = narrow(matmul((index[...] == place).astype(BF16), source[...]))


def student_body(
    student_rows, segment, query, dense_weight, dense_bias, class_weight, class_bias, logits_grad,
    logits, student_grad, small, *, small_rows,
):
    count, _ = student_rows.shape
    pairs, classes = logits_grad.shape
    wide = -(-pairs // LANES) * LANES
    head = SD // SH
    scale = 1.0 / math.sqrt(head)
    rows = student_rows[...]
    member = segment[...] == lax.broadcasted_iota(jnp.int32, (count, wide), 1)
    one_hot = member.astype(F32)
    lane = lax.broadcasted_iota(jnp.int32, (count, SD), 1)

    def by_head(values):
        return [
            jnp.sum(
                jnp.where((lane >= a * head) & (lane < (a + 1) * head), values, 0.0),
                axis=1,
                keepdims=True,
            )
            for a in range(SH)
        ]

    def spread(columns):
        value = columns[0]
        for a in range(1, SH):
            value = jnp.where(lane >= a * head, columns[a], value)
        return jnp.broadcast_to(value, (count, SD))

    def of_pair(row):
        return jnp.sum(jnp.where(member, row, 0.0), axis=1, keepdims=True)

    def over_pair(column):
        return jnp.sum(jnp.where(member, column, 0.0), axis=0, keepdims=True)

    weights = []
    for score in by_head(rows * query[...]):
        score = score * scale
        top = jnp.max(jnp.where(member, score, masked_value), axis=0, keepdims=True)
        exponent = jnp.exp(score - of_pair(top))
        weights.append(exponent / of_pair(over_pair(exponent)))
    weight = spread(weights)
    pooled = left_inner(one_hot, weight * rows, highest)
    dense = jnp.tanh(matmul(pooled, dense_weight[...], highest) + dense_bias[...])
    logits[...] = matmul(dense[:pairs], class_weight[...], highest) + class_bias[...]

    grad = logits_grad[...]
    grad_pre = right_inner(grad, class_weight[...], highest) * (
        1.0 - dense[:pairs] * dense[:pairs]
    )
    small[...] = jnp.zeros_like(small)
    small[:SD] = left_inner(pooled[:pairs], grad_pre, highest)
    small[SD : SD + classes] = left_inner(grad, dense[:pairs], highest)
    at = small_rows
    small[at : at + 1] = jnp.sum(grad_pre, axis=0, keepdims=True)
    small[at + 1 : at + 2, :classes] = jnp.sum(grad, axis=0, keepdims=True)
    grad_pooled = right_inner(grad_pre, dense_weight[...], highest)
    grad_token = matmul(one_hot[:, :pairs], grad_pooled, highest)
    grad_score = []
    for a, inner in enumerate(by_head(rows * grad_token)):
        product = weights[a] * inner
        grad_score.append(weights[a] * (inner - of_pair(over_pair(product))))
    grad_score = spread(grad_score) * scale
    small[at + 2 : at + 3] = jnp.sum(grad_score * rows, axis=0, keepdims=True)
    result = narrow(weight * grad_token + grad_score * query[...])
    student_grad[...] = result
    small[at + 3 : at + 4] = jnp.sum(widen(result), axis=0, keepdims=True)


def norm_grad(grad, pre, gain):
    hat, scale = normalize(pre)
    scaled = grad * gain
    result = scale * (
        scaled
        - jnp.mean(scaled, axis=-1, keepdims=True)
        - hat * jnp.mean(scaled * hat, axis=-1, keepdims=True)
    )
    return (
        result,
        jnp.sum(grad * hat, axis=0, keepdims=True),
        jnp.sum(grad, axis=0, keepdims=True),
    )


def as_columns(rows, count, hidden):
    row = lax.broadcasted_iota(jnp.int32, (LANES, hidden), 0)
    block = jnp.zeros((LANES, hidden), F32)
    for i in range(count):
        block = jnp.where(row == i, rows[i], block)
    return block.T


def down_grad_body(
    slot, returned, student_grad, student, vectors, pre_second, outputs, activated,
    grad_second, grad_down, shards, sums_ref, *, sums, ratio,
):
    step = pl.program_id(0)
    count, hidden = pre_second.shape

    @pl.when(step == 0)
    def _():
        gain = turned(vectors[...])[GAIN2 : GAIN2 + 1]
        place = lax.broadcasted_iota(jnp.int32, (CHUNK, returned.shape[0]), 1)
        parts = []
        for low in range(0, count, CHUNK):
            cut = slice(low, low + CHUNK)
            pick = (slot[cut] == place).astype(BF16)
            grad = matmul(pick, returned[...]) + right_inner(student_grad[cut], student[...])
            result, gain_part, bias_part = norm_grad(grad, pre_second[cut], gain)
            grad_second[cut] = result
            low_result = narrow(result)
            grad_down[cut] = low_result
            parts.append((jnp.sum(widen(low_result), axis=0, keepdims=True), gain_part, bias_part))
        for i in range(3):
            sums_ref[i : i + 1] = sum(part[i] for part in parts)

    sums.store(
        shards,
        left_inner(activated[...], grad_down[...]),
        pl.multiple_of(step * hidden, LANES),
    )

    @pl.when(step == pl.num_programs(0) - 1)
    def _():
        sums.store(shards, left_inner(outputs[...], student_grad[...]), ratio * hidden)
        vector_rows = [sums_ref[i : i + 1] for i in range(3)]
        sums.store(shards, as_columns(vector_rows, 3, hidden), ratio * hidden + SD)


def up_grad_body(
    grad_down, grad_second, down, up, slope, normed, pre_first, context, vectors,
    grad_first, grad_branch, shards, total, bias_rows, *, sums, ratio,
):
    step = pl.program_id(0)
    count, hidden = pre_first.shape
    bias_part = 0.0
    pieces = []
    for low in range(0, count, CHUNK):
        cut = slice(low, low + CHUNK)
        grad = right_inner(grad_down[cut], down[...])
        grad = narrow(grad * widen(slope[cut]))
        pieces.append(grad)
        bias_part = bias_part + jnp.sum(widen(grad), axis=0, keepdims=True)
        update = right_inner(grad, up[...])

        @pl.when(step == 0)
        def _():
            total[cut] = grad_second[cut] + update

        @pl.when(step > 0)
        def _():
            total[cut] += update

    bias_rows[pl.ds(step, 1)] = bias_part
    sums.store(
        shards,
        left_inner(normed[...], jnp.concatenate(pieces, axis=0)),
        pl.multiple_of(step * hidden, LANES),
    )

    @pl.when(step == pl.num_programs(0) - 1)
    def _():
        gain = turned(vectors[...])[GAIN1 : GAIN1 + 1]
        parts = []
        for low in range(0, count, CHUNK):
            cut = slice(low, low + CHUNK)
            result, gain_part, shift_part = norm_grad(total[cut], pre_first[cut], gain)
            grad_first[cut] = result
            low_result = narrow(result)
            grad_branch[cut] = low_result
            parts.append((jnp.sum(widen(low_result), axis=0, keepdims=True), gain_part, shift_part))
        vector_rows = [sum(part[i] for part in parts) for i in range(3)]
        vector_rows += [bias_rows[i : i + 1] for i in range(ratio)]
        sums.store(shards, left_inner(context[...], grad_branch[...]), ratio * hidden)
        sums.store(
            shards, as_columns(vector_rows, 3 + ratio, hidden), (ratio + 1) * hidden
        )


def qkv_grad_body(tokens, grads, shards, bias_rows, *, sums):
    step = pl.program_id(0)
    hidden = tokens.shape[1]
    grad = grads[0]
    bias_rows[pl.ds(step, 1)] = jnp.sum(widen(grad), axis=0, keepdims=True)
    sums.store(
        shards, left_inner(tokens[...], grad), pl.multiple_of(step * hidden, LANES)
    )

    @pl.when(step == pl.num_programs(0) - 1)
    def _():
        vector_rows = [bias_rows[0:1], bias_rows[2:3]]
        sums.store(shards, as_columns(vector_rows, 2, hidden), 3 * hidden)


def token_grad_body(grads, weight, grad_first, result, total):
    step = pl.program_id(0)
    update = right_inner(grads[0], weight[...])

    @pl.when(step == 0)
    def _():
        total[...] = grad_first[...] + update

    @pl.when(step > 0)
    def _():
        total[...] += update

    @pl.when(step == pl.num_programs(0) - 1)
    def _():
        result[...] = narrow(total[...])


def local(
    layout,
    tokens,
    lengths,
    exit_layers,
    destination,
    carried_grad,
    logits_grad,
    qkv_weight,
    query_bias,
    value_bias,
    out_weight,
    out_bias,
    norm1_gain,
    norm1_bias,
    up_weight,
    up_bias,
    down_weight,
    down_bias,
    norm2_gain,
    norm2_bias,
    student_weight,
    student_bias,
    pool_query,
    dense_weight,
    dense_bias,
    class_weight,
    class_bias,
):
    axes, count, dp_count = layout.axes, layout.count, layout.dp_count
    pair_count = lengths.shape[1]
    slots = carried_grad.shape[0]
    slot_width = slots // dp_count
    token_count, hidden = tokens.shape
    inner_dim = up_weight.shape[1]
    part = hidden // count
    ratio = inner_dim // hidden
    classes = class_weight.shape[1]
    sums = Sums(layout, hidden)
    width = 2 * LANES
    blocks = hidden // width
    micro = token_count // ROW

    def array(*shape, dtype=F32):
        return jax.ShapeDtypeStruct(shape, dtype)

    vector_list = (
        query_bias, value_bias, out_bias, norm1_gain, norm1_bias, down_bias, norm2_gain, norm2_bias,
    )
    columns = jnp.concatenate(
        [v[:, None] for v in vector_list]
        + [up_bias.reshape(part, ratio), jnp.zeros((part, LANES - len(vector_list) - ratio), BF16)],
        axis=1,
    )
    packed_width = (4 + 2 * ratio) * hidden + SD + LANES
    packed = pl.pallas_call(
        functools.partial(pack_body, ratio=ratio, hidden=hidden),
        out_shape=array(part, packed_width, dtype=BF16),
        compiler_params=params(),
        name="pack",
    )(qkv_weight, out_weight, up_weight, down_weight, student_weight, columns)
    gathered = lax.all_gather(packed, axes, axis=0, tiled=True)
    student_at = (4 + 2 * ratio) * hidden // LANES
    out_spec = fixed((hidden, hidden), 0, 3)
    up_spec = pl.BlockSpec((hidden, hidden), lambda j: (0, 4 + j))
    down_spec = pl.BlockSpec((hidden, hidden), lambda j: (0, 4 + ratio + j))
    student_spec = fixed((hidden, SD), 0, student_at)
    vector_spec = fixed((hidden, LANES), 0, student_at + 1)
    full_spec = fixed((token_count, hidden))
    column_spec = pl.BlockSpec((token_count, hidden), lambda j: (0, j))

    place = jnp.arange(ROW, dtype=jnp.int32)
    pair_ids = jnp.arange(pair_count, dtype=jnp.int32)
    ends = jnp.cumsum(lengths, axis=1)
    starts = ends - lengths
    alive = (exit_layers > LAYER).astype(jnp.int32)
    targets = destination.reshape(micro, pair_count)
    segment = jnp.sum((place[None, :, None] >= ends[:, None, :]).astype(jnp.int32), axis=2)
    member = (segment[:, :, None] == pair_ids[None, None, :]).astype(jnp.int32)
    token_slot = jnp.sum(
        member * jnp.where(alive > 0, targets * slot_width - starts, -slots - ROW)[:, None, :], axis=2
    ) + place[None, :]
    token_slot = jnp.where(token_slot < 0, -1, token_slot).reshape(token_count, 1)
    flat_segment = (segment + pair_count * jnp.arange(micro, dtype=jnp.int32)[:, None]).reshape(
        token_count, 1
    )
    seg_column, seg_row = segment[:, :, None], segment[:, None, :]
    flat_starts = (starts + ROW * jnp.arange(micro, dtype=jnp.int32)[:, None]).reshape(-1)
    dp_ids = jnp.arange(dp_count, dtype=jnp.int32)
    chosen = (destination.reshape(-1)[None, :] == dp_ids[:, None]).astype(jnp.int32)
    send_start = jnp.sum(chosen * flat_starts[None, :], axis=1)
    send_length = jnp.sum(chosen * (lengths * alive).reshape(-1)[None, :], axis=1)
    slot_place = jnp.arange(slot_width, dtype=jnp.int32)
    slot_token = jnp.where(
        slot_place[None, :] < send_length[:, None], send_start[:, None] + slot_place[None, :], -1
    ).reshape(slots, 1)

    returned = lax.all_to_all(carried_grad, layout.dp, split_axis=0, concat_axis=0, tiled=True)

    row_specs = [
        pl.BlockSpec((1, ROW, 1), lambda r, p: (r, 0, 0)),
        pl.BlockSpec((1, 1, ROW), lambda r, p: (r, 0, 0)),
    ]
    block_spec = pl.BlockSpec((ROW, width), lambda r, p: (r, p))
    pair_flops = 2 * token_count * ROW * hidden
    query, key, value, context = pl.pallas_call(
        attention_body,
        grid=(micro, blocks),
        in_specs=[pl.BlockSpec((ROW, hidden), lambda r, p: (r, 0))]
        + row_specs
        + [
            pl.BlockSpec((hidden, width), lambda r, p: (0, p)),
            pl.BlockSpec((hidden, width), lambda r, p: (0, blocks + p)),
            pl.BlockSpec((hidden, width), lambda r, p: (0, 2 * blocks + p)),
            vector_spec,
        ],
        out_specs=(block_spec,) * 4,
        out_shape=(array(token_count, hidden, dtype=BF16),) * 4,
        scratch_shapes=[pltpu.VMEM((ROW, ROW), F32), pltpu.VMEM((LANES, hidden), F32)],
        compiler_params=params(),
        cost_estimate=cost(16e9, 12e6),
        name="attention",
    )(tokens, seg_column, seg_row, gathered, gathered, gathered, gathered)

    pre_first, normed, activated, slope, pre_second, outputs, student_rows = pl.pallas_call(
        forward_body,
        grid=(ratio,),
        in_specs=[full_spec, full_spec, out_spec, up_spec, down_spec, student_spec, vector_spec, fixed((1, SD))],
        out_specs=(full_spec, full_spec, column_spec, column_spec, full_spec, full_spec, fixed((token_count, SD))),
        out_shape=(
            array(token_count, hidden),
            array(token_count, hidden, dtype=BF16),
            array(token_count, inner_dim, dtype=BF16),
            array(token_count, inner_dim, dtype=BF16),
            array(token_count, hidden),
            array(token_count, hidden, dtype=BF16),
            array(token_count, SD),
        ),
        scratch_shapes=[pltpu.VMEM((token_count, hidden), F32), pltpu.VMEM((LANES, hidden), F32)],
        compiler_params=params(),
        cost_estimate=cost(16e9, 30e6),
        name="forward",
    )(tokens, context, gathered, gathered, gathered, gathered, gathered, student_bias[None, :])

    step = 512 if slots % 512 == 0 else slots
    outgoing = pl.pallas_call(
        select_body,
        grid=(slots // step,),
        in_specs=[pl.BlockSpec((step, 1), lambda i: (i, 0)), full_spec],
        out_specs=pl.BlockSpec((step, hidden), lambda i: (i, 0)),
        out_shape=array(slots, hidden, dtype=BF16),
        compiler_params=params(),
        cost_estimate=cost(2.4e9, 5e6),
        name="select",
    )(slot_token, outputs)
    carried = lax.all_to_all(outgoing, layout.dp, split_axis=0, concat_axis=0, tiled=True)

    small_rows = -(-(SD + classes) // 8) * 8
    logits, student_grad, small = pl.pallas_call(
        functools.partial(student_body, small_rows=small_rows),
        out_shape=(
            array(*logits_grad.shape),
            array(token_count, SD, dtype=BF16),
            array(small_rows + 8, SD),
        ),
        compiler_params=params(),
        cost_estimate=cost(1e9, 2e6),
        name="student",
    )(
        student_rows, flat_segment, pool_query[None, :], dense_weight, dense_bias[None, :],
        class_weight, class_bias[None, :], logits_grad,
    )
    small = jnp.sum(
        lax.all_gather(small, axes, axis=0, tiled=False).reshape((count,) + small.shape), axis=0
    )

    first_width = ratio * hidden + SD + LANES
    grad_second, grad_down, first = pl.pallas_call(
        functools.partial(down_grad_body, sums=sums, ratio=ratio),
        grid=(ratio,),
        in_specs=[
            fixed((token_count, 1)), fixed((slots, hidden)), fixed((token_count, SD)), student_spec,
            vector_spec, full_spec, full_spec, column_spec,
        ],
        out_specs=(full_spec, full_spec, sums.spec(first_width)),
        out_shape=(
            array(token_count, hidden),
            array(token_count, hidden, dtype=BF16),
            sums.shape(first_width),
        ),
        scratch_shapes=[pltpu.VMEM((8, hidden), F32)],
        compiler_params=params(),
        cost_estimate=cost(10e9, 25e6),
        name="down_grad",
    )(token_slot, returned, student_grad, gathered, gathered, pre_second, outputs, activated)
    first_sum = layout.scatter_sum(sums.parts(first))

    second_width = (ratio + 1) * hidden + LANES
    grad_first, grad_branch, second = pl.pallas_call(
        functools.partial(up_grad_body, sums=sums, ratio=ratio),
        grid=(ratio,),
        in_specs=[
            full_spec, full_spec, down_spec, up_spec, column_spec, full_spec, full_spec, full_spec, vector_spec,
        ],
        out_specs=(full_spec, full_spec, sums.spec(second_width)),
        out_shape=(
            array(token_count, hidden),
            array(token_count, hidden, dtype=BF16),
            sums.shape(second_width),
        ),
        scratch_shapes=[pltpu.VMEM((token_count, hidden), F32), pltpu.VMEM((8, hidden), F32)],
        compiler_params=params(),
        cost_estimate=cost(20e9, 35e6),
        name="up_grad",
    )(grad_down, grad_second, gathered, gathered, slope, normed, pre_first, context, gathered)
    second_sum = layout.scatter_sum(sums.parts(second))

    grads = pl.pallas_call(
        attention_grad_body,
        grid=(micro, blocks),
        in_specs=[pl.BlockSpec((ROW, hidden), lambda r, p: (r, 0))]
        + row_specs
        + [block_spec] * 3
        + [pl.BlockSpec((width, hidden), lambda r, p: (p, 3))],
        out_specs=pl.BlockSpec((3, ROW, width), lambda r, p: (0, r, p)),
        out_shape=array(3, token_count, hidden, dtype=BF16),
        scratch_shapes=[pltpu.VMEM((ROW, ROW), F32)],
        compiler_params=params(),
        cost_estimate=cost(28e9, 15e6),
        name="attention_grad",
    )(grad_branch, seg_column, seg_row, query, key, value, gathered)

    third_width = 3 * hidden + LANES
    grads_spec = pl.BlockSpec((1, token_count, hidden), lambda j: (j, 0, 0))
    third = pl.pallas_call(
        functools.partial(qkv_grad_body, sums=sums),
        grid=(3,),
        in_specs=[full_spec, grads_spec],
        out_specs=sums.spec(third_width),
        out_shape=sums.shape(third_width),
        scratch_shapes=[pltpu.VMEM((8, hidden), F32)],
        compiler_params=params(),
        cost_estimate=cost(4e9, 10e6),
        name="qkv_grad",
    )(tokens, grads)
    third_sum = layout.scatter_sum(sums.parts(third))
    tokens_grad = pl.pallas_call(
        token_grad_body,
        grid=(3,),
        in_specs=[grads_spec, pl.BlockSpec((hidden, hidden), lambda j: (0, j)), full_spec],
        out_specs=full_spec,
        out_shape=array(token_count, hidden, dtype=BF16),
        scratch_shapes=[pltpu.VMEM((token_count, hidden), F32)],
        compiler_params=params(),
        cost_estimate=cost(4e9, 14e6),
        name="token_grad",
    )(grads, gathered, grad_first)

    down_grad = first_sum[:, : ratio * hidden].reshape(ratio * part, hidden)
    student_weight_grad = first_sum[:, ratio * hidden : ratio * hidden + SD]
    first_vectors = first_sum[:, ratio * hidden + SD :]
    up_grad = (
        second_sum[:, : ratio * hidden]
        .reshape(part, ratio, hidden)
        .transpose(0, 2, 1)
        .reshape(part, ratio * hidden)
    )
    out_grad = second_sum[:, ratio * hidden : (ratio + 1) * hidden]
    second_vectors = second_sum[:, (ratio + 1) * hidden :]
    qkv_grad = third_sum[:, : 3 * hidden]
    third_vectors = third_sum[:, 3 * hidden :]
    return (
        carried,
        logits,
        tokens_grad,
        qkv_grad,
        third_vectors[:, 0],
        third_vectors[:, 1],
        out_grad,
        second_vectors[:, 0],
        second_vectors[:, 1],
        second_vectors[:, 2],
        up_grad,
        second_vectors[:, 3 : 3 + ratio].reshape(-1),
        down_grad,
        first_vectors[:, 0],
        first_vectors[:, 1],
        first_vectors[:, 2],
        student_weight_grad,
        small[small_rows + 3],
        small[small_rows + 2],
        small[:SD],
        small[small_rows],
        small[SD : SD + classes].T,
        small[small_rows + 1, :classes],
    )


def solution(mesh):
    layout = Layout(mesh)
    rows, flat, whole = P(layout.axes, None), P(layout.axes), P()

    def step(*args):
        return local(layout, *args)

    shard = (flat, flat, rows, flat, flat, flat, rows, flat, rows, flat, flat, flat, rows)
    return jax.shard_map(
        step,
        mesh=layout.mesh,
        in_specs=(rows,) * 7 + shard + (whole,) * 6,
        out_specs=(rows,) * 4 + shard + (whole,) * 6,
        check_vma=False,
    )
```

time: 1150 us -> 602 us (0.52)
  waiting for transfers between devices: 575 us -> 282 us
  matrix products: 220 us -> 0 us
  Pallas kernels: 0 us -> 169 us
  blocking collectives: 189 us -> 24.8 us
  other arithmetic: 66.1 us -> 28.4 us
  local copies, waits for them, and re-layouts: 60.6 us -> 31.5 us
  starting transfers between devices: 12.3 us -> 40.6 us
    reduce_scatter x3 -> x0, waiting for transfers between devices: 388 us -> none  [the longest x1 142 us: local(): lax.psum_scatter(totals[3], ('dp', 'fsdp'), scatter_dimension=0, tiled=True)]
    dot_general x64 -> x0, matrix products: 220 us -> none  [the longest x10 59.5 us: matmul(): return jnp.dot(left, right, preferred_element_type=jnp.float32)]
    pallas_call x0 -> x10, Pallas kernels: none -> 169 us  [the longest x1 35.7 us: local(): pl.pallas_call(functools.partial(up_grad_body, sums=sums, ratio=ratio), g...]
    all_to_all x2 -> x9, waiting for transfers between devices: 0.01 us -> 150 us  [the longest x7 110 us: exchange(): lax.all_to_all(value, self.stages[stage], split_axis=0, concat_axis=0, ti...]
    unnamed x2 -> x0, blocking collectives: 145 us -> none
    unnamed x12 -> x2, waiting for transfers between devices: 139 us -> 0.71 us
    all_gather x4 -> x2, waiting for transfers between devices: 47.6 us -> 131 us  [the longest x1 130 us: local(): gathered = lax.all_gather(packed, axes, axis=0, tiled=True)]
    all_gather x1 -> x0, blocking collectives: 44 us -> none  [local(): lax.all_gather(student_weight, ('dp', 'fsdp'), axis=0, tiled=True)]
  transfers between devices with their start and end apart: 12 -> 11, of which waited for: 7 -> 10; matrix products, arithmetic and copies ran while one was open for 19% -> 7% of each run, Pallas kernels for 0% -> 13%
where the time goes in v1:
time: 602 us; the launch traced here: 591 us
  waiting for transfers between devices  282 us (47%)
  Pallas kernels  169 us (28%)
  starting transfers between devices  40.6 us (7%)
  local copies, waits for them, and re-layouts  31.5 us (5%)
  other arithmetic  28.4 us (5%)
  blocking collectives  24.8 us (4%)
  between operations  14.5 us (2%)
    all_gather x1, waiting for transfers between devices, local(): gathered = lax.all_gather(packed, axes, axis=0, tiled=True)  130 us
    all_to_all x7, waiting for transfers between devices, exchange(): lax.all_to_all(value, self.stages[stage], split_axis=0, concat_axis=0, ti...  110 us
    all_to_all x1, waiting for transfers between devices, local(): lax.all_to_all(outgoing, layout.dp, split_axis=0, concat_axis=0, tiled=True)  40.1 us
    pallas_call x1, Pallas kernels, local(): pl.pallas_call(functools.partial(up_grad_body, sums=sums, ratio=ratio), g...  35.7 us
    pallas_call x1, Pallas kernels, local(): pl.pallas_call(forward_body, grid=(ratio,), in_specs=[full_spec, full_spe...  33 us
    pallas_call x1, Pallas kernels, local(): pl.pallas_call(attention_grad_body, grid=(micro, blocks), in_specs=[pl.Bl...  29.4 us
    all_to_all x7, starting transfers between devices, exchange(): lax.all_to_all(value, self.stages[stage], split_axis=0, concat_axis=0, ti...  28.2 us
    reduce_sum x9, other arithmetic, scatter_sum(): value = jnp.sum(widen(self.exchange(narrow(value), stage)), axis=0)  25 us
  transfers between devices with their start and end apart: 11, of which 10 were waited for; matrix products, arithmetic and copies ran while one was open for 7% of the time, Pallas kernels for 13%

profile of v1, /device:TPU:0, one launch (start us, length us, event | category | flops | bytes accessed | tf_op | source)
XLA Modules:
  0.0 590.8 jit_solution(7972292160466795672)
XLA Ops:
  17.3 7.4 %all-to-all-start.1 = ((bf16[8,192,768]{2,1,0:T(8,128)(2,1)}), bf16[8,192,768]{2,1,0:T(8,128)(2,1)S(1)}, u32[]{:S(2)}, u32[]{:S(2)}) async-start(bf16[8,192,768]{2,1,0:T(8,128)(2,1)} %bitcast.69), calls=%async_computation.1 | async-start | bytes 4718592 | tf_op jit(solution)/shard_map/all_to_all | solution.py:658
  29.9 129.7 %all-gather.4.cloned.1.call-done.wq.wk.wv.vectors.out_weight.up.down.student.weight = bf16[768,9472]{1,0:T(8,128)(2,1)} async-done(((bf16[24,9472]{1,0:T(8,128)(2,1)}), bf16[768,9472]{1,0:T(8,128)(2,1)}) %all-gather.4.cloned.1.call-update) | async-done | bytes 14549008 | tf_op jit(solution)/shard_map/all_gather | solution.py:622
  159.6 21.0 %attention.1 = (bf16[1024,768]{1,0:T(8,128)(2,1)}, bf16[1024,768]{1,0:T(8,128)(2,1)}, bf16[1024,768]{1,0:T(8,128)(2,1)}, bf16[1024,768]{1,0:T(8,128)(2,1)}) custom-call(bf16[1024,768]{1,0:T(8,128)(2,1)} %tokens.5, s32[2,512,1]{2,1,0:T(8,128)} %copy.121.seg_column, s32[2,1,512]{2,1,0:T(1,128)} %broadcast_in_dim.72.seg_row, ...), custom_call_target="tpu_custom_call" | custom-call | flops 16000000000 | bytes 12000000 | tf_op jit(solution)/shard_map/attention/pallas_call | solution.py:666
  180.6 33.0 %forward.1 = (f32[1024,768]{1,0:T(8,128)}, bf16[1024,768]{1,0:T(8,128)(2,1)}, bf16[1024,3072]{1,0:T(8,128)(2,1)}, bf16[1024,3072]{1,0:T(8,128)(2,1)}, f32[1024,7...) custom-call(bf16[1024,768]{1,0:T(8,128)(2,1)} %tokens.5, bf16[1024,768]{1,0:T(8,128)(2,1)} %get-tuple-element.43.context, ...), custom_call_target="tpu_custom_call" | custom-call | flops 16000000000 | bytes 30000000 | tf_op jit(solution)/shard_map/forward/pallas_call | solution.py:685
  213.7 5.8 student.3
  220.9 18.5 %down_grad.1 = (f32[1024,768]{1,0:T(8,128)}, bf16[1024,768]{1,0:T(8,128)(2,1)}, bf16[32,24,3328]{2,1,0:T(8,128)(2,1)}) custom-call(s32[1024,1]{1,0:T(8,128)} %compare_select_fusion.slot, bf16[1536,768]{1,0:T(8,128)(2,1)} %bitcast.60, bf16[1024,128]{1,0:T(8,128)(2,1)} %get-tuple-element.47.student_grad, ...), custom_call_target="tpu_custom_call" | custom-call | flops 10000000000 | bytes 25000000 | tf_op jit(solution)/shard_map/down_grad/pallas_call | solution.py:738
  239.3 35.7 %up_grad.1 = (f32[1024,768]{1,0:T(8,128)}, bf16[1024,768]{1,0:T(8,128)(2,1)}, bf16[32,24,3968]{2,1,0:T(8,128)(2,1)}) custom-call(bf16[1024,768]{1,0:T(8,128)(2,1)} %get-tuple-element.50.grad_down, f32[1024,768]{1,0:T(8,128)} %get-tuple-element.51.grad_second, ...), custom_call_target="tpu_custom_call" | custom-call | flops 20000000000 | bytes 35000000 | tf_op jit(solution)/shard_map/up_grad/pallas_call | solution.py:759
  275.1 29.4 %attention_grad.1.grads = bf16[3,1024,768]{2,1,0:T(8,128)(2,1)} custom-call(bf16[1024,768]{1,0:T(8,128)(2,1)} %get-tuple-element.55.branch, s32[2,512,1]{2,1,0:T(8,128)} %copy.121.seg_column, s32[2,1,512]{2,1,0:T(1,128)} %broadcast_in_dim.72.seg_row, bf16[1024,768]{1,0:T(8,128)(2,1)} %get-tuple-element.56.query, bf16[1024,768]{1,0:T(8,128)(2,1)} %get-tuple-element.57.key, ...), custom_call_target="tpu_custom_call" | custom-call | flops 28000000000 | bytes 15000000 | tf_op jit(solution)/shard_map/attention_grad/pallas_call | solution.py:778
  304.4 8.3 %qkv_grad.1 = bf16[32,24,2432]{2,1,0:T(8,128)(2,1)} custom-call(bf16[1024,768]{1,0:T(8,128)(2,1)} %tokens.5, bf16[3,1024,768]{2,1,0:T(8,128)(2,1)} %attention_grad.1.grads), custom_call_target="tpu_custom_call" | custom-call | flops 4000000000 | bytes 10000000 | tf_op jit(solution)/shard_map/qkv_grad/pallas_call | solution.py:795
  312.8 11.3 %all_to_all.68 = bf16[2,16,24,2432]{3,2,1,0:T(8,128)(2,1)} all-to-all(bf16[2,16,24,2432]{3,2,1,0:T(8,128)(2,1)} %bitcast.65), channel_id=1, replica_groups=mesh['z'=4,'x'=2,'y'=2,'core'=2] {'core'}, dimensions={0} | all-to-all | bytes 7471104 | tf_op jit(solution)/shard_map/all_to_all | solution.py:122
  324.1 6.2 %all-to-all-start.5 = ((bf16[2,16,24,3968]{3,2,1,0:T(8,128)(2,1)}), bf16[2,16,24,3968]{3,2,1,0:T(8,128)(2,1)}, u32[]{:S(2)}, u32[]{:S(2)}) async-start(bf16[2,16,24,3968]{3,2,1,0:T(8,128)(2,1)} %bitcast.63), calls=%async_computation.5 | async-start | bytes 12189696 | tf_op jit(solution)/shard_map/all_to_all | solution.py:122
  336.1 13.5 %all_to_all.69 = bf16[2,16,24,3328]{3,2,1,0:T(8,128)(2,1)} all-to-all(bf16[2,16,24,3328]{3,2,1,0:T(8,128)(2,1)} %bitcast.64), channel_id=1, replica_groups=mesh['z'=4,'x'=2,'y'=2,'core'=2] {'core'}, dimensions={0} | all-to-all | bytes 10223616 | tf_op jit(solution)/shard_map/all_to_all | solution.py:122
  353.2 5.5 reduce_sum.154
  358.7 17.4 %all-to-all-done.3 = bf16[4,4,24,2432]{3,2,1,0:T(8,128)(2,1)S(1)} async-done(((bf16[4,4,24,2432]{3,2,1,0:T(8,128)(2,1)}), bf16[4,4,24,2432]{3,2,1,0:T(8,128)(2,1)S(1)}, u32[]{:S(2)}, u32[]{:S(2)}) %all-to-all-start.3) | async-done | bytes 1867808 | tf_op jit(solution)/shard_map/all_to_all | solution.py:122
  383.7 27.2 %all-to-all-done.9 = bf16[4,4,24,3328]{3,2,1,0:T(8,128)(2,1)S(1)} async-done(((bf16[4,4,24,3328]{3,2,1,0:T(8,128)(2,1)}), bf16[4,4,24,3328]{3,2,1,0:T(8,128)(2,1)S(1)}, u32[]{:S(2)}, u32[]{:S(2)}) %all-to-all-start.9) | async-done | bytes 2555936 | tf_op jit(solution)/shard_map/all_to_all | solution.py:122
  414.4 6.3 %reduce_sum.151 = bf16[16,24,3968]{2,1,0:T(8,128)(2,1)} reduce(bf16[2,16,24,3968]{3,2,1,0:T(8,128)(2,1)} %all-to-all-done.5, bf16[]{:T(256)} %constant.28.clone.1), dimensions={0}, to_apply=%region_8.9 | reduce | flops 1523712 | bytes 9142274 | tf_op jit(solution)/shard_map/reduce_sum | solution.py:128
  420.7 6.3 %all-to-all-done.4 = bf16[4,1,24,2432]{3,2,1,0:T(8,128)(2,1)S(1)} async-done(((bf16[4,1,24,2432]{3,2,1,0:T(8,128)(2,1)}), bf16[4,1,24,2432]{3,2,1,0:T(8,128)(2,1)S(1)}, u32[]{:S(2)}, u32[]{:S(2)}) %all-to-all-start.4) | async-done | bytes 466976 | tf_op jit(solution)/shard_map/all_to_all | solution.py:122
  434.6 31.9 %all-to-all-done.6 = bf16[4,4,24,3968]{3,2,1,0:T(8,128)(2,1)S(1)} async-done(((bf16[4,4,24,3968]{3,2,1,0:T(8,128)(2,1)}), bf16[4,4,24,3968]{3,2,1,0:T(8,128)(2,1)S(1)}, u32[]{:S(2)}, u32[]{:S(2)}) %all-to-all-start.6) | async-done | bytes 3047456 | tf_op jit(solution)/shard_map/all_to_all | solution.py:122
  472.3 14.5 %all-to-all-done.10 = bf16[4,1,24,3328]{3,2,1,0:T(8,128)(2,1)} async-done(((bf16[4,1,24,3328]{3,2,1,0:T(8,128)(2,1)}), bf16[4,1,24,3328]{3,2,1,0:T(8,128)(2,1)}, u32[]{:S(2)}, u32[]{:S(2)}) %all-to-all-start.10) | async-done | bytes 639008 | tf_op jit(solution)/shard_map/all_to_all | solution.py:122
  492.9 5.8 select.5
  498.7 11.2 %all-to-all-done.7 = bf16[4,1,24,3968]{3,2,1,0:T(8,128)(2,1)S(1)} async-done(((bf16[4,1,24,3968]{3,2,1,0:T(8,128)(2,1)}), bf16[4,1,24,3968]{3,2,1,0:T(8,128)(2,1)S(1)}, u32[]{:S(2)}, u32[]{:S(2)}) %all-to-all-start.7) | async-done | bytes 761888 | tf_op jit(solution)/shard_map/all_to_all | solution.py:122
  509.9 4.9 all-to-all-start
  514.8 9.3 %token_grad.1 = bf16[1024,768]{1,0:T(8,128)(2,1)} custom-call(bf16[3,1024,768]{2,1,0:T(8,128)(2,1)} %attention_grad.1.grads, bf16[768,9472]{1,0:T(8,128)(2,1)} %all-gather.4.cloned.1.call-done.wq.wk.wv.vectors.out_weight.up.down.student.weight, f32[1024,768]{1,0:T(8,128)} %get-tuple-element.59.grad_first), custom_call_target="tpu_custom_call" | custom-call | flops 4000000000 | bytes 14000000 | tf_op jit(solution)/shard_map/token_grad/pallas_call | solution.py:807
  537.0 40.1 %all-to-all-done = bf16[8,192,768]{2,1,0:T(8,128)(2,1)S(1)} async-done(((bf16[8,192,768]{2,1,0:T(8,128)(2,1)}), bf16[8,192,768]{2,1,0:T(8,128)(2,1)S(1)}, u32[]{:S(2)}, u32[]{:S(2)}) %all-to-all-start) | async-done | bytes 2359328 | tf_op jit(solution)/shard_map/all_to_all | solution.py:716
  (93 shorter events, 76.1 us)
Async XLA Ops:
  7.2 152.4 %all-gather.4.cloned.1.call-start = ((), (), s32[]{:S(2)}) async-start(), calls=%async_computation.11 | async-start | bytes 15003648 | tf_op jit(solution)/shard_map/all_gather | solution.py:622
  17.3 7.4 %copy-start.6 = (s32[2,4]{1,0:T(2,128)S(1)}, s32[2,4]{1,0:T(2,128)}, u32[]{:S(2)}) copy-start(s32[2,4]{1,0:T(2,128)} %param.27) | copy-start | bytes 100
  17.3 10.5 %copy-start.5 = (f32[128,14]{0,1:T(8,128)S(1)}, f32[128,14]{0,1:T(8,128)}, u32[]{:S(2)}) copy-start(f32[128,14]{0,1:T(8,128)} %param.50) | copy-start | bytes 21508
  17.3 11.3 %copy-start.8 = (s32[1,8]{1,0:T(1,128)S(1)}, s32[1,8]{1,0:T(1,128)}, u32[]{:S(2)}) copy-start(s32[1,8]{1,0:T(1,128)} %param.29) | copy-start | bytes 100
  17.3 11.4 %copy-start.7 = (s32[2,4]{1,0:T(2,128)S(1)}, s32[2,4]{1,0:T(2,128)}, u32[]{:S(2)}) copy-start(s32[2,4]{1,0:T(2,128)} %param.28) | copy-start | bytes 100
  17.3 202.1 %all-to-all-start.1 = ((bf16[8,192,768]{2,1,0:T(8,128)(2,1)}), bf16[8,192,768]{2,1,0:T(8,128)(2,1)S(1)}, u32[]{:S(2)}, u32[]{:S(2)}) async-start(bf16[8,192,768]{2,1,0:T(8,128)(2,1)} %bitcast.69), calls=%async_computation.1 | async-start | bytes 4718592 | tf_op jit(solution)/shard_map/all_to_all | solution.py:658
  219.5 1.4 copy-start.1
  324.1 12.0 %all-to-all-start.5 = ((bf16[2,16,24,3968]{3,2,1,0:T(8,128)(2,1)}), bf16[2,16,24,3968]{3,2,1,0:T(8,128)(2,1)}, u32[]{:S(2)}, u32[]{:S(2)}) async-start(bf16[2,16,24,3968]{3,2,1,0:T(8,128)(2,1)} %bitcast.63), calls=%async_computation.5 | async-start | bytes 12189696 | tf_op jit(solution)/shard_map/all_to_all | solution.py:122
  349.6 26.6 %all-to-all-start.3 = ((bf16[4,4,24,2432]{3,2,1,0:T(8,128)(2,1)}), bf16[4,4,24,2432]{3,2,1,0:T(8,128)(2,1)S(1)}, u32[]{:S(2)}, u32[]{:S(2)}) async-start(bf16[4,4,24,2432]{3,2,1,0:T(8,128)(2,1)} %bitcast.61), calls=%async_computation.3 | async-start | bytes 3735552 | tf_op jit(solution)/shard_map/all_to_all | solution.py:122
  376.1 1.2 copy-start.2
  377.4 33.6 %all-to-all-start.9 = ((bf16[4,4,24,3328]{3,2,1,0:T(8,128)(2,1)}), bf16[4,4,24,3328]{3,2,1,0:T(8,128)(2,1)S(1)}, u32[]{:S(2)}, u32[]{:S(2)}) async-start(bf16[4,4,24,3328]{3,2,1,0:T(8,128)(2,1)} %bitcast.58), calls=%async_computation.9 | async-start | bytes 5111808 | tf_op jit(solution)/shard_map/all_to_all | solution.py:122
  410.9 9.7 %copy-start = (bf16[4,4,24,3328]{3,2,1,0:T(8,128)(2,1)}, bf16[4,4,24,3328]{3,2,1,0:T(8,128)(2,1)S(1)}, u32[]{:S(2)}) copy-start(bf16[4,4,24,3328]{3,2,1,0:T(8,128)(2,1)S(1)} %all-to-all-done.9) | copy-start | bytes 7667716
  410.9 16.0 %all-to-all-start.4 = ((bf16[4,1,24,2432]{3,2,1,0:T(8,128)(2,1)}), bf16[4,1,24,2432]{3,2,1,0:T(8,128)(2,1)S(1)}, u32[]{:S(2)}, u32[]{:S(2)}) async-start(bf16[4,1,24,2432]{3,2,1,0:T(8,128)(2,1)} %bitcast.21), calls=%async_computation.4 | async-start | bytes 933888 | tf_op jit(solution)/shard_map/all_to_all | solution.py:122
  427.0 0.8 copy-start.3
  427.8 38.8 %all-to-all-start.6 = ((bf16[4,4,24,3968]{3,2,1,0:T(8,128)(2,1)}), bf16[4,4,24,3968]{3,2,1,0:T(8,128)(2,1)S(1)}, u32[]{:S(2)}, u32[]{:S(2)}) async-start(bf16[4,4,24,3968]{3,2,1,0:T(8,128)(2,1)} %bitcast.23), calls=%async_computation.6 | async-start | bytes 6094848 | tf_op jit(solution)/shard_map/all_to_all | solution.py:122
  466.5 20.2 %all-to-all-start.10 = ((bf16[4,1,24,3328]{3,2,1,0:T(8,128)(2,1)}), bf16[4,1,24,3328]{3,2,1,0:T(8,128)(2,1)}, u32[]{:S(2)}, u32[]{:S(2)}) async-start(bf16[4,1,24,3328]{3,2,1,0:T(8,128)(2,1)} %bitcast.67), calls=%async_computation.10 | async-start | bytes 1277952 | tf_op jit(solution)/shard_map/all_to_all | solution.py:122
  486.7 23.1 %all-to-all-start.7 = ((bf16[4,1,24,3968]{3,2,1,0:T(8,128)(2,1)}), bf16[4,1,24,3968]{3,2,1,0:T(8,128)(2,1)S(1)}, u32[]{:S(2)}, u32[]{:S(2)}) async-start(bf16[4,1,24,3968]{3,2,1,0:T(8,128)(2,1)} %bitcast.66), calls=%async_computation.7 | async-start | bytes 1523712 | tf_op jit(solution)/shard_map/all_to_all | solution.py:122
  490.2 88.0 %all-gather.6.cloned.1.call-start = ((), (), s32[]{:S(2)}) async-start(), calls=%async_computation.12 | async-start | bytes 2568192 | tf_op jit(solution)/shard_map/all_gather | solution.py:734
  509.9 67.2 %all-to-all-start = ((bf16[8,192,768]{2,1,0:T(8,128)(2,1)}), bf16[8,192,768]{2,1,0:T(8,128)(2,1)S(1)}, u32[]{:S(2)}, u32[]{:S(2)}) async-start(bf16[8,192,768]{2,1,0:T(8,128)(2,1)} %bitcast.70), calls=%async_computation | async-start | bytes 4718592 | tf_op jit(solution)/shard_map/all_to_all | solution.py:716
  514.8 9.3 %copy-start.4 = (bf16[4,1,24,2432]{3,2,1,0:T(8,128)(2,1)S(1)}, bf16[4,1,24,2432]{3,2,1,0:T(8,128)(2,1)}, u32[]{:S(2)}) copy-start(bf16[4,1,24,2432]{3,2,1,0:T(8,128)(2,1)} %copy-done.3) | copy-start | bytes 1400836
Sparse Core Ops, SparseCore 0:
  17.4 142.1 all-gather.3
  493.9 84.2 all-gather.5

commit v2 on v1

--- a/solution.py
+++ b/solution.py
@@ -22,18 +22,6 @@
 highest = lax.Precision.HIGHEST
 norm_eps = 1e-12
 masked_value = -1e30
-
-tail_scale = 0.425
-tail_terms = (
-    0.2397720031195156,
-    0.2404005560164679,
-    0.20920268278012027,
-    0.22961437095935636,
-    -0.06054995293320506,
-    0.3670545366443018,
-    -0.292749557721544,
-    0.06725537014453116,
-)
 
 QUERY_BIAS, VALUE_BIAS, OUT_BIAS, GAIN1, BIAS1, DOWN_BIAS, GAIN2, BIAS2, UP_BIAS = range(9)
 
@@ -123,10 +111,34 @@
             value, self.stages[stage], split_axis=0, concat_axis=0, tiled=True
         )
 
-    def scatter_sum(self, value):
-        for stage in range(len(self.stages)):
-            value = jnp.sum(widen(self.exchange(narrow(value), stage)), axis=0)
-        return value[0]
+    def gather(self, value):
+        for stage in reversed(range(len(self.stages))):
+            copies = jnp.broadcast_to(value, (self.extents[stage],) + value.shape)
+            value = lax.all_to_all(
+                copies, self.stages[stage], split_axis=0, concat_axis=0, tiled=True
+            )
+        order = [name for stage in self.stages for name in stage]
+        tail = value.shape[-2:]
+        value = value.reshape(tuple(self.mesh.shape[name] for name in order) + tail)
+        back = tuple(order.index(name) for name in self.axes)
+        value = value.transpose(back + (len(order), len(order) + 1))
+        return value.reshape(self.count * tail[0], tail[1])
+
+    def permutes(self, value, stage):
+        extent, axes = self.extents[stage], self.stages[stage]
+        value = value.reshape((extent, value.shape[0] // extent) + value.shape[1:])
+        me = lax.axis_index(axes)
+        parts = [lax.dynamic_index_in_dim(value, me, 0, keepdims=False)]
+        for step in range(1, extent):
+            part = lax.dynamic_index_in_dim(value, lax.rem(me + step, extent), 0, keepdims=False)
+            pairs = [(i, (i + step) % extent) for i in range(extent)]
+            parts.append(lax.ppermute(part, axes, pairs))
+        return parts
+
+    def total(self, arrived, dtype=BF16):
+        if isinstance(arrived, list):
+            return sum(widen(part) for part in arrived).astype(dtype)
+        return jnp.sum(widen(arrived), axis=0).astype(dtype)
 
 
 def store_parts(ref, value, place, column):
@@ -140,10 +152,10 @@
 
 
 class Sums:
-    def __init__(self, layout, rows):
+    def __init__(self, layout, rows, split=True):
         self.layout = layout
         self.count, self.part = layout.count, rows // layout.count
-        self.split = self.part % 8 == 0
+        self.split = split and self.part % 8 == 0
 
     def shape(self, columns):
         if self.split:
@@ -173,11 +185,10 @@
     return (source == (target % width) * ratio + target // width).astype(dtype)
 
 
-def pack_body(qkv, out, up, down, student, columns, packed, *, ratio, hidden):
-    part = qkv.shape[0]
-    packed[:, : 3 * hidden] = qkv[...]
-    packed[:, 3 * hidden : 4 * hidden] = out[...]
-    base = 4 * hidden
+def pack_body(out, up, down, student, packed, *, ratio, hidden):
+    part = out.shape[0]
+    packed[:, :hidden] = out[...]
+    base = hidden
     mix = interleave(LANES, ratio, BF16)
     for chunk in range(hidden // LANES):
         piece = narrow(
@@ -194,7 +205,6 @@
         packed[:, base + j * hidden : base + (j + 1) * hidden] = narrow(matmul(pick, down[...]))
     base += ratio * hidden
     packed[:, base : base + SD] = student[...]
-    packed[:, base + SD :] = columns[...]
 
 
 def turned(vectors):
@@ -275,6 +285,10 @@
         grads[2, :, cut] = narrow(grad_v)
 
 
+def attention_grad_next_body(*refs):
+    attention_grad_body(*refs[:7], *refs[8:])
+
+
 def normalize(values):
     average = jnp.mean(values, axis=-1, keepdims=True)
     centered = values - average
@@ -284,14 +298,8 @@
 
 
 def gelu_and_slope(x):
-    t = 1.0 / (1.0 + (tail_scale / math.sqrt(2.0)) * jnp.abs(x))
-    bell = jnp.exp(-0.5 * (x * x))
-    tail = F32(0.5 * tail_terms[-1])
-    for term in tail_terms[-2::-1]:
-        tail = tail * t + 0.5 * term
-    tail = tail * t * bell
-    phi = jnp.where(x < 0.0, tail, 1.0 - tail)
-    return x * phi, phi + x * (bell * (1.0 / math.sqrt(2.0 * math.pi)))
+    phi = 0.5 + 0.5 * lax.erf(x * math.sqrt(0.5))
+    return x * phi, phi + x * (jnp.exp(-0.5 * (x * x)) * (1.0 / math.sqrt(2.0 * math.pi)))
 
 
 CHUNK = 256
@@ -348,7 +356,7 @@
 
 def student_body(
     student_rows, segment, query, dense_weight, dense_bias, class_weight, class_bias, logits_grad,
-    logits, student_grad, small, *, small_rows,
+    logits, student_grad, small,
 ):
     count, _ = student_rows.shape
     pairs, classes = logits_grad.shape
@@ -398,11 +406,11 @@
         1.0 - dense[:pairs] * dense[:pairs]
     )
     small[...] = jnp.zeros_like(small)
-    small[:SD] = left_inner(pooled[:pairs], grad_pre, highest)
-    small[SD : SD + classes] = left_inner(grad, dense[:pairs], highest)
-    at = small_rows
-    small[at : at + 1] = jnp.sum(grad_pre, axis=0, keepdims=True)
-    small[at + 1 : at + 2, :classes] = jnp.sum(grad, axis=0, keepdims=True)
+    small[:pairs] = pooled[:pairs]
+    small[pairs : 2 * pairs] = grad_pre
+    small[2 * pairs : 3 * pairs] = dense[:pairs]
+    small[3 * pairs : 4 * pairs, :classes] = grad
+    at = 4 * pairs
     grad_pooled = right_inner(grad_pre, dense_weight[...], highest)
     grad_token = matmul(one_hot[:, :pairs], grad_pooled, highest)
     grad_score = []
@@ -410,10 +418,26 @@
         product = weights[a] * inner
         grad_score.append(weights[a] * (inner - of_pair(over_pair(product))))
     grad_score = spread(grad_score) * scale
-    small[at + 2 : at + 3] = jnp.sum(grad_score * rows, axis=0, keepdims=True)
+    small[at : at + 1] = jnp.sum(grad_score * rows, axis=0, keepdims=True)
     result = narrow(weight * grad_token + grad_score * query[...])
     student_grad[...] = result
-    small[at + 3 : at + 4] = jnp.sum(widen(result), axis=0, keepdims=True)
+    small[at + 1 : at + 2] = jnp.sum(widen(result), axis=0, keepdims=True)
+
+
+def head_sums_body(gathered, dense_weight_grad, class_weight_grad, rows, *, pairs):
+    everyone = gathered[...]
+    width = everyone.shape[2]
+
+    def factor(i):
+        return everyone[:, i * pairs : (i + 1) * pairs].reshape(-1, width)
+
+    pooled, grad_pre, dense, grad = (factor(i) for i in range(4))
+    dense_weight_grad[...] = left_inner(pooled, grad_pre, highest)
+    class_weight_grad[...] = left_inner(dense, grad, highest)
+    total = jnp.sum(everyone[:, 4 * pairs : 4 * pairs + 8], axis=0)
+    row = lax.broadcasted_iota(jnp.int32, (8, width), 0)
+    total = jnp.where(row == 2, jnp.sum(grad_pre, axis=0, keepdims=True), total)
+    rows[...] = jnp.where(row == 3, jnp.sum(grad, axis=0, keepdims=True), total)
 
 
 def norm_grad(grad, pre, gain):
@@ -482,6 +506,11 @@
 ):
     step = pl.program_id(0)
     count, hidden = pre_first.shape
+
+    @pl.when(step == 0)
+    def _():
+        total[...] = grad_second[...]
+
     bias_part = 0.0
     pieces = []
     for low in range(0, count, CHUNK):
@@ -490,15 +519,7 @@
         grad = narrow(grad * widen(slope[cut]))
         pieces.append(grad)
         bias_part = bias_part + jnp.sum(widen(grad), axis=0, keepdims=True)
-        update = right_inner(grad, up[...])
-
-        @pl.when(step == 0)
-        def _():
-            total[cut] = grad_second[cut] + update
-
-        @pl.when(step > 0)
-        def _():
-            total[cut] += update
+        total[cut] += right_inner(grad, up[...])
 
     bias_rows[pl.ds(step, 1)] = bias_part
     sums.store(
@@ -596,7 +617,7 @@
     part = hidden // count
     ratio = inner_dim // hidden
     classes = class_weight.shape[1]
-    sums = Sums(layout, hidden)
+    sums, whole_sums = Sums(layout, hidden), Sums(layout, hidden, split=False)
     width = 2 * LANES
     blocks = hidden // width
     micro = token_count // ROW
@@ -612,20 +633,21 @@
         + [up_bias.reshape(part, ratio), jnp.zeros((part, LANES - len(vector_list) - ratio), BF16)],
         axis=1,
     )
-    packed_width = (4 + 2 * ratio) * hidden + SD + LANES
+    packed_width = (1 + 2 * ratio) * hidden + SD
     packed = pl.pallas_call(
         functools.partial(pack_body, ratio=ratio, hidden=hidden),
         out_shape=array(part, packed_width, dtype=BF16),
         compiler_params=params(),
         name="pack",
-    )(qkv_weight, out_weight, up_weight, down_weight, student_weight, columns)
+    )(out_weight, up_weight, down_weight, student_weight)
     gathered = lax.all_gather(packed, axes, axis=0, tiled=True)
-    student_at = (4 + 2 * ratio) * hidden // LANES
-    out_spec = fixed((hidden, hidden), 0, 3)
-    up_spec = pl.BlockSpec((hidden, hidden), lambda j: (0, 4 + j))
-    down_spec = pl.BlockSpec((hidden, hidden), lambda j: (0, 4 + ratio + j))
+    entry = layout.gather(jnp.concatenate([qkv_weight, columns], axis=1))
+    student_at = (1 + 2 * ratio) * hidden // LANES
+    out_spec = fixed((hidden, hidden), 0, 0)
+    up_spec = pl.BlockSpec((hidden, hidden), lambda j: (0, 1 + j))
+    down_spec = pl.BlockSpec((hidden, hidden), lambda j: (0, 1 + ratio + j))
     student_spec = fixed((hidden, SD), 0, student_at)
-    vector_spec = fixed((hidden, LANES), 0, student_at + 1)
+    vector_spec = fixed((hidden, LANES), 0, 3 * hidden // LANES)
     full_spec = fixed((token_count, hidden))
     column_spec = pl.BlockSpec((token_count, hidden), lambda j: (0, j))
 
@@ -654,8 +676,6 @@
     slot_token = jnp.where(
         slot_place[None, :] < send_length[:, None], send_start[:, None] + slot_place[None, :], -1
     ).reshape(slots, 1)
-
-    returned = lax.all_to_all(carried_grad, layout.dp, split_axis=0, concat_axis=0, tiled=True)
 
     row_specs = [
         pl.BlockSpec((1, ROW, 1), lambda r, p: (r, 0, 0)),
@@ -678,9 +698,12 @@
         out_shape=(array(token_count, hidden, dtype=BF16),) * 4,
         scratch_shapes=[pltpu.VMEM((ROW, ROW), F32), pltpu.VMEM((LANES, hidden), F32)],
         compiler_params=params(),
-        cost_estimate=cost(16e9, 12e6),
+        cost_estimate=cost(1e6, 1e5),
         name="attention",
-    )(tokens, seg_column, seg_row, gathered, gathered, gathered, gathered)
+    )(tokens, seg_column, seg_row, entry, entry, entry, entry)
+
+    context, carried_grad = lax.optimization_barrier((context, carried_grad))
+    returned = lax.all_to_all(carried_grad, layout.dp, split_axis=0, concat_axis=0, tiled=True)
 
     pre_first, normed, activated, slope, pre_second, outputs, student_rows = pl.pallas_call(
         forward_body,
@@ -698,9 +721,9 @@
         ),
         scratch_shapes=[pltpu.VMEM((token_count, hidden), F32), pltpu.VMEM((LANES, hidden), F32)],
         compiler_params=params(),
-        cost_estimate=cost(16e9, 30e6),
+        cost_estimate=cost(1e6, 1e5),
         name="forward",
-    )(tokens, context, gathered, gathered, gathered, gathered, gathered, student_bias[None, :])
+    )(tokens, context, gathered, gathered, gathered, gathered, entry, student_bias[None, :])
 
     step = 512 if slots % 512 == 0 else slots
     outgoing = pl.pallas_call(
@@ -710,50 +733,46 @@
         out_specs=pl.BlockSpec((step, hidden), lambda i: (i, 0)),
         out_shape=array(slots, hidden, dtype=BF16),
         compiler_params=params(),
-        cost_estimate=cost(2.4e9, 5e6),
+        cost_estimate=cost(1e6, 1e5),
         name="select",
     )(slot_token, outputs)
+    outgoing, student_rows = lax.optimization_barrier((outgoing, student_rows))
     carried = lax.all_to_all(outgoing, layout.dp, split_axis=0, concat_axis=0, tiled=True)
-
-    small_rows = -(-(SD + classes) // 8) * 8
+    pairs = logits_grad.shape[0]
     logits, student_grad, small = pl.pallas_call(
-        functools.partial(student_body, small_rows=small_rows),
+        student_body,
         out_shape=(
             array(*logits_grad.shape),
             array(token_count, SD, dtype=BF16),
-            array(small_rows + 8, SD),
+            array(4 * pairs + 8, SD),
         ),
         compiler_params=params(),
-        cost_estimate=cost(1e9, 2e6),
+        cost_estimate=cost(1e6, 1e5),
         name="student",
     )(
         student_rows, flat_segment, pool_query[None, :], dense_weight, dense_bias[None, :],
         class_weight, class_bias[None, :], logits_grad,
     )
-    small = jnp.sum(
-        lax.all_gather(small, axes, axis=0, tiled=False).reshape((count,) + small.shape), axis=0
-    )
-
     first_width = ratio * hidden + SD + LANES
     grad_second, grad_down, first = pl.pallas_call(
-        functools.partial(down_grad_body, sums=sums, ratio=ratio),
+        functools.partial(down_grad_body, sums=whole_sums, ratio=ratio),
         grid=(ratio,),
         in_specs=[
             fixed((token_count, 1)), fixed((slots, hidden)), fixed((token_count, SD)), student_spec,
             vector_spec, full_spec, full_spec, column_spec,
         ],
-        out_specs=(full_spec, full_spec, sums.spec(first_width)),
+        out_specs=(full_spec, full_spec, whole_sums.spec(first_width)),
         out_shape=(
             array(token_count, hidden),
             array(token_count, hidden, dtype=BF16),
-            sums.shape(first_width),
+            whole_sums.shape(first_width),
         ),
         scratch_shapes=[pltpu.VMEM((8, hidden), F32)],
         compiler_params=params(),
-        cost_estimate=cost(10e9, 25e6),
+        cost_estimate=cost(1e6, 1e5),
         name="down_grad",
-    )(token_slot, returned, student_grad, gathered, gathered, pre_second, outputs, activated)
-    first_sum = layout.scatter_sum(sums.parts(first))
+    )(token_slot, returned, student_grad, gathered, entry, pre_second, outputs, activated)
+    first_sum = widen(lax.psum_scatter(first, axes, scatter_dimension=0, tiled=True))
 
     second_width = (ratio + 1) * hidden + LANES
     grad_first, grad_branch, second = pl.pallas_call(
@@ -770,25 +789,41 @@
         ),
         scratch_shapes=[pltpu.VMEM((token_count, hidden), F32), pltpu.VMEM((8, hidden), F32)],
         compiler_params=params(),
-        cost_estimate=cost(20e9, 35e6),
+        cost_estimate=cost(1e6, 1e5),
         name="up_grad",
-    )(grad_down, grad_second, gathered, gathered, slope, normed, pre_first, context, gathered)
-    second_sum = layout.scatter_sum(sums.parts(second))
-
-    grads = pl.pallas_call(
-        attention_grad_body,
-        grid=(micro, blocks),
-        in_specs=[pl.BlockSpec((ROW, hidden), lambda r, p: (r, 0))]
-        + row_specs
-        + [block_spec] * 3
-        + [pl.BlockSpec((width, hidden), lambda r, p: (p, 3))],
-        out_specs=pl.BlockSpec((3, ROW, width), lambda r, p: (0, r, p)),
-        out_shape=array(3, token_count, hidden, dtype=BF16),
-        scratch_shapes=[pltpu.VMEM((ROW, ROW), F32)],
-        compiler_params=params(),
-        cost_estimate=cost(28e9, 15e6),
-        name="attention_grad",
-    )(grad_branch, seg_column, seg_row, query, key, value, gathered)
+    )(grad_down, grad_second, gathered, gathered, slope, normed, pre_first, context, entry)
+    def attention_grad(r, *operands):
+        rows_before = operands[7:]
+        return pl.pallas_call(
+            attention_grad_body if not rows_before else attention_grad_next_body,
+            grid=(1, blocks),
+            in_specs=[
+                pl.BlockSpec((ROW, hidden), lambda _, p: (r, 0)),
+                pl.BlockSpec((1, ROW, 1), lambda _, p: (r, 0, 0)),
+                pl.BlockSpec((1, 1, ROW), lambda _, p: (r, 0, 0)),
+            ]
+            + [pl.BlockSpec((ROW, width), lambda _, p: (r, p))] * 3
+            + [pl.BlockSpec((width, hidden), lambda _, p: (p, 0))]
+            + [pl.BlockSpec(memory_space=pl.ANY)] * len(rows_before),
+            out_specs=pl.BlockSpec((3, ROW, width), lambda _, p: (0, r, p)),
+            out_shape=array(3, token_count, hidden, dtype=BF16),
+            scratch_shapes=[pltpu.VMEM((ROW, ROW), F32)],
+            input_output_aliases={7: 0} if rows_before else {},
+            compiler_params=params(),
+            cost_estimate=cost(1e6, 1e5),
+            name="attention_grad",
+        )(*operands)
+
+    row_operands = (grad_branch, seg_column, seg_row, query, key, value, gathered)
+    grads = attention_grad(0, *row_operands)
+    second, carried = lax.optimization_barrier((second, carried))
+    arrived = layout.exchange(sums.parts(second), 0)
+    grads, arrived = lax.optimization_barrier((grads, arrived))
+    second = layout.total(arrived)
+    grads, second = lax.optimization_barrier((grads, second))
+    second_arrived = layout.exchange(second, 1)
+    for r in range(1, micro):
+        grads = attention_grad(r, *row_operands, grads)
 
     third_width = 3 * hidden + LANES
     grads_spec = pl.BlockSpec((1, token_count, hidden), lambda j: (j, 0, 0))
@@ -800,10 +835,18 @@
         out_shape=sums.shape(third_width),
         scratch_shapes=[pltpu.VMEM((8, hidden), F32)],
         compiler_params=params(),
-        cost_estimate=cost(4e9, 10e6),
+        cost_estimate=cost(1e6, 1e5),
         name="qkv_grad",
     )(tokens, grads)
-    third_sum = layout.scatter_sum(sums.parts(third))
+    third, second_arrived = lax.optimization_barrier((sums.parts(third), second_arrived))
+    third = layout.total(layout.permutes(third, 0))
+    second = layout.total(second_arrived)
+    third_arrived = layout.permutes(third, 1)
+    second_arrived = layout.permutes(second, 2)
+    third, small = lax.optimization_barrier((third, small))
+    small = lax.all_to_all(
+        jnp.broadcast_to(small, (count,) + small.shape), axes, split_axis=0, concat_axis=0, tiled=True
+    )
     tokens_grad = pl.pallas_call(
         token_grad_body,
         grid=(3,),
@@ -812,9 +855,22 @@
         out_shape=array(token_count, hidden, dtype=BF16),
         scratch_shapes=[pltpu.VMEM((token_count, hidden), F32)],
         compiler_params=params(),
-        cost_estimate=cost(4e9, 14e6),
+        cost_estimate=cost(1e6, 1e5),
         name="token_grad",
-    )(grads, gathered, grad_first)
+    )(grads, entry, grad_first)
+    third_arrived, second_arrived, tokens_grad, first_sum, small = lax.optimization_barrier(
+        (third_arrived, second_arrived, tokens_grad, first_sum, small)
+    )
+    third = layout.total(third_arrived)
+    third_arrived = layout.exchange(third, 2)
+    second_sum = layout.total(second_arrived, F32)[0]
+    dense_weight_grad, class_weight_grad, head_rows = pl.pallas_call(
+        functools.partial(head_sums_body, pairs=pairs),
+        out_shape=(array(SD, SD), array(SD, SD), array(8, SD)),
+        compiler_params=params(),
+        name="head_sums",
+    )(small)
+    third_sum = layout.total(third_arrived, F32)[0]
 
     down_grad = first_sum[:, : ratio * hidden].reshape(ratio * part, hidden)
     student_weight_grad = first_sum[:, ratio * hidden : ratio * hidden + SD]
@@ -847,12 +903,12 @@
         first_vectors[:, 1],
         first_vectors[:, 2],
         student_weight_grad,
-        small[small_rows + 3],
-        small[small_rows + 2],
-        small[:SD],
-        small[small_rows],
-        small[SD : SD + classes].T,
-        small[small_rows + 1, :classes],
+        head_rows[1],
+        head_rows[0],
+        dense_weight_grad,
+        head_rows[2],
+        class_weight_grad[:, :classes],
+        head_rows[3, :classes],
     )
 
 

time: 602 us -> 408 us (0.68)
  waiting for transfers between devices: 282 us -> 79.7 us
  blocking collectives: 24.8 us -> 49.3 us
  other arithmetic: 28.4 us -> 17.5 us
  Pallas kernels: 169 us -> 160 us
  local copies, waits for them, and re-layouts: 31.5 us -> 38.8 us
    all_gather x1, waiting for transfers between devices: 130 us -> 0.01 us  [local(): gathered = lax.all_gather(packed, axes, axis=0, tiled=True)]
    all_to_all x7 -> x2, waiting for transfers between devices: 110 us -> 15.9 us  [exchange(): lax.all_to_all(value, self.stages[stage], split_axis=0, concat_axis=0, ti...]
    all_to_all x1, waiting for transfers between devices: 40.1 us -> 0.01 us  [local(): lax.all_to_all(outgoing, layout.dp, split_axis=0, concat_axis=0, tiled=True)]
    all_to_all x0 -> x2, blocking collectives: none -> 34.2 us  [gather(): lax.all_to_all(copies, self.stages[stage], split_axis=0, concat_axis=0, t...]
    all_to_all x0 -> x2, waiting for transfers between devices: none -> 27.8 us  [the longest x1 27.8 us: gather(): lax.all_to_all(copies, self.stages[stage], split_axis=0, concat_axis=0, t...]
    all_to_all x1, waiting for transfers between devices: 0.01 us -> 21.6 us  [local(): lax.all_to_all(carried_grad, layout.dp, split_axis=0, concat_axis=0, tile...]
    reduce_sum x10 -> x3, other arithmetic: 26.8 us -> 7.93 us  [total(): return jnp.sum(widen(arrived), axis=0).astype(dtype)]
    ppermute x0 -> x7, waiting for transfers between devices: none -> 14.5 us  [permutes(): parts.append(lax.ppermute(part, axes, pairs))]
  transfers between devices with their start and end apart: 11 -> 15, of which waited for: 10 -> 7; matrix products, arithmetic and copies ran while one was open for 7% -> 12% of each run, Pallas kernels for 13% -> 39%
where the time goes in v2:
time: 408 us; the launch traced here: 402 us
  Pallas kernels  160 us (39%)
  waiting for transfers between devices  79.7 us (20%)
  blocking collectives  49.3 us (12%)
  starting transfers between devices  42.4 us (10%)
  local copies, waits for them, and re-layouts  38.8 us (10%)
  other arithmetic  17.5 us (4%)
  between operations  14.6 us (4%)
    all_to_all x2, blocking collectives, gather(): lax.all_to_all(copies, self.stages[stage], split_axis=0, concat_axis=0, t...  34.2 us
    pallas_call x2, Pallas kernels, attention_grad(): pl.pallas_call(attention_grad_body if not rows_before else attention_grad...  32.1 us
    pallas_call x1, Pallas kernels, local(): pl.pallas_call(functools.partial(up_grad_body, sums=sums, ratio=ratio), g...  30.1 us
    all_to_all x1, waiting for transfers between devices, gather(): lax.all_to_all(copies, self.stages[stage], split_axis=0, concat_axis=0, t...  27.8 us
    pallas_call x1, Pallas kernels, local(): pl.pallas_call(forward_body, grid=(ratio,), in_specs=[full_spec, full_spe...  24.6 us
    all_to_all x1, waiting for transfers between devices, local(): lax.all_to_all(carried_grad, layout.dp, split_axis=0, concat_axis=0, tile...  21.6 us
    pallas_call x1, Pallas kernels, local(): pl.pallas_call(attention_body, grid=(micro, blocks), in_specs=[pl.BlockSp...  21 us
    pallas_call x1, Pallas kernels, local(): pl.pallas_call(functools.partial(down_grad_body, sums=whole_sums, ratio=r...  18.5 us
  transfers between devices with their start and end apart: 15, of which 7 were waited for; matrix products, arithmetic and copies ran while one was open for 12% of the time, Pallas kernels for 39%

profile of v2, /device:TPU:0, one launch (start us, length us, event | category | flops | bytes accessed | tf_op | source)
XLA Modules:
  0.0 402.3 jit_solution(12319189901297586224)
XLA Ops:
  17.6 25.8 %all_to_all.58 = bf16[4,24,2432]{2,1,0:T(8,128)(2,1)S(1)} all-to-all(bf16[4,24,2432]{2,1,0:T(8,128)(2,1)S(1)} %broadcast_in_dim.95), channel_id=1, replica_groups=mesh['z'=4,'x'=2,'y'=2,'core'=2] {'z'}, dimensions={0} | all-to-all | bytes 933888 | tf_op jit(solution)/shard_map/all_to_all | solution.py:117
  50.4 27.8 %all-to-all-done.1 = bf16[4,4,24,2432]{3,2,1,0:T(8,128)(2,1)S(1)} async-done(((bf16[4,4,24,2432]{3,2,1,0:T(8,128)(2,1)}), bf16[4,4,24,2432]{3,2,1,0:T(8,128)(2,1)S(1)}, u32[]{:S(2)}, u32[]{:S(2)}) %all-to-all-start.1) | async-done | bytes 1867808 | tf_op jit(solution)/shard_map/all_to_all | solution.py:117
  78.6 8.4 %all_to_all.59 = bf16[2,4,4,24,2432]{4,3,1,2,0:T(8,128)(2,1)S(1)} all-to-all(bf16[2,4,4,24,2432]{4,3,1,2,0:T(8,128)(2,1)S(1)} %broadcast_in_dim.97), channel_id=1, replica_groups=mesh['z'=4,'x'=2,'y'=2,'core'=2] {'core'}, dimensions={0} | all-to-all | bytes 7471104 | tf_op jit(solution)/shard_map/all_to_all | solution.py:117
  89.0 21.0 %attention.1 = (bf16[1024,768]{1,0:T(8,128)(2,1)}, bf16[1024,768]{1,0:T(8,128)(2,1)}, bf16[1024,768]{1,0:T(8,128)(2,1)}, bf16[1024,768]{1,0:T(8,128)(2,1)}) custom-call(bf16[1024,768]{1,0:T(8,128)(2,1)} %tokens.5, s32[2,512,1]{2,1,0:T(8,128)} %copy.134.seg_column.refs_1_, s32[2,1,512]{2,1,0:T(1,128)} %broadcast_in_dim.85.seg_row.refs_2_, ...), custom_call_target="tpu_custom_call" | custom-call | flops 1000000 | bytes 100000 | tf_op jit(solution)/shard_map/attention/pallas_call | solution.py:686
  110.1 5.8 %all-to-all-start.3 = ((bf16[8,192,768]{2,1,0:T(8,128)(2,1)}), bf16[8,192,768]{2,1,0:T(8,128)(2,1)S(1)}, u32[]{:S(2)}, u32[]{:S(2)}) async-start(bf16[8,192,768]{2,1,0:T(8,128)(2,1)} %bitcast.82), calls=%async_computation.3 | async-start | bytes 4718592 | tf_op jit(solution)/shard_map/all_to_all | solution.py:706
  118.0 24.6 %forward.1 = (f32[1024,768]{1,0:T(8,128)}, bf16[1024,768]{1,0:T(8,128)(2,1)}, bf16[1024,3072]{1,0:T(8,128)(2,1)}, bf16[1024,3072]{1,0:T(8,128)(2,1)}, f32[1024,7...) custom-call(bf16[1024,768]{1,0:T(8,128)(2,1)} %tokens.5, bf16[1024,768]{1,0:T(8,128)(2,1)} %get-tuple-element.72.context, ...), custom_call_target="tpu_custom_call" | custom-call | flops 1000000 | bytes 100000 | tf_op jit(solution)/shard_map/forward/pallas_call | solution.py:708
  142.7 5.8 %select.19 = bf16[1536,768]{1,0:T(8,128)(2,1)} custom-call(s32[1536,1]{1,0:T(8,128)} %select_n.76.index, bf16[1024,768]{1,0:T(8,128)(2,1)} %get-tuple-element.73.source.outputs), custom_call_target="tpu_custom_call" | custom-call | flops 1000000 | bytes 100000 | tf_op jit(solution)/shard_map/select/pallas_call | solution.py:729
  148.5 21.6 %all-to-all-done.3 = bf16[8,192,768]{2,1,0:T(8,128)(2,1)S(1)} async-done(((bf16[8,192,768]{2,1,0:T(8,128)(2,1)}), bf16[8,192,768]{2,1,0:T(8,128)(2,1)S(1)}, u32[]{:S(2)}, u32[]{:S(2)}) %all-to-all-start.3) | async-done | bytes 2359328 | tf_op jit(solution)/shard_map/all_to_all | solution.py:706
  171.5 4.4 %all-to-all-start.4 = ((bf16[8,192,768]{2,1,0:T(8,128)(2,1)}), bf16[8,192,768]{2,1,0:T(8,128)(2,1)}, u32[]{:S(2)}, u32[]{:S(2)}) async-start(bf16[8,192,768]{2,1,0:T(8,128)(2,1)} %bitcast.78), calls=%async_computation.4 | async-start | bytes 4718592 | tf_op jit(solution)/shard_map/all_to_all | solution.py:740
  179.2 5.6 %student.3 = (f32[8,14]{1,0:T(8,128)}, bf16[1024,128]{1,0:T(8,128)(2,1)}, f32[40,128]{1,0:T(8,128)}) custom-call(f32[1024,128]{1,0:T(8,128)} %get-tuple-element.75.student_rows, s32[1024,1]{1,0:T(8,128)} %bitcast.83, f32[1,128]{1,0:T(1,128)} %bitcast.88, f32[128,128]{1,0:T(8,128)} %dense_weight.1, f32[1,128]{1,0:T(1,128)} %bitcast.89, ...), custom_call_target="tpu_custom_call" | custom-call | flops 1000000 | bytes 100000 | tf_op jit(solution)/shard_map/student/pallas_call | solution.py:742
  184.8 18.5 %down_grad.1 = (f32[1024,768]{1,0:T(8,128)}, bf16[1024,768]{1,0:T(8,128)(2,1)}, bf16[768,3328]{1,0:T(8,128)(2,1)}) custom-call(s32[1024,1]{1,0:T(8,128)} %compare_select_fusion.slot, bf16[1536,768]{1,0:T(8,128)(2,1)} %bitcast.77, bf16[1024,128]{1,0:T(8,128)(2,1)} %get-tuple-element.76.student_grad, ...), custom_call_target="tpu_custom_call" | custom-call | flops 1000000 | bytes 100000 | tf_op jit(solution)/shard_map/down_grad/pallas_call | solution.py:757
  203.3 30.1 %up_grad.1 = (f32[1024,768]{1,0:T(8,128)}, bf16[1024,768]{1,0:T(8,128)(2,1)}, bf16[32,24,3968]{2,1,0:T(8,128)(2,1)}) custom-call(bf16[1024,768]{1,0:T(8,128)(2,1)} %get-tuple-element.79.grad_down, f32[1024,768]{1,0:T(8,128)} %get-tuple-element.80.grad_second, bf16[768,7040]{1,0:T(8,128)(2,1)} %all-gather.2.cloned.1.call-done.out_weight.up.down.student.refs_6_, ...), custom_call_target="tpu_custom_call" | custom-call | flops 1000000 | bytes 100000 | tf_op jit(solution)/shard_map/up_grad/pallas_call | solution.py:778
  233.4 16.1 %attention_grad.2.refs_7_ = bf16[3,1024,768]{2,1,0:T(8,128)(2,1)} custom-call(bf16[1024,768]{1,0:T(8,128)(2,1)} %get-tuple-element.88.branch.refs_0_, s32[2,512,1]{2,1,0:T(8,128)} %copy.134.seg_column.refs_1_, s32[2,1,512]{2,1,0:T(1,128)} %broadcast_in_dim.85.seg_row.refs_2_, bf16[1024,768]{1,0:T(8,128)(2,1)} %get-tuple-element.89.query.refs_3_, ...), custom_call_target="tpu_custom_call" | custom-call | flops 1000000 | bytes 100000 | tf_op jit(solution)/shard_map/attention_grad/pallas_call | solution.py:797
  249.5 15.1 %all_to_all.60 = bf16[2,16,24,3968]{3,2,1,0:T(8,128)(2,1)} all-to-all(bf16[2,16,24,3968]{3,2,1,0:T(8,128)(2,1)} %bitcast.81), channel_id=1, replica_groups=mesh['z'=4,'x'=2,'y'=2,'core'=2] {'core'}, dimensions={0} | all-to-all | bytes 12189696 | tf_op jit(solution)/shard_map/all_to_all | solution.py:110
  264.6 6.3 %reduce_sum.73 = bf16[16,24,3968]{2,1,0:T(8,128)(2,1)} reduce(bf16[2,16,24,3968]{3,2,1,0:T(8,128)(2,1)} %all_to_all.60, bf16[]{:T(256)} %constant.80.clone.1), dimensions={0}, to_apply=%region_5.6 | reduce | flops 1523712 | bytes 9142274 | tf_op jit(solution)/shard_map/reduce_sum | solution.py:141
  270.9 4.2 %all-to-all-start.6 = ((bf16[4,4,24,3968]{3,2,1,0:T(8,128)(2,1)}), bf16[4,4,24,3968]{3,2,1,0:T(8,128)(2,1)S(1)}, u32[]{:S(2)}, u32[]{:S(2)}) async-start(bf16[4,4,24,3968]{3,2,1,0:T(8,128)(2,1)} %bitcast.23), calls=%async_computation.6 | async-start | bytes 6094848 | tf_op jit(solution)/shard_map/all_to_all | solution.py:110
  275.2 16.0 %attention_grad.3.grads = bf16[3,1024,768]{2,1,0:T(8,128)(2,1)} custom-call(bf16[1024,768]{1,0:T(8,128)(2,1)} %get-tuple-element.88.branch.refs_0_, s32[2,512,1]{2,1,0:T(8,128)} %copy.134.seg_column.refs_1_, s32[2,1,512]{2,1,0:T(1,128)} %broadcast_in_dim.85.seg_row.refs_2_, ...), custom_call_target="tpu_custom_call", output_to_operand_aliasing={{}: (7, {})} | custom-call | flops 1000000 | bytes 100000 | tf_op jit(solution)/shard_map/attention_grad/pallas_call | solution.py:797
  291.2 8.1 %qkv_grad.1 = bf16[32,24,2432]{2,1,0:T(8,128)(2,1)} custom-call(bf16[1024,768]{1,0:T(8,128)(2,1)} %tokens.5, bf16[3,1024,768]{2,1,0:T(8,128)(2,1)} %attention_grad.3.grads), custom_call_target="tpu_custom_call" | custom-call | flops 1000000 | bytes 100000 | tf_op jit(solution)/shard_map/qkv_grad/pallas_call | solution.py:830
  299.3 15.8 %all-to-all-done.6 = bf16[4,4,24,3968]{3,2,1,0:T(8,128)(2,1)S(1)} async-done(((bf16[4,4,24,3968]{3,2,1,0:T(8,128)(2,1)}), bf16[4,4,24,3968]{3,2,1,0:T(8,128)(2,1)S(1)}, u32[]{:S(2)}, u32[]{:S(2)}) %all-to-all-start.6) | async-done | bytes 3047456 | tf_op jit(solution)/shard_map/all_to_all | solution.py:110
  318.0 4.2 %collective-permute-done = bf16[16,24,2432]{2,1,0:T(8,128)(2,1)} collective-permute-done((bf16[16,24,2432]{2,1,0:T(8,128)(2,1)}, bf16[16,24,2432]{2,1,0:T(8,128)(2,1)}, u32[]{:S(2)}, u32[]{:S(2)}) %collective-permute-start) | collective-permute-done | bytes 1867808 | tf_op jit(solution)/shard_map/ppermute | solution.py:135
  326.8 4.8 %all-to-all-start.7 = ((f32[32,40,128]{2,1,0:T(8,128)}), f32[32,40,128]{2,1,0:T(8,128)}, u32[]{:S(2)}, u32[]{:S(2)}) async-start(f32[32,40,128]{2,1,0:T(8,128)} %broadcast_in_dim.103), calls=%async_computation.8 | async-start | bytes 1310720 | tf_op jit(solution)/shard_map/all_to_all | solution.py:847
  344.3 7.1 %collective-permute-done.4 = bf16[1,24,3968]{2,1,0:T(8,128)(2,1)S(1)} collective-permute-done((bf16[1,24,3968]{2,1,0:T(8,128)(2,1)S(1)}, bf16[1,24,3968]{2,1,0:T(8,128)(2,1)S(1)}, u32[]{:S(2)}, u32[]{:S(2)}) %collective-permute-start.4) | collective-permute-done | bytes 190496 | tf_op jit(solution)/shard_map/ppermute | solution.py:135
  352.1 9.5 %token_grad.1 = bf16[1024,768]{1,0:T(8,128)(2,1)} custom-call(bf16[3,1024,768]{2,1,0:T(8,128)(2,1)} %attention_grad.3.grads, bf16[768,2432]{1,0:T(8,128)(2,1)} %bitcast.73, f32[1024,768]{1,0:T(8,128)} %get-tuple-element.99.grad_first), custom_call_target="tpu_custom_call" | custom-call | flops 1000000 | bytes 100000 | tf_op jit(solution)/shard_map/token_grad/pallas_call | solution.py:850
  368.0 9.7 %all-to-all-start.8 = ((bf16[4,1,24,2432]{3,2,1,0:T(8,128)(2,1)}), bf16[4,1,24,2432]{3,2,1,0:T(8,128)(2,1)S(1)}, u32[]{:S(2)}, u32[]{:S(2)}) async-start(bf16[4,1,24,2432]{3,2,1,0:T(8,128)(2,1)} %fusion.1), calls=%async_computation.9 | async-start | bytes 933888 | tf_op jit(solution)/shard_map/all_to_all | solution.py:110
  (111 shorter events, 71.5 us)
Async XLA Ops:
  7.2 110.8 %all-gather.2.cloned.1.call-start = ((), (), s32[]{:S(2)}) async-start(), calls=%async_computation.10 | async-start | bytes 11151360 | tf_op jit(solution)/shard_map/all_gather | solution.py:643
  44.7 3.8 copy-start.7
  44.7 33.4 %all-to-all-start.1 = ((bf16[4,4,24,2432]{3,2,1,0:T(8,128)(2,1)}), bf16[4,4,24,2432]{3,2,1,0:T(8,128)(2,1)S(1)}, u32[]{:S(2)}, u32[]{:S(2)}) async-start(bf16[4,4,24,2432]{3,2,1,0:T(8,128)(2,1)} %broadcast_in_dim.96), calls=%async_computation.1 | async-start | bytes 3735552 | tf_op jit(solution)/shard_map/all_to_all | solution.py:117
  110.0 5.9 %copy-start.9 = (s32[1,8]{1,0:T(1,128)S(1)}, s32[1,8]{1,0:T(1,128)}, u32[]{:S(2)}) copy-start(s32[1,8]{1,0:T(1,128)} %param.29) | copy-start | bytes 100
  110.1 6.0 %copy-start.8 = (s32[2,4]{1,0:T(2,128)S(1)}, s32[2,4]{1,0:T(2,128)}, u32[]{:S(2)}) copy-start(s32[2,4]{1,0:T(2,128)} %param.28) | copy-start | bytes 100
  110.1 60.0 %all-to-all-start.3 = ((bf16[8,192,768]{2,1,0:T(8,128)(2,1)}), bf16[8,192,768]{2,1,0:T(8,128)(2,1)S(1)}, u32[]{:S(2)}, u32[]{:S(2)}) async-start(bf16[8,192,768]{2,1,0:T(8,128)(2,1)} %bitcast.82), calls=%async_computation.3 | async-start | bytes 4718592 | tf_op jit(solution)/shard_map/all_to_all | solution.py:706
  170.0 7.3 %copy-start.6 = (f32[128,14]{0,1:T(8,128)S(1)}, f32[128,14]{0,1:T(8,128)}, u32[]{:S(2)}) copy-start(f32[128,14]{0,1:T(8,128)} %param.50) | copy-start | bytes 21508
  171.5 78.0 %all-to-all-start.4 = ((bf16[8,192,768]{2,1,0:T(8,128)(2,1)}), bf16[8,192,768]{2,1,0:T(8,128)(2,1)}, u32[]{:S(2)}, u32[]{:S(2)}) async-start(bf16[8,192,768]{2,1,0:T(8,128)(2,1)} %bitcast.78), calls=%async_computation.4 | async-start | bytes 4718592 | tf_op jit(solution)/shard_map/all_to_all | solution.py:740
  175.9 185.7 %reduce-scatter.2.cloned.1.call-start = ((), (), s32[]{:S(2)}) async-start(), calls=%async_computation.11 | async-start | bytes 5271552 | tf_op jit(solution)/shard_map/reduce_scatter | solution.py:775
  270.9 44.2 %all-to-all-start.6 = ((bf16[4,4,24,3968]{3,2,1,0:T(8,128)(2,1)}), bf16[4,4,24,3968]{3,2,1,0:T(8,128)(2,1)S(1)}, u32[]{:S(2)}, u32[]{:S(2)}) async-start(bf16[4,4,24,3968]{3,2,1,0:T(8,128)(2,1)} %bitcast.23), calls=%async_computation.6 | async-start | bytes 6094848 | tf_op jit(solution)/shard_map/all_to_all | solution.py:110
  318.0 4.2 %collective-permute-start = (bf16[16,24,2432]{2,1,0:T(8,128)(2,1)}, bf16[16,24,2432]{2,1,0:T(8,128)(2,1)}, u32[]{:S(2)}, u32[]{:S(2)}) collective-permute-start(bf16[16,24,2432]{2,1,0:T(8,128)(2,1)} %dynamic-slice_bitcast_fusion), channel_id=1, source_target_pairs={{0,1},{1,0},{2,3},{3,2},{4,5},{5,4},{6,7},{7,6},{8,9},{9,8},{10,11... | collective-permute-start | bytes 5603336 | tf_op jit(solution)/shard_map/ppermute | solution.py:135
  318.0 7.9 %copy-start.5 = (f32[40,128]{1,0:T(8,128)S(1)}, f32[40,128]{1,0:T(8,128)}, u32[]{:S(2)}) copy-start(f32[40,128]{1,0:T(8,128)} %get-tuple-element.102) | copy-start | bytes 61444
  326.8 39.0 %all-to-all-start.7 = ((f32[32,40,128]{2,1,0:T(8,128)}), f32[32,40,128]{2,1,0:T(8,128)}, u32[]{:S(2)}, u32[]{:S(2)}) async-start(f32[32,40,128]{2,1,0:T(8,128)} %broadcast_in_dim.103), calls=%async_computation.8 | async-start | bytes 1310720 | tf_op jit(solution)/shard_map/all_to_all | solution.py:847
  333.2 6.3 %copy-start.1 = (bf16[4,24,3968]{2,1,0:T(8,128)(2,1)S(1)}, bf16[4,24,3968]{2,1,0:T(8,128)(2,1)}, u32[]{:S(2)}) copy-start(bf16[4,24,3968]{2,1,0:T(8,128)(2,1)} %reduce_sum.74) | copy-start | bytes 2285572
  334.9 30.9 %collective-permute-start.1 = (bf16[4,24,2432]{2,1,0:T(8,128)(2,1)S(1)}, bf16[4,24,2432]{2,1,0:T(8,128)(2,1)S(1)}, u32[]{:S(2)}, u32[]{:S(2)}) collective-permute-start(bf16[4,24,2432]{2,1,0:T(8,128)(2,1)S(1)} %get-tuple-element.244), channel_id=1, source_target_pairs={{0,2},{2,4},{4,6},{6,0},{1,3},{3,5},{5,7},{7,1},{8,10},{10,12},{12... | collective-permute-start | bytes 1400840 | tf_op jit(solution)/shard_map/ppermute | solution.py:135
  336.6 29.1 %collective-permute-start.2 = (bf16[4,24,2432]{2,1,0:T(8,128)(2,1)S(1)}, bf16[4,24,2432]{2,1,0:T(8,128)(2,1)}, u32[]{:S(2)}, u32[]{:S(2)}) collective-permute-start(bf16[4,24,2432]{2,1,0:T(8,128)(2,1)S(1)} %get-tuple-element.243), channel_id=1, source_target_pairs={{0,4},{2,6},{4,0},{6,2},{1,5},{3,7},{5,1},{7,3},{8,12},{10,14},{12... | collective-permute-start | bytes 1400840 | tf_op jit(solution)/shard_map/ppermute | solution.py:135
  338.1 27.7 %collective-permute-start.3 = (bf16[4,24,2432]{2,1,0:T(8,128)(2,1)S(1)}, bf16[4,24,2432]{2,1,0:T(8,128)(2,1)}, u32[]{:S(2)}, u32[]{:S(2)}) collective-permute-start(bf16[4,24,2432]{2,1,0:T(8,128)(2,1)S(1)} %get-tuple-element.242), channel_id=1, source_target_pairs={{0,6},{2,0},{4,2},{6,4},{1,7},{3,1},{5,3},{7,5},{8,14},{10,8},{12,... | collective-permute-start | bytes 1400840 | tf_op jit(solution)/shard_map/ppermute | solution.py:135
  340.4 10.9 %collective-permute-start.4 = (bf16[1,24,3968]{2,1,0:T(8,128)(2,1)S(1)}, bf16[1,24,3968]{2,1,0:T(8,128)(2,1)S(1)}, u32[]{:S(2)}, u32[]{:S(2)}) collective-permute-start(bf16[1,24,3968]{2,1,0:T(8,128)(2,1)S(1)} %get-tuple-element.248), channel_id=1, source_target_pairs={{0,8},{8,16},{16,24},{24,0},{1,9},{9,17},{17,25},{25,1},{2,10},{10... | collective-permute-start | bytes 571400 | tf_op jit(solution)/shard_map/ppermute | solution.py:135
  341.8 20.7 %collective-permute-start.5 = (bf16[1,24,3968]{2,1,0:T(8,128)(2,1)}, bf16[1,24,3968]{2,1,0:T(8,128)(2,1)S(1)}, u32[]{:S(2)}, u32[]{:S(2)}) collective-permute-start(bf16[1,24,3968]{2,1,0:T(8,128)(2,1)} %get-tuple-element.247), channel_id=1, source_target_pairs={{0,16},{8,24},{16,0},{24,8},{1,17},{9,25},{17,1},{25,9},{2,18},{10... | collective-permute-start | bytes 571400 | tf_op jit(solution)/shard_map/ppermute | solution.py:135
  351.3 14.4 %collective-permute-start.6 = (bf16[1,24,3968]{2,1,0:T(8,128)(2,1)}, bf16[1,24,3968]{2,1,0:T(8,128)(2,1)}, u32[]{:S(2)}, u32[]{:S(2)}) collective-permute-start(bf16[1,24,3968]{2,1,0:T(8,128)(2,1)} %get-tuple-element.246), channel_id=1, source_target_pairs={{0,24},{8,0},{16,8},{24,16},{1,25},{9,1},{17,9},{25,17},{2,26},{10... | collective-permute-start | bytes 571400 | tf_op jit(solution)/shard_map/ppermute | solution.py:135
  362.5 17.0 %copy-start.2 = (f32[24,3328]{1,0:T(8,128)}, f32[24,3328]{1,0:T(8,128)S(1)}, u32[]{:S(2)}) copy-start(f32[24,3328]{1,0:T(8,128)S(1)} %convert_element_type.63) | copy-start | bytes 958468
  362.5 5.4 %copy-start.4 = (bf16[1,24,3968]{2,1,0:T(8,128)(2,1)}, bf16[1,24,3968]{2,1,0:T(8,128)(2,1)S(1)}, u32[]{:S(2)}) copy-start(bf16[1,24,3968]{2,1,0:T(8,128)(2,1)S(1)} %collective-permute-done.5) | copy-start | bytes 571396
  368.0 22.6 %all-to-all-start.8 = ((bf16[4,1,24,2432]{3,2,1,0:T(8,128)(2,1)}), bf16[4,1,24,2432]{3,2,1,0:T(8,128)(2,1)S(1)}, u32[]{:S(2)}, u32[]{:S(2)}) async-start(bf16[4,1,24,2432]{3,2,1,0:T(8,128)(2,1)} %fusion.1), calls=%async_computation.9 | async-start | bytes 933888 | tf_op jit(solution)/shard_map/all_to_all | solution.py:110
  380.3 7.0 %copy-start.3 = (f32[24,3328]{1,0:T(8,128)S(1)}, f32[24,3328]{1,0:T(8,128)}, u32[]{:S(2)}) copy-start(f32[24,3328]{1,0:T(8,128)} %copy-done.2) | copy-start | bytes 958468
  (2 other events, 4.1 us)
Sparse Core Ops, SparseCore 0:
  10.9 106.4 all-gather.1
  203.4 127.2 reduce-scatter.1

commit v3 on v2

--- a/solution.py
+++ b/solution.py
@@ -103,6 +103,8 @@
                 position = position * self.sizes[axis] + at[axis]
             self.place.append(position)
         self.device_at = [self.place.index(i) for i in range(self.count)]
+        rest = self.count // self.sizes[0]
+        self.late_place = [d % rest * self.sizes[0] + d // rest for d in range(self.count)]
 
     def exchange(self, value, stage):
         extent = self.extents[stage]
@@ -111,18 +113,26 @@
             value, self.stages[stage], split_axis=0, concat_axis=0, tiled=True
         )
 
-    def gather(self, value):
+    def gather(self, value, beside):
         for stage in reversed(range(len(self.stages))):
             copies = jnp.broadcast_to(value, (self.extents[stage],) + value.shape)
             value = lax.all_to_all(
                 copies, self.stages[stage], split_axis=0, concat_axis=0, tiled=True
             )
+            if stage == len(self.stages) - 1:
+                value, beside = lax.optimization_barrier((value, beside))
         order = [name for stage in self.stages for name in stage]
         tail = value.shape[-2:]
         value = value.reshape(tuple(self.mesh.shape[name] for name in order) + tail)
         back = tuple(order.index(name) for name in self.axes)
         value = value.transpose(back + (len(order), len(order) + 1))
-        return value.reshape(self.count * tail[0], tail[1])
+        return value.reshape(self.count * tail[0], tail[1]), beside
+
+    def late_sum(self, value):
+        return lax.psum_scatter(value, self.axes[1:], scatter_dimension=0, tiled=True)
+
+    def last_sum(self, value):
+        return lax.psum_scatter(value, self.axes[:1], scatter_dimension=0, tiled=True)
 
     def permutes(self, value, stage):
         extent, axes = self.extents[stage], self.stages[stage]
@@ -141,41 +151,116 @@
         return jnp.sum(widen(arrived), axis=0).astype(dtype)
 
 
-def store_parts(ref, value, place, column):
+def store_parts(ref, place, value, column):
+    width = value.shape[1]
+    if len(ref.shape) == 2:
+        ref[:, pl.ds(column, width)] = value.astype(ref.dtype)
+        return
     count, part, _ = ref.shape
-    width = value.shape[1]
-    value = value.astype(ref.dtype) if part % 16 == 0 else value
     for device in range(count):
         ref[place[device], :, pl.ds(column, width)] = value[
             device * part : (device + 1) * part
         ].astype(ref.dtype)
 
 
+def add_body(left, right, result):
+    result[...] = (widen(left[...]) + widen(right[...])).astype(result.dtype)
+
+
+def add(left, right):
+    parts, part, columns = left.shape
+    step = 4 if parts % 4 == 0 else 1
+    spec = pl.BlockSpec((step, part, columns), lambda i: (i, 0, 0))
+    return pl.pallas_call(
+        add_body,
+        grid=(parts // step,),
+        in_specs=[spec, spec],
+        out_specs=spec,
+        out_shape=jax.ShapeDtypeStruct(left.shape, left.dtype),
+        compiler_params=params(),
+        cost_estimate=cost(1e6, 1e5),
+        name="add",
+    )(left, right)
+
+
+class Return:
+    def __init__(self, layout, slots):
+        self.layout, self.slots = layout, slots
+        extents = [layout.mesh.shape[name] for name in layout.dp]
+        self.staged = len(extents) == 2 and extents[1] == 2
+        self.extent = extents[0]
+        self.here = [lax.axis_index(name) for name in layout.dp]
+
+    def first_stage(self, value):
+        if not self.staged:
+            return [value]
+        value = value.reshape((self.extent, 2, self.slots // (2 * self.extent)) + value.shape[1:])
+        near = lax.dynamic_index_in_dim(value, self.here[1], 1, keepdims=False)
+        far = lax.dynamic_index_in_dim(value, 1 - self.here[1], 1, keepdims=False)
+        return [near, lax.ppermute(far, self.layout.dp[1], [(0, 1), (1, 0)])]
+
+    def second_stage(self, arrived):
+        if not self.staged:
+            return [lax.all_to_all(arrived[0], self.layout.dp, split_axis=0, concat_axis=0, tiled=True)]
+        both = jnp.stack(arrived, axis=1)
+        both = both.reshape((self.extent, -1) + both.shape[3:])
+        pieces = []
+        for step in range(self.extent):
+            piece = lax.dynamic_index_in_dim(
+                both, lax.rem(self.here[0] + step, self.extent), 0, keepdims=False
+            )
+            if step > 0:
+                pairs = [(i, (i + step) % self.extent) for i in range(self.extent)]
+                piece = lax.ppermute(piece, self.layout.dp[0], pairs)
+            pieces.append(piece)
+        return pieces
+
+    def position(self, target):
+        if not self.staged:
+            return target
+        step = lax.rem(self.here[0] + self.extent - target // 2, self.extent)
+        return 2 * step + jnp.bitwise_xor(target % 2, self.here[1])
+
+
 class Sums:
     def __init__(self, layout, rows, split=True):
         self.layout = layout
         self.count, self.part = layout.count, rows // layout.count
-        self.split = split and self.part % 8 == 0
-
-    def shape(self, columns):
+        self.split = split and self.part % 8 == 0 and layout.extents[0] == 2
+
+    def shapes(self, columns):
         if self.split:
-            return jax.ShapeDtypeStruct((self.count, self.part, columns), BF16)
-        return jax.ShapeDtypeStruct((self.count * self.part, columns), BF16)
-
-    def spec(self, columns):
-        return fixed(self.shape(columns).shape)
-
-    def store(self, ref, value, column):
+            return (jax.ShapeDtypeStruct((self.count // 2, self.part, columns), BF16),) * 2
+        return (jax.ShapeDtypeStruct((self.count * self.part, columns), BF16),)
+
+    def specs(self, columns):
+        return tuple(fixed(shape.shape) for shape in self.shapes(columns))
+
+    def store(self, refs, core, value, column):
+        width = value.shape[1]
+        if not self.split:
+            refs[0][:, pl.ds(column, width)] = value.astype(BF16)
+            return
+        half = self.count // 2
+
+        def put(mine):
+            for device in range(self.count):
+                position = self.layout.place[device]
+                ref = refs[0] if position // half == mine else refs[1]
+                ref[position % half, :, pl.ds(column, width)] = value[
+                    device * self.part : (device + 1) * self.part
+                ].astype(BF16)
+
+        for mine in range(2):
+            pl.when(core[0] == mine)(functools.partial(put, mine))
+
+    def first_stage(self, values):
         if self.split:
-            store_parts(ref, value, self.layout.place, column)
-        else:
-            ref[:, pl.ds(column, value.shape[1])] = value.astype(ref.dtype)
-
-    def parts(self, value):
-        if self.split:
-            return value
-        value = value.reshape(self.count, self.part, value.shape[1])
-        return value[jnp.asarray(self.layout.device_at)]
+            other = lax.ppermute(values[1], self.layout.stages[0], [(0, 1), (1, 0)])
+            return add(values[0], other)
+        value = values[0].reshape(self.count, self.part, values[0].shape[1])
+        value = value[jnp.asarray(self.layout.device_at)]
+        return self.layout.total(self.layout.permutes(value, 0))
 
 
 def interleave(width, ratio, dtype):
@@ -212,7 +297,7 @@
 
 
 def attention_body(
-    tokens, seg_column, seg_row, wq, wk, wv, vectors, query, key, value, context, mask, rows
+    tokens, seg_column, seg_row, wq, wk, wv, vectors, query, key, value, context, log_totals, mask, rows
 ):
     step = pl.program_id(1)
     width = wq.shape[1]
@@ -242,15 +327,18 @@
         for head in range(LANES // HD):
             mine = (lane >= head * HD) & (lane < (head + 1) * HD)
             scores = right_inner(k_block, jnp.where(mine, q_block, BF16(0))) + mask[...]
-            exponent = jnp.exp(scores - jnp.max(scores, axis=0, keepdims=True))
+            top = jnp.max(scores, axis=0, keepdims=True)
+            exponent = jnp.exp(scores - top)
             total = jnp.sum(exponent, axis=0, keepdims=True)
             probs = narrow(exponent * (1.0 / total))
+            at = block * (LANES // HD) + head
+            log_totals[0, at : at + 1] = top + jnp.log(total)
             parts.append(matmul(v_turned[head * HD : (head + 1) * HD], probs))
         context[:, cut] = narrow(jnp.concatenate(parts, axis=0)).T
 
 
 def attention_grad_body(
-    branch, seg_column, seg_row, query, key, value, out_weight, grads, mask
+    branch, seg_column, seg_row, query, key, value, log_totals, out_weight, grads, mask
 ):
     width = query.shape[1]
 
@@ -271,9 +359,8 @@
             q_head = jnp.where(mine, q_block, BF16(0))
             g_head = jnp.where(mine, g_block, BF16(0))
             scores = right_inner(k_block, q_head) + mask[...]
-            exponent = jnp.exp(scores - jnp.max(scores, axis=0, keepdims=True))
-            total = jnp.sum(exponent, axis=0, keepdims=True)
-            probs = exponent * (1.0 / total)
+            at = block * (LANES // HD) + head
+            probs = jnp.exp(scores - log_totals[0, at : at + 1])
             grad_probs = right_inner(v_block, g_head)
             inner = jnp.sum(probs * grad_probs, axis=0, keepdims=True)
             grad_scores = narrow(probs * (grad_probs - inner))
@@ -283,10 +370,6 @@
         grads[0, :, cut] = narrow(jnp.concatenate(grad_q, axis=0) * scale).T
         grads[1, :, cut] = narrow(grad_k)
         grads[2, :, cut] = narrow(grad_v)
-
-
-def attention_grad_next_body(*refs):
-    attention_grad_body(*refs[:7], *refs[8:])
 
 
 def normalize(values):
@@ -464,21 +547,24 @@
 
 
 def down_grad_body(
-    slot, returned, student_grad, student, vectors, pre_second, outputs, activated,
-    grad_second, grad_down, shards, sums_ref, *, sums, ratio,
+    slot, student_grad, student, vectors, pre_second, outputs, activated, *refs, ratio, place,
 ):
+    *returned, grad_second, grad_down, shards, sums_ref = refs
     step = pl.program_id(0)
     count, hidden = pre_second.shape
 
     @pl.when(step == 0)
     def _():
         gain = turned(vectors[...])[GAIN2 : GAIN2 + 1]
-        place = lax.broadcasted_iota(jnp.int32, (CHUNK, returned.shape[0]), 1)
+        length = returned[0].shape[0]
+        slot_place = lax.broadcasted_iota(jnp.int32, (CHUNK, length), 1)
         parts = []
         for low in range(0, count, CHUNK):
             cut = slice(low, low + CHUNK)
-            pick = (slot[cut] == place).astype(BF16)
-            grad = matmul(pick, returned[...]) + right_inner(student_grad[cut], student[...])
+            grad = right_inner(student_grad[cut], student[...])
+            for i, piece in enumerate(returned):
+                pick = (slot[cut] - i * length == slot_place).astype(BF16)
+                grad += matmul(pick, piece[...])
             result, gain_part, bias_part = norm_grad(grad, pre_second[cut], gain)
             grad_second[cut] = result
             low_result = narrow(result)
@@ -487,24 +573,27 @@
         for i in range(3):
             sums_ref[i : i + 1] = sum(part[i] for part in parts)
 
-    sums.store(
+    store_parts(
         shards,
+        place,
         left_inner(activated[...], grad_down[...]),
         pl.multiple_of(step * hidden, LANES),
     )
 
     @pl.when(step == pl.num_programs(0) - 1)
     def _():
-        sums.store(shards, left_inner(outputs[...], student_grad[...]), ratio * hidden)
+        at = ratio * hidden
+        store_parts(shards, place, left_inner(outputs[...], student_grad[...]), at)
         vector_rows = [sums_ref[i : i + 1] for i in range(3)]
-        sums.store(shards, as_columns(vector_rows, 3, hidden), ratio * hidden + SD)
+        store_parts(shards, place, as_columns(vector_rows, 3, hidden), at + SD)
 
 
 def up_grad_body(
-    grad_down, grad_second, down, up, slope, normed, pre_first, context, vectors,
-    grad_first, grad_branch, shards, total, bias_rows, *, sums, ratio,
+    core, grad_down, grad_second, down, up, slope, normed, pre_first, context, vectors,
+    grad_first, grad_branch, *refs, sums, ratio,
 ):
     step = pl.program_id(0)
+    *shards, total, bias_rows = refs
     count, hidden = pre_first.shape
 
     @pl.when(step == 0)
@@ -524,6 +613,7 @@
     bias_rows[pl.ds(step, 1)] = bias_part
     sums.store(
         shards,
+        core,
         left_inner(normed[...], jnp.concatenate(pieces, axis=0)),
         pl.multiple_of(step * hidden, LANES),
     )
@@ -541,25 +631,26 @@
             parts.append((jnp.sum(widen(low_result), axis=0, keepdims=True), gain_part, shift_part))
         vector_rows = [sum(part[i] for part in parts) for i in range(3)]
         vector_rows += [bias_rows[i : i + 1] for i in range(ratio)]
-        sums.store(shards, left_inner(context[...], grad_branch[...]), ratio * hidden)
+        sums.store(shards, core, left_inner(context[...], grad_branch[...]), ratio * hidden)
         sums.store(
-            shards, as_columns(vector_rows, 3 + ratio, hidden), (ratio + 1) * hidden
+            shards, core, as_columns(vector_rows, 3 + ratio, hidden), (ratio + 1) * hidden
         )
 
 
-def qkv_grad_body(tokens, grads, shards, bias_rows, *, sums):
+def qkv_grad_body(core, tokens, grads, *refs, sums):
     step = pl.program_id(0)
+    *shards, bias_rows = refs
     hidden = tokens.shape[1]
     grad = grads[0]
     bias_rows[pl.ds(step, 1)] = jnp.sum(widen(grad), axis=0, keepdims=True)
     sums.store(
-        shards, left_inner(tokens[...], grad), pl.multiple_of(step * hidden, LANES)
+        shards, core, left_inner(tokens[...], grad), pl.multiple_of(step * hidden, LANES)
     )
 
     @pl.when(step == pl.num_programs(0) - 1)
     def _():
         vector_rows = [bias_rows[0:1], bias_rows[2:3]]
-        sums.store(shards, as_columns(vector_rows, 2, hidden), 3 * hidden)
+        sums.store(shards, core, as_columns(vector_rows, 2, hidden), 3 * hidden)
 
 
 def token_grad_body(grads, weight, grad_first, result, total):
@@ -577,6 +668,58 @@
     @pl.when(step == pl.num_programs(0) - 1)
     def _():
         result[...] = narrow(total[...])
+
+
+def stacked(parts):
+    return jnp.concatenate([part.reshape(-1, part.shape[-1]) for part in parts], axis=0)
+
+
+def first_end_body(*refs, hidden, ratio):
+    *parts, down_grad, student_grad, vectors = refs
+    rows = parts[0].shape[-2]
+    every = stacked([widen(part[...]) for part in parts])
+    target = lax.broadcasted_iota(jnp.int32, (rows * ratio, every.shape[0]), 0)
+    source = lax.broadcasted_iota(jnp.int32, (rows * ratio, every.shape[0]), 1) % rows
+    every_low = narrow(every)
+    result = 0.0
+    for j in range(ratio):
+        pick = (target == source * ratio + j).astype(BF16)
+        result += matmul(pick, every_low[:, j * hidden : (j + 1) * hidden])
+    down_grad[...] = result
+    total = sum(every[i : i + rows, ratio * hidden :] for i in range(0, every.shape[0], rows))
+    student_grad[...] = total[:, :SD]
+    vectors[...] = total[:, SD:]
+
+
+def second_end_body(*refs, hidden, ratio):
+    *parts, up_grad, out_grad, vectors = refs
+    rows = parts[0].shape[-2]
+    every = stacked([widen(part[...]) for part in parts])
+    every_low = narrow(every)
+    mix = interleave(LANES, ratio, BF16)
+    for chunk in range(hidden // LANES):
+        piece = jnp.concatenate(
+            [
+                every_low[:, j * hidden + chunk * LANES : j * hidden + (chunk + 1) * LANES]
+                for j in range(ratio)
+            ],
+            axis=1,
+        )
+        piece = right_inner(piece, mix)
+        at = chunk * ratio * LANES
+        up_grad[:, at : at + ratio * LANES] = sum(
+            piece[i : i + rows] for i in range(0, piece.shape[0], rows)
+        )
+    total = sum(every[i : i + rows, ratio * hidden :] for i in range(0, every.shape[0], rows))
+    out_grad[...] = total[:, :hidden]
+    vectors[...] = total[:, hidden:]
+
+
+def third_end_body(*refs, hidden):
+    *parts, qkv_grad, vectors = refs
+    total = sum(widen(part[...]).reshape(part.shape[-2:]) for part in parts)
+    qkv_grad[...] = total[:, : 3 * hidden]
+    vectors[...] = total[:, 3 * hidden :]
 
 
 def local(
@@ -617,7 +760,9 @@
     part = hidden // count
     ratio = inner_dim // hidden
     classes = class_weight.shape[1]
-    sums, whole_sums = Sums(layout, hidden), Sums(layout, hidden, split=False)
+    sums = Sums(layout, hidden)
+    core = lax.axis_index(layout.stages[0]).astype(jnp.int32).reshape(1)
+    core_spec = pl.BlockSpec(memory_space=pltpu.SMEM)
     width = 2 * LANES
     blocks = hidden // width
     micro = token_count // ROW
@@ -641,7 +786,10 @@
         name="pack",
     )(out_weight, up_weight, down_weight, student_weight)
     gathered = lax.all_gather(packed, axes, axis=0, tiled=True)
-    entry = layout.gather(jnp.concatenate([qkv_weight, columns], axis=1))
+    returning = Return(layout, slots)
+    entry, returned = layout.gather(
+        jnp.concatenate([qkv_weight, columns], axis=1), returning.first_stage(carried_grad)
+    )
     student_at = (1 + 2 * ratio) * hidden // LANES
     out_spec = fixed((hidden, hidden), 0, 0)
     up_spec = pl.BlockSpec((hidden, hidden), lambda j: (0, 1 + j))
@@ -656,7 +804,7 @@
     ends = jnp.cumsum(lengths, axis=1)
     starts = ends - lengths
     alive = (exit_layers > LAYER).astype(jnp.int32)
-    targets = destination.reshape(micro, pair_count)
+    targets = returning.position(destination.reshape(micro, pair_count))
     segment = jnp.sum((place[None, :, None] >= ends[:, None, :]).astype(jnp.int32), axis=2)
     member = (segment[:, :, None] == pair_ids[None, None, :]).astype(jnp.int32)
     token_slot = jnp.sum(
@@ -677,13 +825,16 @@
         slot_place[None, :] < send_length[:, None], send_start[:, None] + slot_place[None, :], -1
     ).reshape(slots, 1)
 
+
     row_specs = [
         pl.BlockSpec((1, ROW, 1), lambda r, p: (r, 0, 0)),
         pl.BlockSpec((1, 1, ROW), lambda r, p: (r, 0, 0)),
     ]
     block_spec = pl.BlockSpec((ROW, width), lambda r, p: (r, p))
     pair_flops = 2 * token_count * ROW * hidden
-    query, key, value, context = pl.pallas_call(
+    heads = max(8, width // HD)
+    log_spec = pl.BlockSpec((1, heads, ROW), lambda r, p: (r * blocks + p, 0, 0))
+    query, key, value, context, log_totals = pl.pallas_call(
         attention_body,
         grid=(micro, blocks),
         in_specs=[pl.BlockSpec((ROW, hidden), lambda r, p: (r, 0))]
@@ -694,16 +845,16 @@
             pl.BlockSpec((hidden, width), lambda r, p: (0, 2 * blocks + p)),
             vector_spec,
         ],
-        out_specs=(block_spec,) * 4,
-        out_shape=(array(token_count, hidden, dtype=BF16),) * 4,
+        out_specs=(block_spec,) * 4 + (log_spec,),
+        out_shape=(array(token_count, hidden, dtype=BF16),) * 4 + (array(micro * blocks, heads, ROW),),
         scratch_shapes=[pltpu.VMEM((ROW, ROW), F32), pltpu.VMEM((LANES, hidden), F32)],
         compiler_params=params(),
         cost_estimate=cost(1e6, 1e5),
         name="attention",
     )(tokens, seg_column, seg_row, entry, entry, entry, entry)
 
-    context, carried_grad = lax.optimization_barrier((context, carried_grad))
-    returned = lax.all_to_all(carried_grad, layout.dp, split_axis=0, concat_axis=0, tiled=True)
+    context, returned = lax.optimization_barrier((context, returned))
+    returned = returning.second_stage(returned)
 
     pre_first, normed, activated, slope, pre_second, outputs, student_rows = pl.pallas_call(
         forward_body,
@@ -736,8 +887,7 @@
         cost_estimate=cost(1e6, 1e5),
         name="select",
     )(slot_token, outputs)
-    outgoing, student_rows = lax.optimization_barrier((outgoing, student_rows))
-    carried = lax.all_to_all(outgoing, layout.dp, split_axis=0, concat_axis=0, tiled=True)
+
     pairs = logits_grad.shape[0]
     logits, student_grad, small = pl.pallas_call(
         student_body,
@@ -753,100 +903,98 @@
         student_rows, flat_segment, pool_query[None, :], dense_weight, dense_bias[None, :],
         class_weight, class_bias[None, :], logits_grad,
     )
+    outgoing, student_grad, *returned = lax.optimization_barrier((outgoing, student_grad, *returned))
+    carried = lax.all_to_all(outgoing, layout.dp, split_axis=0, concat_axis=0, tiled=True)
+
     first_width = ratio * hidden + SD + LANES
+    first_shape = (count, part, first_width) if part % 8 == 0 else (hidden, first_width)
     grad_second, grad_down, first = pl.pallas_call(
-        functools.partial(down_grad_body, sums=whole_sums, ratio=ratio),
+        functools.partial(down_grad_body, ratio=ratio, place=layout.late_place),
         grid=(ratio,),
         in_specs=[
-            fixed((token_count, 1)), fixed((slots, hidden)), fixed((token_count, SD)), student_spec,
+            fixed((token_count, 1)), fixed((token_count, SD)), student_spec,
             vector_spec, full_spec, full_spec, column_spec,
-        ],
-        out_specs=(full_spec, full_spec, whole_sums.spec(first_width)),
+        ]
+        + [fixed(piece.shape) for piece in returned],
+        out_specs=(full_spec, full_spec, fixed(first_shape)),
         out_shape=(
             array(token_count, hidden),
             array(token_count, hidden, dtype=BF16),
-            whole_sums.shape(first_width),
+            array(*first_shape, dtype=BF16),
         ),
         scratch_shapes=[pltpu.VMEM((8, hidden), F32)],
         compiler_params=params(),
         cost_estimate=cost(1e6, 1e5),
         name="down_grad",
-    )(token_slot, returned, student_grad, gathered, entry, pre_second, outputs, activated)
-    first_sum = widen(lax.psum_scatter(first, axes, scatter_dimension=0, tiled=True))
+    )(token_slot, student_grad, gathered, entry, pre_second, outputs, activated, *returned)
+    if part % 8 != 0:
+        order = [layout.late_place.index(i) for i in range(count)]
+        first = first.reshape(count, part, first_width)[jnp.asarray(order)]
+    first_part = layout.late_sum(first)
 
     second_width = (ratio + 1) * hidden + LANES
-    grad_first, grad_branch, second = pl.pallas_call(
+    grad_first, grad_branch, *second = pl.pallas_call(
         functools.partial(up_grad_body, sums=sums, ratio=ratio),
         grid=(ratio,),
         in_specs=[
-            full_spec, full_spec, down_spec, up_spec, column_spec, full_spec, full_spec, full_spec, vector_spec,
+            core_spec, full_spec, full_spec, down_spec, up_spec, column_spec, full_spec, full_spec, full_spec,
+            vector_spec,
         ],
-        out_specs=(full_spec, full_spec, sums.spec(second_width)),
+        out_specs=(full_spec, full_spec) + sums.specs(second_width),
         out_shape=(
             array(token_count, hidden),
             array(token_count, hidden, dtype=BF16),
-            sums.shape(second_width),
-        ),
+        )
+        + sums.shapes(second_width),
         scratch_shapes=[pltpu.VMEM((token_count, hidden), F32), pltpu.VMEM((8, hidden), F32)],
         compiler_params=params(),
         cost_estimate=cost(1e6, 1e5),
         name="up_grad",
-    )(grad_down, grad_second, gathered, gathered, slope, normed, pre_first, context, entry)
-    def attention_grad(r, *operands):
-        rows_before = operands[7:]
-        return pl.pallas_call(
-            attention_grad_body if not rows_before else attention_grad_next_body,
-            grid=(1, blocks),
-            in_specs=[
-                pl.BlockSpec((ROW, hidden), lambda _, p: (r, 0)),
-                pl.BlockSpec((1, ROW, 1), lambda _, p: (r, 0, 0)),
-                pl.BlockSpec((1, 1, ROW), lambda _, p: (r, 0, 0)),
-            ]
-            + [pl.BlockSpec((ROW, width), lambda _, p: (r, p))] * 3
-            + [pl.BlockSpec((width, hidden), lambda _, p: (p, 0))]
-            + [pl.BlockSpec(memory_space=pl.ANY)] * len(rows_before),
-            out_specs=pl.BlockSpec((3, ROW, width), lambda _, p: (0, r, p)),
-            out_shape=array(3, token_count, hidden, dtype=BF16),
-            scratch_shapes=[pltpu.VMEM((ROW, ROW), F32)],
-            input_output_aliases={7: 0} if rows_before else {},
-            compiler_params=params(),
-            cost_estimate=cost(1e6, 1e5),
-            name="attention_grad",
-        )(*operands)
-
-    row_operands = (grad_branch, seg_column, seg_row, query, key, value, gathered)
-    grads = attention_grad(0, *row_operands)
-    second, carried = lax.optimization_barrier((second, carried))
-    arrived = layout.exchange(sums.parts(second), 0)
-    grads, arrived = lax.optimization_barrier((grads, arrived))
-    second = layout.total(arrived)
-    grads, second = lax.optimization_barrier((grads, second))
+    )(core, grad_down, grad_second, gathered, gathered, slope, normed, pre_first, context, entry)
+    second, grad_branch, carried = lax.optimization_barrier(
+        (sums.first_stage(second), grad_branch, carried)
+    )
     second_arrived = layout.exchange(second, 1)
-    for r in range(1, micro):
-        grads = attention_grad(r, *row_operands, grads)
+    grads = pl.pallas_call(
+        attention_grad_body,
+        grid=(micro, blocks),
+        in_specs=[pl.BlockSpec((ROW, hidden), lambda r, p: (r, 0))]
+        + row_specs
+        + [block_spec] * 3
+        + [log_spec, pl.BlockSpec((width, hidden), lambda r, p: (p, 0))],
+        out_specs=pl.BlockSpec((3, ROW, width), lambda r, p: (0, r, p)),
+        out_shape=array(3, token_count, hidden, dtype=BF16),
+        scratch_shapes=[pltpu.VMEM((ROW, ROW), F32)],
+        compiler_params=params(),
+        cost_estimate=cost(1e6, 1e5),
+        name="attention_grad",
+    )(grad_branch, seg_column, seg_row, query, key, value, log_totals, gathered)
 
     third_width = 3 * hidden + LANES
     grads_spec = pl.BlockSpec((1, token_count, hidden), lambda j: (j, 0, 0))
     third = pl.pallas_call(
         functools.partial(qkv_grad_body, sums=sums),
         grid=(3,),
-        in_specs=[full_spec, grads_spec],
-        out_specs=sums.spec(third_width),
-        out_shape=sums.shape(third_width),
+        in_specs=[core_spec, full_spec, grads_spec],
+        out_specs=sums.specs(third_width),
+        out_shape=sums.shapes(third_width),
         scratch_shapes=[pltpu.VMEM((8, hidden), F32)],
         compiler_params=params(),
         cost_estimate=cost(1e6, 1e5),
         name="qkv_grad",
-    )(tokens, grads)
-    third, second_arrived = lax.optimization_barrier((sums.parts(third), second_arrived))
-    third = layout.total(layout.permutes(third, 0))
-    second = layout.total(second_arrived)
-    third_arrived = layout.permutes(third, 1)
-    second_arrived = layout.permutes(second, 2)
-    third, small = lax.optimization_barrier((third, small))
+    )(core, tokens, grads)
+    third, second_arrived, small = lax.optimization_barrier((third, second_arrived, small))
     small = lax.all_to_all(
         jnp.broadcast_to(small, (count,) + small.shape), axes, split_axis=0, concat_axis=0, tiled=True
     )
+    third = sums.first_stage(third)
+    third, second_arrived, first_part = lax.optimization_barrier((third, second_arrived, first_part))
+    third_arrived = layout.permutes(third, 1)
+    third_arrived[0], second_arrived, small, first_part = lax.optimization_barrier(
+        (third_arrived[0], second_arrived, small, first_part)
+    )
+    first_part = layout.last_sum(first_part)
+    second_arrived = layout.exchange(layout.total(second_arrived), 2)
     tokens_grad = pl.pallas_call(
         token_grad_body,
         grid=(3,),
@@ -858,33 +1006,40 @@
         cost_estimate=cost(1e6, 1e5),
         name="token_grad",
     )(grads, entry, grad_first)
-    third_arrived, second_arrived, tokens_grad, first_sum, small = lax.optimization_barrier(
-        (third_arrived, second_arrived, tokens_grad, first_sum, small)
-    )
-    third = layout.total(third_arrived)
-    third_arrived = layout.exchange(third, 2)
-    second_sum = layout.total(second_arrived, F32)[0]
     dense_weight_grad, class_weight_grad, head_rows = pl.pallas_call(
         functools.partial(head_sums_body, pairs=pairs),
         out_shape=(array(SD, SD), array(SD, SD), array(8, SD)),
         compiler_params=params(),
+        cost_estimate=cost(1e6, 1e5),
         name="head_sums",
     )(small)
-    third_sum = layout.total(third_arrived, F32)[0]
-
-    down_grad = first_sum[:, : ratio * hidden].reshape(ratio * part, hidden)
-    student_weight_grad = first_sum[:, ratio * hidden : ratio * hidden + SD]
-    first_vectors = first_sum[:, ratio * hidden + SD :]
-    up_grad = (
-        second_sum[:, : ratio * hidden]
-        .reshape(part, ratio, hidden)
-        .transpose(0, 2, 1)
-        .reshape(part, ratio * hidden)
-    )
-    out_grad = second_sum[:, ratio * hidden : (ratio + 1) * hidden]
-    second_vectors = second_sum[:, (ratio + 1) * hidden :]
-    qkv_grad = third_sum[:, : 3 * hidden]
-    third_vectors = third_sum[:, 3 * hidden :]
+    third_arrived, second_arrived, first_part, tokens_grad, dense_weight_grad = lax.optimization_barrier(
+        (third_arrived, second_arrived, first_part, tokens_grad, dense_weight_grad)
+    )
+    third = layout.total(third_arrived)
+    third_arrived = layout.permutes(third, 2)
+
+    def end(body, name, arrived, *shapes):
+        return pl.pallas_call(
+            body,
+            out_shape=tuple(array(*shape) for shape in shapes),
+            compiler_params=params(),
+            cost_estimate=cost(1e6, 1e5),
+            name=name,
+        )(*arrived)
+
+    down_grad, student_weight_grad, first_vectors = end(
+        functools.partial(first_end_body, hidden=hidden, ratio=ratio), "first_end", [first_part],
+        (ratio * part, hidden), (part, SD), (part, LANES),
+    )
+    up_grad, out_grad, second_vectors = end(
+        functools.partial(second_end_body, hidden=hidden, ratio=ratio), "second_end", [second_arrived],
+        (part, inner_dim), (part, hidden), (part, LANES),
+    )
+    qkv_grad, third_vectors = end(
+        functools.partial(third_end_body, hidden=hidden), "third_end", third_arrived,
+        (part, 3 * hidden), (part, LANES),
+    )
     return (
         carried,
         logits,

time: 408 us -> 370 us (0.907)
  blocking collectives: 49.3 us -> 31.8 us
  waiting for transfers between devices: 79.7 us -> 63.5 us
  Pallas kernels: 160 us -> 171 us
  other arithmetic: 17.5 us -> 7.31 us
  local copies, waits for them, and re-layouts: 38.8 us -> 30.6 us
    all_to_all x1 -> x0, waiting for transfers between devices: 21.6 us -> none  [local(): lax.all_to_all(carried_grad, layout.dp, split_axis=0, concat_axis=0, tile...]
    all_to_all x1 -> x0, blocking collectives: 15.1 us -> none  [exchange(): lax.all_to_all(value, self.stages[stage], split_axis=0, concat_axis=0, ti...]
    all_to_all x1, waiting for transfers between devices: 0.01 us -> 10.9 us  [local(): lax.all_to_all(jnp.broadcast_to(small, (count,) + small.shape), axes, spl...]
    pallas_call x3 -> x7, Pallas kernels: 50.6 us -> 61 us  [the longest x1 25.8 us: local(): pl.pallas_call(attention_grad_body, grid=(micro, blocks), in_specs=[pl.Bl...]
    ppermute x0 -> x6, starting transfers between devices: none -> 8.49 us  [the longest x3 5.48 us: second_stage(): piece = lax.ppermute(piece, self.layout.dp[0], pairs)]
    all_to_all x1, starting transfers between devices: 4.38 us -> 12.8 us  [local(): lax.all_to_all(outgoing, layout.dp, split_axis=0, concat_axis=0, tiled=True)]
    ppermute x0 -> x6, waiting for transfers between devices: none -> 8.36 us  [the longest x2 5.86 us: first_stage(): other = lax.ppermute(values[1], self.layout.stages[0], [(0, 1), (1, 0)])]
    ppermute x7 -> x6, waiting for transfers between devices: 14.5 us -> 6.68 us  [permutes(): parts.append(lax.ppermute(part, axes, pairs))]
  transfers between devices with their start and end apart: 15 -> 20, of which waited for: 7 -> 7; matrix products, arithmetic and copies ran while one was open for 12% -> 8% of each run, Pallas kernels for 39% -> 46%
where the time goes in v3:
time: 370 us; the launch traced here: 364 us
  Pallas kernels  171 us (46%)
  waiting for transfers between devices  63.5 us (17%)
  starting transfers between devices  44.8 us (12%)
  blocking collectives  31.8 us (9%)
  local copies, waits for them, and re-layouts  30.6 us (8%)
  between operations  14.3 us (4%)
  other arithmetic  7.31 us (2%)
    all_to_all x2, blocking collectives, gather(): lax.all_to_all(copies, self.stages[stage], split_axis=0, concat_axis=0, t...  31.8 us
    pallas_call x1, Pallas kernels, local(): pl.pallas_call(functools.partial(up_grad_body, sums=sums, ratio=ratio), g...  30.7 us
    pallas_call x1, Pallas kernels, local(): pl.pallas_call(attention_grad_body, grid=(micro, blocks), in_specs=[pl.Bl...  25.8 us
    all_to_all x1, waiting for transfers between devices, gather(): lax.all_to_all(copies, self.stages[stage], split_axis=0, concat_axis=0, t...  24.8 us
    pallas_call x1, Pallas kernels, local(): pl.pallas_call(forward_body, grid=(ratio,), in_specs=[full_spec, full_spe...  24.6 us
    pallas_call x1, Pallas kernels, local(): pl.pallas_call(attention_body, grid=(micro, blocks), in_specs=[pl.BlockSp...  20.9 us
    pallas_call x1, Pallas kernels, local(): pl.pallas_call(functools.partial(down_grad_body, ratio=ratio, place=layou...  19.3 us
    all_to_all x1, starting transfers between devices, local(): lax.all_to_all(outgoing, layout.dp, split_axis=0, concat_axis=0, tiled=True)  12.8 us
  transfers between devices with their start and end apart: 20, of which 7 were waited for; matrix products, arithmetic and copies ran while one was open for 8% of the time, Pallas kernels for 46%

profile of v3, /device:TPU:0, one launch (start us, length us, event | category | flops | bytes accessed | tf_op | source)
XLA Modules:
  0.0 363.5 jit_solution(5379878791482746152)
XLA Ops:
  15.9 24.9 %all_to_all.42 = bf16[4,24,2432]{2,1,0:T(8,128)(2,1)S(1)} all-to-all(bf16[4,24,2432]{2,1,0:T(8,128)(2,1)S(1)} %broadcast_in_dim.96), channel_id=1, replica_groups=mesh['z'=4,'x'=2,'y'=2,'core'=2] {'z'}, dimensions={0} | all-to-all | bytes 933888 | tf_op jit(solution)/shard_map/all_to_all | solution.py:119
  44.6 4.1 %all-to-all-start.1 = ((bf16[4,4,24,2432]{3,2,1,0:T(8,128)(2,1)}), bf16[4,4,24,2432]{3,2,1,0:T(8,128)(2,1)S(1)}, u32[]{:S(2)}, u32[]{:S(2)}) async-start(bf16[4,4,24,2432]{3,2,1,0:T(8,128)(2,1)} %broadcast_in_dim.97), calls=%async_computation.1 | async-start | bytes 3735552 | tf_op jit(solution)/shard_map/all_to_all | solution.py:119
  52.2 24.8 %all-to-all-done.1 = bf16[4,4,24,2432]{3,2,1,0:T(8,128)(2,1)S(1)} async-done(((bf16[4,4,24,2432]{3,2,1,0:T(8,128)(2,1)}), bf16[4,4,24,2432]{3,2,1,0:T(8,128)(2,1)S(1)}, u32[]{:S(2)}, u32[]{:S(2)}) %all-to-all-start.1) | async-done | bytes 1867808 | tf_op jit(solution)/shard_map/all_to_all | solution.py:119
  77.4 6.9 %all_to_all.43 = bf16[2,4,4,24,2432]{4,3,1,2,0:T(8,128)(2,1)S(1)} all-to-all(bf16[2,4,4,24,2432]{4,3,1,2,0:T(8,128)(2,1)S(1)} %broadcast_in_dim.98), channel_id=1, replica_groups=mesh['z'=4,'x'=2,'y'=2,'core'=2] {'core'}, dimensions={0} | all-to-all | bytes 7471104 | tf_op jit(solution)/shard_map/all_to_all | solution.py:119
  86.4 20.9 %attention.1 = (bf16[1024,768]{1,0:T(8,128)(2,1)}, bf16[1024,768]{1,0:T(8,128)(2,1)}, bf16[1024,768]{1,0:T(8,128)(2,1)}, bf16[1024,768]{1,0:T(8,128)(2,1)}, f32[6,8,512]{2,1,0:T(8,128)}) custom-call(bf16[1024,768]{1,0:T(8,128)(2,1)} %tokens.5, s32[2,512,1]{2,1,0:T(8,128)} %copy.123.seg_column, s32[2,1,512]{2,1,0:T(1,128)} %broadcast_in_dim.86.seg_row, ...), custom_call_target="tpu_custom_call" | custom-call | flops 1000000 | bytes 100000 | tf_op jit(solution)/shard_map/attention/pallas_call | solution.py:837
  119.1 24.6 %forward.1 = (f32[1024,768]{1,0:T(8,128)}, bf16[1024,768]{1,0:T(8,128)(2,1)}, bf16[1024,3072]{1,0:T(8,128)(2,1)}, bf16[1024,3072]{1,0:T(8,128)(2,1)}, f32[1024,7...) custom-call(bf16[1024,768]{1,0:T(8,128)(2,1)} %tokens.5, bf16[1024,768]{1,0:T(8,128)(2,1)} %get-tuple-element.96.context, ...), custom_call_target="tpu_custom_call" | custom-call | flops 1000000 | bytes 100000 | tf_op jit(solution)/shard_map/forward/pallas_call | solution.py:859
  143.7 5.8 %select.27 = bf16[1536,768]{1,0:T(8,128)(2,1)} custom-call(s32[1536,1]{1,0:T(8,128)} %select_n.98.index, bf16[1024,768]{1,0:T(8,128)(2,1)} %get-tuple-element.97.source.outputs), custom_call_target="tpu_custom_call" | custom-call | flops 1000000 | bytes 100000 | tf_op jit(solution)/shard_map/select/pallas_call | solution.py:880
  149.5 5.6 %student.3 = (f32[8,14]{1,0:T(8,128)}, bf16[1024,128]{1,0:T(8,128)(2,1)}, f32[40,128]{1,0:T(8,128)}) custom-call(f32[1024,128]{1,0:T(8,128)} %get-tuple-element.98.student_rows, s32[1024,1]{1,0:T(8,128)} %bitcast.85, f32[1,128]{1,0:T(1,128)} %bitcast.90, f32[128,128]{1,0:T(8,128)} %dense_weight.1, f32[1,128]{1,0:T(1,128)} %bitcast.91, ...), custom_call_target="tpu_custom_call" | custom-call | flops 1000000 | bytes 100000 | tf_op jit(solution)/shard_map/student/pallas_call | solution.py:892
  156.3 12.8 %all-to-all-start.3 = ((bf16[8,192,768]{2,1,0:T(8,128)(2,1)}), bf16[8,192,768]{2,1,0:T(8,128)(2,1)S(1)}, u32[]{:S(2)}, u32[]{:S(2)}) async-start(bf16[8,192,768]{2,1,0:T(8,128)(2,1)} %bitcast.79), calls=%async_computation.3 | async-start | bytes 4718592 | tf_op jit(solution)/shard_map/all_to_all | solution.py:907
  170.6 19.3 %down_grad.1 = (f32[1024,768]{1,0:T(8,128)}, bf16[1024,768]{1,0:T(8,128)(2,1)}, bf16[32,24,3328]{2,1,0:T(8,128)(2,1)}) custom-call(s32[1024,1]{1,0:T(8,128)} %compare_select_fusion.slot, bf16[1024,128]{1,0:T(8,128)(2,1)} %get-tuple-element.102.student_grad, bf16[768,7040]{1,0:T(8,128)(2,1)} %all-gather.2.cloned.1.call-done.out_weight.up.down.student, ...), custom_call_target="tpu_custom_call" | custom-call | flops 1000000 | bytes 100000 | tf_op jit(solution)/shard_map/down_grad/pallas_call | solution.py:911
  189.9 30.7 %up_grad.1 = (f32[1024,768]{1,0:T(8,128)}, bf16[1024,768]{1,0:T(8,128)(2,1)}, bf16[16,24,3968]{2,1,0:T(8,128)(2,1)}, bf16[16,24,3968]{2,1,0:T(8,128)(2,1)}) custom-call(s32[1]{0:T(128)} %bitcast.core, bf16[1024,768]{1,0:T(8,128)(2,1)} %get-tuple-element.109.grad_down, f32[1024,768]{1,0:T(8,128)} %get-tuple-element.110.grad_second, ...), custom_call_target="tpu_custom_call" | custom-call | flops 1000000 | bytes 100000 | tf_op jit(solution)/shard_map/up_grad/pallas_call | solution.py:936
  220.6 5.9 %collective-permute-done.4.right = bf16[16,24,3968]{2,1,0:T(8,128)(2,1)} collective-permute-done((bf16[16,24,3968]{2,1,0:T(8,128)(2,1)}, bf16[16,24,3968]{2,1,0:T(8,128)(2,1)}, u32[]{:S(2)}, u32[]{:S(2)}) %collective-permute-start.4) | collective-permute-done | bytes 3047456 | tf_op jit(solution)/shard_map/ppermute | solution.py:259
  226.5 5.1 %add.224 = bf16[16,24,3968]{2,1,0:T(8,128)(2,1)} custom-call(bf16[16,24,3968]{2,1,0:T(8,128)(2,1)} %get-tuple-element.114.left, bf16[16,24,3968]{2,1,0:T(8,128)(2,1)} %collective-permute-done.4.right), custom_call_target="tpu_custom_call" | custom-call | flops 1000000 | bytes 100000 | tf_op jit(solution)/shard_map/add/pallas_call | solution.py:174
  232.9 4.3 %all-to-all-start.4 = ((bf16[4,4,24,3968]{3,2,1,0:T(8,128)(2,1)}), bf16[4,4,24,3968]{3,2,1,0:T(8,128)(2,1)S(1)}, u32[]{:S(2)}, u32[]{:S(2)}) async-start(bf16[4,4,24,3968]{3,2,1,0:T(8,128)(2,1)} %bitcast.77), calls=%async_computation.4 | async-start | bytes 6094848 | tf_op jit(solution)/shard_map/all_to_all | solution.py:112
  237.2 25.8 %attention_grad.1.grads = bf16[3,1024,768]{2,1,0:T(8,128)(2,1)} custom-call(bf16[1024,768]{1,0:T(8,128)(2,1)} %get-tuple-element.120.branch, s32[2,512,1]{2,1,0:T(8,128)} %copy.123.seg_column, s32[2,1,512]{2,1,0:T(1,128)} %broadcast_in_dim.86.seg_row, bf16[1024,768]{1,0:T(8,128)(2,1)} %get-tuple-element.121.query, bf16[1024,768]{1,0:T(8,128)(2,1)} %get-tuple-element.122.key, ...), custom_call_target="tpu_custom_call" | custom-call | flops 1000000 | bytes 100000 | tf_op jit(solution)/shard_map/attention_grad/pallas_call | solution.py:958
  263.1 8.6 %qkv_grad.1 = (bf16[16,24,2432]{2,1,0:T(8,128)(2,1)}, bf16[16,24,2432]{2,1,0:T(8,128)(2,1)}) custom-call(s32[1]{0:T(128)} %bitcast.core, bf16[1024,768]{1,0:T(8,128)(2,1)} %tokens.5, bf16[3,1024,768]{2,1,0:T(8,128)(2,1)} %attention_grad.1.grads), custom_call_target="tpu_custom_call" | custom-call | flops 1000000 | bytes 100000 | tf_op jit(solution)/shard_map/qkv_grad/pallas_call | solution.py:975
  271.7 6.9 %all-to-all-done.4 = bf16[4,4,24,3968]{3,2,1,0:T(8,128)(2,1)S(1)} async-done(((bf16[4,4,24,3968]{3,2,1,0:T(8,128)(2,1)}), bf16[4,4,24,3968]{3,2,1,0:T(8,128)(2,1)S(1)}, u32[]{:S(2)}, u32[]{:S(2)}) %all-to-all-start.4) | async-done | bytes 3047456 | tf_op jit(solution)/shard_map/all_to_all | solution.py:112
  279.4 4.8 %all-to-all-start.5 = ((f32[32,40,128]{2,1,0:T(8,128)}), f32[32,40,128]{2,1,0:T(8,128)}, u32[]{:S(2)}, u32[]{:S(2)}) async-start(f32[32,40,128]{2,1,0:T(8,128)} %broadcast_in_dim.103), calls=%async_computation.6 | async-start | bytes 1310720 | tf_op jit(solution)/shard_map/all_to_all | solution.py:987
  284.3 4.2 %add.225 = bf16[16,24,2432]{2,1,0:T(8,128)(2,1)} custom-call(bf16[16,24,2432]{2,1,0:T(8,128)(2,1)} %get-tuple-element.129.left, bf16[16,24,2432]{2,1,0:T(8,128)(2,1)} %collective-permute-done.5.right), custom_call_target="tpu_custom_call" | custom-call | flops 1000000 | bytes 100000 | tf_op jit(solution)/shard_map/add/pallas_call | solution.py:174
  291.2 10.9 %all-to-all-done.5.gathered = f32[32,40,128]{2,1,0:T(8,128)} async-done(((f32[32,40,128]{2,1,0:T(8,128)}), f32[32,40,128]{2,1,0:T(8,128)}, u32[]{:S(2)}, u32[]{:S(2)}) %all-to-all-start.5) | async-done | bytes 655392 | tf_op jit(solution)/shard_map/all_to_all | solution.py:987
  303.8 3.5 all-to-all-start.6
  311.7 9.3 %token_grad.1 = bf16[1024,768]{1,0:T(8,128)(2,1)} custom-call(bf16[3,1024,768]{2,1,0:T(8,128)(2,1)} %attention_grad.1.grads, bf16[768,2432]{1,0:T(8,128)(2,1)} %bitcast.75, f32[1024,768]{1,0:T(8,128)} %get-tuple-element.140.grad_first), custom_call_target="tpu_custom_call" | custom-call | flops 1000000 | bytes 100000 | tf_op jit(solution)/shard_map/token_grad/pallas_call | solution.py:998
  324.4 6.7 %collective-permute-done.8 = bf16[4,24,2432]{2,1,0:T(8,128)(2,1)S(1)} collective-permute-done((bf16[4,24,2432]{2,1,0:T(8,128)(2,1)}, bf16[4,24,2432]{2,1,0:T(8,128)(2,1)S(1)}, u32[]{:S(2)}, u32[]{:S(2)}) %collective-permute-start.8) | collective-permute-done | bytes 466976 | tf_op jit(solution)/shard_map/ppermute | solution.py:145
  331.1 5.8 %all-to-all-done.6.refs_0_ = bf16[4,1,24,3968]{3,2,1,0:T(8,128)(2,1)S(1)} async-done(((bf16[4,1,24,3968]{3,2,1,0:T(8,128)(2,1)}), bf16[4,1,24,3968]{3,2,1,0:T(8,128)(2,1)S(1)}, u32[]{:S(2)}, u32[]{:S(2)}) %all-to-all-start.6) | async-done | bytes 761888 | tf_op jit(solution)/shard_map/all_to_all | solution.py:112
  (145 shorter events, 67.1 us)
Async XLA Ops:
  7.2 111.9 %all-gather.2.cloned.1.call-start = ((), (), s32[]{:S(2)}) async-start(), calls=%async_computation.9 | async-start | bytes 11151360 | tf_op jit(solution)/shard_map/all_gather | solution.py:788
  11.8 31.5 %collective-permute-start = (bf16[4,192,768]{2,1,0:T(8,128)(2,1)S(1)}, bf16[4,192,768]{2,1,0:T(8,128)(2,1)}, u32[]{:S(2)}, u32[]{:S(2)}) collective-permute-start(bf16[4,192,768]{2,1,0:T(8,128)(2,1)S(1)} %get-tuple-element.290), channel_id=1, source_target_pairs={{0,4},{4,0},{1,5},{5,1},{2,6},{6,2},{3,7},{7,3},{8,12},{12,8},{9,1... | collective-permute-start | bytes 3538952 | tf_op jit(solution)/shard_map/ppermute | solution.py:200
  44.6 32.3 %all-to-all-start.1 = ((bf16[4,4,24,2432]{3,2,1,0:T(8,128)(2,1)}), bf16[4,4,24,2432]{3,2,1,0:T(8,128)(2,1)S(1)}, u32[]{:S(2)}, u32[]{:S(2)}) async-start(bf16[4,4,24,2432]{3,2,1,0:T(8,128)(2,1)} %broadcast_in_dim.97), calls=%async_computation.1 | async-start | bytes 3735552 | tf_op jit(solution)/shard_map/all_to_all | solution.py:119
  110.0 45.1 %collective-permute-start.1 = (bf16[384,768]{1,0:T(8,128)(2,1)}, bf16[384,768]{1,0:T(8,128)(2,1)S(1)}, u32[]{:S(2)}, u32[]{:S(2)}) collective-permute-start(bf16[384,768]{1,0:T(8,128)(2,1)} %get-tuple-element.288), channel_id=1, source_target_pairs={{0,8},{8,16},{16,24},{24,0},{1,9},{9,17},{17,25},{25,1},{2,10},{10... | collective-permute-start | bytes 1769480 | tf_op jit(solution)/shard_map/ppermute | solution.py:214
  111.5 43.6 %collective-permute-start.2 = (bf16[384,768]{1,0:T(8,128)(2,1)S(1)}, bf16[384,768]{1,0:T(8,128)(2,1)S(1)}, u32[]{:S(2)}, u32[]{:S(2)}) collective-permute-start(bf16[384,768]{1,0:T(8,128)(2,1)S(1)} %get-tuple-element.287), channel_id=1, source_target_pairs={{0,16},{8,24},{16,0},{24,8},{1,17},{9,25},{17,1},{25,9},{2,18},{10... | collective-permute-start | bytes 1769480 | tf_op jit(solution)/shard_map/ppermute | solution.py:214
  113.9 41.2 %collective-permute-start.3 = (bf16[384,768]{1,0:T(8,128)(2,1)S(1)}, bf16[384,768]{1,0:T(8,128)(2,1)S(1)}, u32[]{:S(2)}, u32[]{:S(2)}) collective-permute-start(bf16[384,768]{1,0:T(8,128)(2,1)S(1)} %get-tuple-element.286), channel_id=1, source_target_pairs={{0,24},{8,0},{16,8},{24,16},{1,25},{9,1},{17,9},{25,17},{2,26},{10... | collective-permute-start | bytes 1769480 | tf_op jit(solution)/shard_map/ppermute | solution.py:214
  156.3 75.2 %all-to-all-start.3 = ((bf16[8,192,768]{2,1,0:T(8,128)(2,1)}), bf16[8,192,768]{2,1,0:T(8,128)(2,1)S(1)}, u32[]{:S(2)}, u32[]{:S(2)}) async-start(bf16[8,192,768]{2,1,0:T(8,128)(2,1)} %bitcast.79), calls=%async_computation.3 | async-start | bytes 4718592 | tf_op jit(solution)/shard_map/all_to_all | solution.py:907
  169.1 119.4 %reduce-scatter.3.cloned.1.call-start = ((), (), s32[]{:S(2)}) async-start(), calls=%async_computation.10 | async-start | bytes 5750784 | tf_op jit(solution)/shard_map/reduce_scatter | solution.py:132
  220.6 5.9 %collective-permute-start.4 = (bf16[16,24,3968]{2,1,0:T(8,128)(2,1)}, bf16[16,24,3968]{2,1,0:T(8,128)(2,1)}, u32[]{:S(2)}, u32[]{:S(2)}) collective-permute-start(bf16[16,24,3968]{2,1,0:T(8,128)(2,1)} %get-tuple-element.115), channel_id=1, source_target_pairs={{0,1},{1,0},{2,3},{3,2},{4,5},{5,4},{6,7},{7,6},{8,9},{9,8},{10,11... | collective-permute-start | bytes 9142280 | tf_op jit(solution)/shard_map/ppermute | solution.py:259
  232.9 45.6 %all-to-all-start.4 = ((bf16[4,4,24,3968]{3,2,1,0:T(8,128)(2,1)}), bf16[4,4,24,3968]{3,2,1,0:T(8,128)(2,1)S(1)}, u32[]{:S(2)}, u32[]{:S(2)}) async-start(bf16[4,4,24,3968]{3,2,1,0:T(8,128)(2,1)} %bitcast.77), calls=%async_computation.4 | async-start | bytes 6094848 | tf_op jit(solution)/shard_map/all_to_all | solution.py:112
  263.1 15.4 %copy-start.12 = (f32[40,128]{1,0:T(8,128)S(1)}, f32[40,128]{1,0:T(8,128)}, u32[]{:S(2)}) copy-start(f32[40,128]{1,0:T(8,128)} %get-tuple-element.135) | copy-start | bytes 61444
  278.5 5.8 %collective-permute-start.5 = (bf16[16,24,2432]{2,1,0:T(8,128)(2,1)}, bf16[16,24,2432]{2,1,0:T(8,128)(2,1)}, u32[]{:S(2)}, u32[]{:S(2)}) collective-permute-start(bf16[16,24,2432]{2,1,0:T(8,128)(2,1)} %get-tuple-element.130), channel_id=1, source_target_pairs={{0,1},{1,0},{2,3},{3,2},{4,5},{5,4},{6,7},{7,6},{8,9},{9,8},{10,11... | collective-permute-start | bytes 5603336 | tf_op jit(solution)/shard_map/ppermute | solution.py:259
  279.4 22.7 %all-to-all-start.5 = ((f32[32,40,128]{2,1,0:T(8,128)}), f32[32,40,128]{2,1,0:T(8,128)}, u32[]{:S(2)}, u32[]{:S(2)}) async-start(f32[32,40,128]{2,1,0:T(8,128)} %broadcast_in_dim.103), calls=%async_computation.6 | async-start | bytes 1310720 | tf_op jit(solution)/shard_map/all_to_all | solution.py:987
  284.3 52.7 %reduce-scatter.5.cloned.1.call-start = ((), (), s32[]{:S(2)}) async-start(), calls=%async_computation.11 | async-start | bytes 798720 | tf_op jit(solution)/shard_map/reduce_scatter | solution.py:135
  303.8 33.2 %all-to-all-start.6 = ((bf16[4,1,24,3968]{3,2,1,0:T(8,128)(2,1)}), bf16[4,1,24,3968]{3,2,1,0:T(8,128)(2,1)S(1)}, u32[]{:S(2)}, u32[]{:S(2)}) async-start(bf16[4,1,24,3968]{3,2,1,0:T(8,128)(2,1)} %bitcast.83), calls=%async_computation.7 | async-start | bytes 1523712 | tf_op jit(solution)/shard_map/all_to_all | solution.py:112
  307.3 17.1 %collective-permute-start.6 = (bf16[4,24,2432]{2,1,0:T(8,128)(2,1)}, bf16[4,24,2432]{2,1,0:T(8,128)(2,1)S(1)}, u32[]{:S(2)}, u32[]{:S(2)}) collective-permute-start(bf16[4,24,2432]{2,1,0:T(8,128)(2,1)} %get-tuple-element.294), channel_id=1, source_target_pairs={{0,2},{2,4},{4,6},{6,0},{1,3},{3,5},{5,7},{7,1},{8,10},{10,12},{12... | collective-permute-start | bytes 1400840 | tf_op jit(solution)/shard_map/ppermute | solution.py:145
  308.7 15.7 %collective-permute-start.7 = (bf16[4,24,2432]{2,1,0:T(8,128)(2,1)}, bf16[4,24,2432]{2,1,0:T(8,128)(2,1)S(1)}, u32[]{:S(2)}, u32[]{:S(2)}) collective-permute-start(bf16[4,24,2432]{2,1,0:T(8,128)(2,1)} %get-tuple-element.293), channel_id=1, source_target_pairs={{0,4},{2,6},{4,0},{6,2},{1,5},{3,7},{5,1},{7,3},{8,12},{10,14},{12... | collective-permute-start | bytes 1400840 | tf_op jit(solution)/shard_map/ppermute | solution.py:145
  310.2 20.9 %collective-permute-start.8 = (bf16[4,24,2432]{2,1,0:T(8,128)(2,1)}, bf16[4,24,2432]{2,1,0:T(8,128)(2,1)S(1)}, u32[]{:S(2)}, u32[]{:S(2)}) collective-permute-start(bf16[4,24,2432]{2,1,0:T(8,128)(2,1)} %get-tuple-element.292), channel_id=1, source_target_pairs={{0,6},{2,0},{4,2},{6,4},{1,7},{3,1},{5,3},{7,5},{8,14},{10,8},{12,... | collective-permute-start | bytes 1400840 | tf_op jit(solution)/shard_map/ppermute | solution.py:145
  323.1 19.8 %copy-start.11 = (f32[128,128]{1,0:T(8,128)S(1)}, f32[128,128]{1,0:T(8,128)}, u32[]{:S(2)}) copy-start(f32[128,128]{1,0:T(8,128)} %get-tuple-element.160) | copy-start | bytes 196612
  324.4 12.5 %copy-start.6 = (bf16[4,24,2432]{2,1,0:T(8,128)(2,1)}, bf16[4,24,2432]{2,1,0:T(8,128)(2,1)S(1)}, u32[]{:S(2)}) copy-start(bf16[4,24,2432]{2,1,0:T(8,128)(2,1)S(1)} %collective-permute-done.6) | copy-start | bytes 1400836
  337.0 18.4 %copy-start.1 = (bf16[8,192,768]{2,1,0:T(8,128)(2,1)S(1)}, bf16[8,192,768]{2,1,0:T(8,128)(2,1)}, u32[]{:S(2)}) copy-start(bf16[8,192,768]{2,1,0:T(8,128)(2,1)} %copy-done) | copy-start | bytes 7077892
  339.7 11.8 %collective-permute-start.10 = (bf16[1,24,2432]{2,1,0:T(8,128)(2,1)}, bf16[1,24,2432]{2,1,0:T(8,128)(2,1)S(1)}, u32[]{:S(2)}, u32[]{:S(2)}) collective-permute-start(bf16[1,24,2432]{2,1,0:T(8,128)(2,1)} %get-tuple-element.297), channel_id=1, source_target_pairs={{0,16},{8,24},{16,0},{24,8},{1,17},{9,25},{17,1},{25,9},{2,18},{10... | collective-permute-start | bytes 350216 | tf_op jit(solution)/shard_map/ppermute | solution.py:145
  339.7 11.8 %collective-permute-start.11 = (bf16[1,24,2432]{2,1,0:T(8,128)(2,1)S(1)}, bf16[1,24,2432]{2,1,0:T(8,128)(2,1)}, u32[]{:S(2)}, u32[]{:S(2)}) collective-permute-start(bf16[1,24,2432]{2,1,0:T(8,128)(2,1)S(1)} %get-tuple-element.296), channel_id=1, source_target_pairs={{0,24},{8,0},{16,8},{24,16},{1,25},{9,1},{17,9},{25,17},{2,26},{10... | collective-permute-start | bytes 350216 | tf_op jit(solution)/shard_map/ppermute | solution.py:145
  341.1 10.4 %collective-permute-start.9 = (bf16[1,24,2432]{2,1,0:T(8,128)(2,1)S(1)}, bf16[1,24,2432]{2,1,0:T(8,128)(2,1)}, u32[]{:S(2)}, u32[]{:S(2)}) collective-permute-start(bf16[1,24,2432]{2,1,0:T(8,128)(2,1)S(1)} %get-tuple-element.298), channel_id=1, source_target_pairs={{0,8},{8,16},{16,24},{24,0},{1,9},{9,17},{17,25},{25,1},{2,10},{10... | collective-permute-start | bytes 350216 | tf_op jit(solution)/shard_map/ppermute | solution.py:145
  (22 other events, 111.5 us)
Sparse Core Ops, SparseCore 0:
  10.9 100.6 all-gather.1
  190.0 79.5 reduce-scatter.2
  302.3 29.2 reduce-scatter.4

commit v4 on v3

--- a/solution.py
+++ b/solution.py
@@ -990,10 +990,10 @@
     third = sums.first_stage(third)
     third, second_arrived, first_part = lax.optimization_barrier((third, second_arrived, first_part))
     third_arrived = layout.permutes(third, 1)
-    third_arrived[0], second_arrived, small, first_part = lax.optimization_barrier(
-        (third_arrived[0], second_arrived, small, first_part)
-    )
     first_part = layout.last_sum(first_part)
+    third_arrived[1], second_arrived, small = lax.optimization_barrier(
+        (third_arrived[1], second_arrived, small)
+    )
     second_arrived = layout.exchange(layout.total(second_arrived), 2)
     tokens_grad = pl.pallas_call(
         token_grad_body,
@@ -1013,8 +1013,8 @@
         cost_estimate=cost(1e6, 1e5),
         name="head_sums",
     )(small)
-    third_arrived, second_arrived, first_part, tokens_grad, dense_weight_grad = lax.optimization_barrier(
-        (third_arrived, second_arrived, first_part, tokens_grad, dense_weight_grad)
+    third_arrived, first_part, tokens_grad, dense_weight_grad = lax.optimization_barrier(
+        (third_arrived, first_part, tokens_grad, dense_weight_grad)
     )
     third = layout.total(third_arrived)
     third_arrived = layout.permutes(third, 2)

time: 370 us -> 367 us (level)
  waiting for transfers between devices: 63.5 us -> 55 us
    all_to_all x1, waiting for transfers between devices: 10.9 us -> 4.28 us  [local(): lax.all_to_all(jnp.broadcast_to(small, (count,) + small.shape), axes, spl...]
    all_to_all x2, waiting for transfers between devices: 12.7 us -> 6.84 us  [exchange(): lax.all_to_all(value, self.stages[stage], split_axis=0, concat_axis=0, ti...]
    ppermute x6, waiting for transfers between devices: 6.68 us -> 10.7 us  [permutes(): parts.append(lax.ppermute(part, axes, pairs))]
    unnamed x60 -> x54, local copies, waits for them, and re-layouts: 7.91 us -> 8.79 us
  transfers between devices with their start and end apart: 20 -> 20, of which waited for: 7 -> 6; matrix products, arithmetic and copies ran while one was open for 8% -> 9% of each run, Pallas kernels for 46% -> 46%
where the time goes in v4:
time: 367 us; the launch traced here: 360 us
  Pallas kernels  171 us (47%)
  waiting for transfers between devices  55 us (15%)
  starting transfers between devices  48 us (13%)
  local copies, waits for them, and re-layouts  32.9 us (9%)
  blocking collectives  31.8 us (9%)
  between operations  14.3 us (4%)
  other arithmetic  7.15 us (2%)
    all_to_all x2, blocking collectives, gather(): lax.all_to_all(copies, self.stages[stage], split_axis=0, concat_axis=0, t...  31.8 us
    pallas_call x1, Pallas kernels, local(): pl.pallas_call(functools.partial(up_grad_body, sums=sums, ratio=ratio), g...  30.7 us
    pallas_call x1, Pallas kernels, local(): pl.pallas_call(attention_grad_body, grid=(micro, blocks), in_specs=[pl.Bl...  25.8 us
    all_to_all x1, waiting for transfers between devices, gather(): lax.all_to_all(copies, self.stages[stage], split_axis=0, concat_axis=0, t...  24.8 us
    pallas_call x1, Pallas kernels, local(): pl.pallas_call(forward_body, grid=(ratio,), in_specs=[full_spec, full_spe...  24.5 us
    pallas_call x1, Pallas kernels, local(): pl.pallas_call(attention_body, grid=(micro, blocks), in_specs=[pl.BlockSp...  20.9 us
    pallas_call x1, Pallas kernels, local(): pl.pallas_call(functools.partial(down_grad_body, ratio=ratio, place=layou...  19.2 us
    all_to_all x1, starting transfers between devices, local(): lax.all_to_all(outgoing, layout.dp, split_axis=0, concat_axis=0, tiled=True)  12.9 us
  transfers between devices with their start and end apart: 20, of which 6 were waited for; matrix products, arithmetic and copies ran while one was open for 9% of the time, Pallas kernels for 46%

profile of v4, /device:TPU:0, one launch (start us, length us, event | category | flops | bytes accessed | tf_op | source)
XLA Modules:
  0.0 360.2 jit_solution(17999153755050822732)
XLA Ops:
  11.8 3.0 collective-permute-start
  15.9 24.9 %all_to_all.42 = bf16[4,24,2432]{2,1,0:T(8,128)(2,1)S(1)} all-to-all(bf16[4,24,2432]{2,1,0:T(8,128)(2,1)S(1)} %broadcast_in_dim.96), channel_id=1, replica_groups=mesh['z'=4,'x'=2,'y'=2,'core'=2] {'z'}, dimensions={0} | all-to-all | bytes 933888 | tf_op jit(solution)/shard_map/all_to_all | solution.py:119
  44.6 4.1 %all-to-all-start.1 = ((bf16[4,4,24,2432]{3,2,1,0:T(8,128)(2,1)}), bf16[4,4,24,2432]{3,2,1,0:T(8,128)(2,1)S(1)}, u32[]{:S(2)}, u32[]{:S(2)}) async-start(bf16[4,4,24,2432]{3,2,1,0:T(8,128)(2,1)} %broadcast_in_dim.97), calls=%async_computation.1 | async-start | bytes 3735552 | tf_op jit(solution)/shard_map/all_to_all | solution.py:119
  52.1 24.8 %all-to-all-done.1 = bf16[4,4,24,2432]{3,2,1,0:T(8,128)(2,1)S(1)} async-done(((bf16[4,4,24,2432]{3,2,1,0:T(8,128)(2,1)}), bf16[4,4,24,2432]{3,2,1,0:T(8,128)(2,1)S(1)}, u32[]{:S(2)}, u32[]{:S(2)}) %all-to-all-start.1) | async-done | bytes 1867808 | tf_op jit(solution)/shard_map/all_to_all | solution.py:119
  77.4 6.9 %all_to_all.43 = bf16[2,4,4,24,2432]{4,3,1,2,0:T(8,128)(2,1)S(1)} all-to-all(bf16[2,4,4,24,2432]{4,3,1,2,0:T(8,128)(2,1)S(1)} %broadcast_in_dim.98), channel_id=1, replica_groups=mesh['z'=4,'x'=2,'y'=2,'core'=2] {'core'}, dimensions={0} | all-to-all | bytes 7471104 | tf_op jit(solution)/shard_map/all_to_all | solution.py:119
  86.4 20.9 %attention.1 = (bf16[1024,768]{1,0:T(8,128)(2,1)}, bf16[1024,768]{1,0:T(8,128)(2,1)}, bf16[1024,768]{1,0:T(8,128)(2,1)}, bf16[1024,768]{1,0:T(8,128)(2,1)}, f32[6,8,512]{2,1,0:T(8,128)}) custom-call(bf16[1024,768]{1,0:T(8,128)(2,1)} %tokens.5, s32[2,512,1]{2,1,0:T(8,128)} %copy.123.seg_column, s32[2,1,512]{2,1,0:T(1,128)} %broadcast_in_dim.86.seg_row, ...), custom_call_target="tpu_custom_call" | custom-call | flops 1000000 | bytes 100000 | tf_op jit(solution)/shard_map/attention/pallas_call | solution.py:837
  119.1 24.5 %forward.1 = (f32[1024,768]{1,0:T(8,128)}, bf16[1024,768]{1,0:T(8,128)(2,1)}, bf16[1024,3072]{1,0:T(8,128)(2,1)}, bf16[1024,3072]{1,0:T(8,128)(2,1)}, f32[1024,7...) custom-call(bf16[1024,768]{1,0:T(8,128)(2,1)} %tokens.5, bf16[1024,768]{1,0:T(8,128)(2,1)} %get-tuple-element.94.context, ...), custom_call_target="tpu_custom_call" | custom-call | flops 1000000 | bytes 100000 | tf_op jit(solution)/shard_map/forward/pallas_call | solution.py:859
  143.6 5.8 %select.27 = bf16[1536,768]{1,0:T(8,128)(2,1)} custom-call(s32[1536,1]{1,0:T(8,128)} %select_n.98.index, bf16[1024,768]{1,0:T(8,128)(2,1)} %get-tuple-element.95.source.outputs), custom_call_target="tpu_custom_call" | custom-call | flops 1000000 | bytes 100000 | tf_op jit(solution)/shard_map/select/pallas_call | solution.py:880
  149.4 5.6 %student.3 = (f32[8,14]{1,0:T(8,128)}, bf16[1024,128]{1,0:T(8,128)(2,1)}, f32[40,128]{1,0:T(8,128)}) custom-call(f32[1024,128]{1,0:T(8,128)} %get-tuple-element.96.student_rows, s32[1024,1]{1,0:T(8,128)} %bitcast.85, f32[1,128]{1,0:T(1,128)} %bitcast.90, f32[128,128]{1,0:T(8,128)} %dense_weight.1, f32[1,128]{1,0:T(1,128)} %bitcast.91, ...), custom_call_target="tpu_custom_call" | custom-call | flops 1000000 | bytes 100000 | tf_op jit(solution)/shard_map/student/pallas_call | solution.py:892
  156.3 12.9 %all-to-all-start.3 = ((bf16[8,192,768]{2,1,0:T(8,128)(2,1)}), bf16[8,192,768]{2,1,0:T(8,128)(2,1)S(1)}, u32[]{:S(2)}, u32[]{:S(2)}) async-start(bf16[8,192,768]{2,1,0:T(8,128)(2,1)} %bitcast.79), calls=%async_computation.3 | async-start | bytes 4718592 | tf_op jit(solution)/shard_map/all_to_all | solution.py:907
  170.6 19.2 %down_grad.1 = (f32[1024,768]{1,0:T(8,128)}, bf16[1024,768]{1,0:T(8,128)(2,1)}, bf16[32,24,3328]{2,1,0:T(8,128)(2,1)}) custom-call(s32[1024,1]{1,0:T(8,128)} %compare_select_fusion.slot, bf16[1024,128]{1,0:T(8,128)(2,1)} %get-tuple-element.100.student_grad, bf16[768,7040]{1,0:T(8,128)(2,1)} %all-gather.2.cloned.1.call-done.out_weight.up.down.student, ...), custom_call_target="tpu_custom_call" | custom-call | flops 1000000 | bytes 100000 | tf_op jit(solution)/shard_map/down_grad/pallas_call | solution.py:911
  189.9 30.7 %up_grad.1 = (f32[1024,768]{1,0:T(8,128)}, bf16[1024,768]{1,0:T(8,128)(2,1)}, bf16[16,24,3968]{2,1,0:T(8,128)(2,1)}, bf16[16,24,3968]{2,1,0:T(8,128)(2,1)}) custom-call(s32[1]{0:T(128)} %bitcast.core, bf16[1024,768]{1,0:T(8,128)(2,1)} %get-tuple-element.107.grad_down, f32[1024,768]{1,0:T(8,128)} %get-tuple-element.108.grad_second, ...), custom_call_target="tpu_custom_call" | custom-call | flops 1000000 | bytes 100000 | tf_op jit(solution)/shard_map/up_grad/pallas_call | solution.py:936
  220.6 5.9 %collective-permute-done.4.right = bf16[16,24,3968]{2,1,0:T(8,128)(2,1)} collective-permute-done((bf16[16,24,3968]{2,1,0:T(8,128)(2,1)}, bf16[16,24,3968]{2,1,0:T(8,128)(2,1)}, u32[]{:S(2)}, u32[]{:S(2)}) %collective-permute-start.4) | collective-permute-done | bytes 3047456 | tf_op jit(solution)/shard_map/ppermute | solution.py:259
  226.4 5.1 %add.224 = bf16[16,24,3968]{2,1,0:T(8,128)(2,1)} custom-call(bf16[16,24,3968]{2,1,0:T(8,128)(2,1)} %get-tuple-element.112.left, bf16[16,24,3968]{2,1,0:T(8,128)(2,1)} %collective-permute-done.4.right), custom_call_target="tpu_custom_call" | custom-call | flops 1000000 | bytes 100000 | tf_op jit(solution)/shard_map/add/pallas_call | solution.py:174
  232.9 4.3 %all-to-all-start.4 = ((bf16[4,4,24,3968]{3,2,1,0:T(8,128)(2,1)}), bf16[4,4,24,3968]{3,2,1,0:T(8,128)(2,1)S(1)}, u32[]{:S(2)}, u32[]{:S(2)}) async-start(bf16[4,4,24,3968]{3,2,1,0:T(8,128)(2,1)} %bitcast.77), calls=%async_computation.4 | async-start | bytes 6094848 | tf_op jit(solution)/shard_map/all_to_all | solution.py:112
  237.2 25.8 %attention_grad.1.grads = bf16[3,1024,768]{2,1,0:T(8,128)(2,1)} custom-call(bf16[1024,768]{1,0:T(8,128)(2,1)} %get-tuple-element.118.branch, s32[2,512,1]{2,1,0:T(8,128)} %copy.123.seg_column, s32[2,1,512]{2,1,0:T(1,128)} %broadcast_in_dim.86.seg_row, bf16[1024,768]{1,0:T(8,128)(2,1)} %get-tuple-element.119.query, bf16[1024,768]{1,0:T(8,128)(2,1)} %get-tuple-element.120.key, ...), custom_call_target="tpu_custom_call" | custom-call | flops 1000000 | bytes 100000 | tf_op jit(solution)/shard_map/attention_grad/pallas_call | solution.py:958
  263.1 8.6 %qkv_grad.1 = (bf16[16,24,2432]{2,1,0:T(8,128)(2,1)}, bf16[16,24,2432]{2,1,0:T(8,128)(2,1)}) custom-call(s32[1]{0:T(128)} %bitcast.core, bf16[1024,768]{1,0:T(8,128)(2,1)} %tokens.5, bf16[3,1024,768]{2,1,0:T(8,128)(2,1)} %attention_grad.1.grads), custom_call_target="tpu_custom_call" | custom-call | flops 1000000 | bytes 100000 | tf_op jit(solution)/shard_map/qkv_grad/pallas_call | solution.py:975
  271.7 6.8 %all-to-all-done.4 = bf16[4,4,24,3968]{3,2,1,0:T(8,128)(2,1)S(1)} async-done(((bf16[4,4,24,3968]{3,2,1,0:T(8,128)(2,1)}), bf16[4,4,24,3968]{3,2,1,0:T(8,128)(2,1)S(1)}, u32[]{:S(2)}, u32[]{:S(2)}) %all-to-all-start.4) | async-done | bytes 3047456 | tf_op jit(solution)/shard_map/all_to_all | solution.py:112
  279.4 4.8 %all-to-all-start.5 = ((f32[32,40,128]{2,1,0:T(8,128)}), f32[32,40,128]{2,1,0:T(8,128)}, u32[]{:S(2)}, u32[]{:S(2)}) async-start(f32[32,40,128]{2,1,0:T(8,128)} %broadcast_in_dim.103), calls=%async_computation.6 | async-start | bytes 1310720 | tf_op jit(solution)/shard_map/all_to_all | solution.py:987
  284.3 4.2 %add.225 = bf16[16,24,2432]{2,1,0:T(8,128)(2,1)} custom-call(bf16[16,24,2432]{2,1,0:T(8,128)(2,1)} %get-tuple-element.127.left, bf16[16,24,2432]{2,1,0:T(8,128)(2,1)} %collective-permute-done.5.right), custom_call_target="tpu_custom_call" | custom-call | flops 1000000 | bytes 100000 | tf_op jit(solution)/shard_map/add/pallas_call | solution.py:174
  295.8 9.3 %token_grad.1 = bf16[1024,768]{1,0:T(8,128)(2,1)} custom-call(bf16[3,1024,768]{2,1,0:T(8,128)(2,1)} %attention_grad.1.grads, bf16[768,2432]{1,0:T(8,128)(2,1)} %bitcast.75, f32[1024,768]{1,0:T(8,128)} %get-tuple-element.136.grad_first), custom_call_target="tpu_custom_call" | custom-call | flops 1000000 | bytes 100000 | tf_op jit(solution)/shard_map/token_grad/pallas_call | solution.py:998
  305.0 4.3 %all-to-all-done.5.gathered = f32[32,40,128]{2,1,0:T(8,128)} async-done(((f32[32,40,128]{2,1,0:T(8,128)}), f32[32,40,128]{2,1,0:T(8,128)}, u32[]{:S(2)}, u32[]{:S(2)}) %all-to-all-start.5) | async-done | bytes 655392 | tf_op jit(solution)/shard_map/all_to_all | solution.py:987
  310.9 3.5 all-to-all-start.6
  330.7 10.7 %collective-permute-done.10.refs_2_ = bf16[1,24,2432]{2,1,0:T(8,128)(2,1)S(1)} collective-permute-done((bf16[1,24,2432]{2,1,0:T(8,128)(2,1)}, bf16[1,24,2432]{2,1,0:T(8,128)(2,1)S(1)}, u32[]{:S(2)}, u32[]{:S(2)}) %collective-permute-start.10) | collective-permute-done | bytes 116768 | tf_op jit(solution)/shard_map/ppermute | solution.py:145
  (140 shorter events, 69.4 us)
Async XLA Ops:
  7.2 111.9 %all-gather.2.cloned.1.call-start = ((), (), s32[]{:S(2)}) async-start(), calls=%async_computation.9 | async-start | bytes 11151360 | tf_op jit(solution)/shard_map/all_gather | solution.py:788
  11.8 31.5 %collective-permute-start = (bf16[4,192,768]{2,1,0:T(8,128)(2,1)S(1)}, bf16[4,192,768]{2,1,0:T(8,128)(2,1)}, u32[]{:S(2)}, u32[]{:S(2)}) collective-permute-start(bf16[4,192,768]{2,1,0:T(8,128)(2,1)S(1)} %get-tuple-element.286), channel_id=1, source_target_pairs={{0,4},{4,0},{1,5},{5,1},{2,6},{6,2},{3,7},{7,3},{8,12},{12,8},{9,1... | collective-permute-start | bytes 3538952 | tf_op jit(solution)/shard_map/ppermute | solution.py:200
  44.6 32.3 %all-to-all-start.1 = ((bf16[4,4,24,2432]{3,2,1,0:T(8,128)(2,1)}), bf16[4,4,24,2432]{3,2,1,0:T(8,128)(2,1)S(1)}, u32[]{:S(2)}, u32[]{:S(2)}) async-start(bf16[4,4,24,2432]{3,2,1,0:T(8,128)(2,1)} %broadcast_in_dim.97), calls=%async_computation.1 | async-start | bytes 3735552 | tf_op jit(solution)/shard_map/all_to_all | solution.py:119
  108.8 9.5 %copy-start.10 = (f32[128,14]{0,1:T(8,128)S(1)}, f32[128,14]{0,1:T(8,128)}, u32[]{:S(2)}) copy-start(f32[128,14]{0,1:T(8,128)} %param.50) | copy-start | bytes 21508
  110.0 45.0 %collective-permute-start.1 = (bf16[384,768]{1,0:T(8,128)(2,1)}, bf16[384,768]{1,0:T(8,128)(2,1)S(1)}, u32[]{:S(2)}, u32[]{:S(2)}) collective-permute-start(bf16[384,768]{1,0:T(8,128)(2,1)} %get-tuple-element.284), channel_id=1, source_target_pairs={{0,8},{8,16},{16,24},{24,0},{1,9},{9,17},{17,25},{25,1},{2,10},{10... | collective-permute-start | bytes 1769480 | tf_op jit(solution)/shard_map/ppermute | solution.py:214
  111.5 43.5 %collective-permute-start.2 = (bf16[384,768]{1,0:T(8,128)(2,1)S(1)}, bf16[384,768]{1,0:T(8,128)(2,1)S(1)}, u32[]{:S(2)}, u32[]{:S(2)}) collective-permute-start(bf16[384,768]{1,0:T(8,128)(2,1)S(1)} %get-tuple-element.283), channel_id=1, source_target_pairs={{0,16},{8,24},{16,0},{24,8},{1,17},{9,25},{17,1},{25,9},{2,18},{10... | collective-permute-start | bytes 1769480 | tf_op jit(solution)/shard_map/ppermute | solution.py:214
  113.9 41.1 %collective-permute-start.3 = (bf16[384,768]{1,0:T(8,128)(2,1)S(1)}, bf16[384,768]{1,0:T(8,128)(2,1)S(1)}, u32[]{:S(2)}, u32[]{:S(2)}) collective-permute-start(bf16[384,768]{1,0:T(8,128)(2,1)S(1)} %get-tuple-element.282), channel_id=1, source_target_pairs={{0,24},{8,0},{16,8},{24,16},{1,25},{9,1},{17,9},{25,17},{2,26},{10... | collective-permute-start | bytes 1769480 | tf_op jit(solution)/shard_map/ppermute | solution.py:214
  156.3 75.2 %all-to-all-start.3 = ((bf16[8,192,768]{2,1,0:T(8,128)(2,1)}), bf16[8,192,768]{2,1,0:T(8,128)(2,1)S(1)}, u32[]{:S(2)}, u32[]{:S(2)}) async-start(bf16[8,192,768]{2,1,0:T(8,128)(2,1)} %bitcast.79), calls=%async_computation.3 | async-start | bytes 4718592 | tf_op jit(solution)/shard_map/all_to_all | solution.py:907
  169.1 119.4 %reduce-scatter.3.cloned.1.call-start = ((), (), s32[]{:S(2)}) async-start(), calls=%async_computation.10 | async-start | bytes 5750784 | tf_op jit(solution)/shard_map/reduce_scatter | solution.py:132
  220.6 5.9 %collective-permute-start.4 = (bf16[16,24,3968]{2,1,0:T(8,128)(2,1)}, bf16[16,24,3968]{2,1,0:T(8,128)(2,1)}, u32[]{:S(2)}, u32[]{:S(2)}) collective-permute-start(bf16[16,24,3968]{2,1,0:T(8,128)(2,1)} %get-tuple-element.113), channel_id=1, source_target_pairs={{0,1},{1,0},{2,3},{3,2},{4,5},{5,4},{6,7},{7,6},{8,9},{9,8},{10,11... | collective-permute-start | bytes 9142280 | tf_op jit(solution)/shard_map/ppermute | solution.py:259
  232.9 45.6 %all-to-all-start.4 = ((bf16[4,4,24,3968]{3,2,1,0:T(8,128)(2,1)}), bf16[4,4,24,3968]{3,2,1,0:T(8,128)(2,1)S(1)}, u32[]{:S(2)}, u32[]{:S(2)}) async-start(bf16[4,4,24,3968]{3,2,1,0:T(8,128)(2,1)} %bitcast.77), calls=%async_computation.4 | async-start | bytes 6094848 | tf_op jit(solution)/shard_map/all_to_all | solution.py:112
  263.1 15.4 %copy-start.9 = (f32[40,128]{1,0:T(8,128)S(1)}, f32[40,128]{1,0:T(8,128)}, u32[]{:S(2)}) copy-start(f32[40,128]{1,0:T(8,128)} %get-tuple-element.133) | copy-start | bytes 61444
  278.5 5.8 %collective-permute-start.5 = (bf16[16,24,2432]{2,1,0:T(8,128)(2,1)}, bf16[16,24,2432]{2,1,0:T(8,128)(2,1)}, u32[]{:S(2)}, u32[]{:S(2)}) collective-permute-start(bf16[16,24,2432]{2,1,0:T(8,128)(2,1)} %get-tuple-element.128), channel_id=1, source_target_pairs={{0,1},{1,0},{2,3},{3,2},{4,5},{5,4},{6,7},{7,6},{8,9},{9,8},{10,11... | collective-permute-start | bytes 5603336 | tf_op jit(solution)/shard_map/ppermute | solution.py:259
  279.4 29.9 %all-to-all-start.5 = ((f32[32,40,128]{2,1,0:T(8,128)}), f32[32,40,128]{2,1,0:T(8,128)}, u32[]{:S(2)}, u32[]{:S(2)}) async-start(f32[32,40,128]{2,1,0:T(8,128)} %broadcast_in_dim.103), calls=%async_computation.6 | async-start | bytes 1310720 | tf_op jit(solution)/shard_map/all_to_all | solution.py:987
  284.3 33.6 %reduce-scatter.5.cloned.1.call-start = ((), (), s32[]{:S(2)}) async-start(), calls=%async_computation.11 | async-start | bytes 798720 | tf_op jit(solution)/shard_map/reduce_scatter | solution.py:135
  291.1 18.2 %collective-permute-start.6 = (bf16[4,24,2432]{2,1,0:T(8,128)(2,1)S(1)}, bf16[4,24,2432]{2,1,0:T(8,128)(2,1)}, u32[]{:S(2)}, u32[]{:S(2)}) collective-permute-start(bf16[4,24,2432]{2,1,0:T(8,128)(2,1)S(1)} %get-tuple-element.290), channel_id=1, source_target_pairs={{0,2},{2,4},{4,6},{6,0},{1,3},{3,5},{5,7},{7,1},{8,10},{10,12},{12... | collective-permute-start | bytes 1400840 | tf_op jit(solution)/shard_map/ppermute | solution.py:145
  292.9 25.0 %collective-permute-start.7 = (bf16[4,24,2432]{2,1,0:T(8,128)(2,1)}, bf16[4,24,2432]{2,1,0:T(8,128)(2,1)}, u32[]{:S(2)}, u32[]{:S(2)}) collective-permute-start(bf16[4,24,2432]{2,1,0:T(8,128)(2,1)} %get-tuple-element.289), channel_id=1, source_target_pairs={{0,4},{2,6},{4,0},{6,2},{1,5},{3,7},{5,1},{7,3},{8,12},{10,14},{12... | collective-permute-start | bytes 1400840 | tf_op jit(solution)/shard_map/ppermute | solution.py:145
  294.3 23.5 %collective-permute-start.8 = (bf16[4,24,2432]{2,1,0:T(8,128)(2,1)}, bf16[4,24,2432]{2,1,0:T(8,128)(2,1)}, u32[]{:S(2)}, u32[]{:S(2)}) collective-permute-start(bf16[4,24,2432]{2,1,0:T(8,128)(2,1)} %get-tuple-element.288), channel_id=1, source_target_pairs={{0,6},{2,0},{4,2},{6,4},{1,7},{3,1},{5,3},{7,5},{8,14},{10,8},{12,... | collective-permute-start | bytes 1400840 | tf_op jit(solution)/shard_map/ppermute | solution.py:145
  310.9 34.4 %all-to-all-start.6 = ((bf16[4,1,24,3968]{3,2,1,0:T(8,128)(2,1)}), bf16[4,1,24,3968]{3,2,1,0:T(8,128)(2,1)S(1)}, u32[]{:S(2)}, u32[]{:S(2)}) async-start(bf16[4,1,24,3968]{3,2,1,0:T(8,128)(2,1)} %bitcast.83), calls=%async_computation.8 | async-start | bytes 1523712 | tf_op jit(solution)/shard_map/all_to_all | solution.py:112
  316.5 10.0 %copy-start.8 = (f32[128,128]{1,0:T(8,128)S(1)}, f32[128,128]{1,0:T(8,128)}, u32[]{:S(2)}) copy-start(f32[128,128]{1,0:T(8,128)} %get-tuple-element.156) | copy-start | bytes 196612
  317.9 34.2 %copy-start.1 = (bf16[8,192,768]{2,1,0:T(8,128)(2,1)S(1)}, bf16[8,192,768]{2,1,0:T(8,128)(2,1)}, u32[]{:S(2)}) copy-start(bf16[8,192,768]{2,1,0:T(8,128)(2,1)} %copy-done) | copy-start | bytes 7077892
  320.5 20.9 %collective-permute-start.10 = (bf16[1,24,2432]{2,1,0:T(8,128)(2,1)}, bf16[1,24,2432]{2,1,0:T(8,128)(2,1)S(1)}, u32[]{:S(2)}, u32[]{:S(2)}) collective-permute-start(bf16[1,24,2432]{2,1,0:T(8,128)(2,1)} %get-tuple-element.293), channel_id=1, source_target_pairs={{0,16},{8,24},{16,0},{24,8},{1,17},{9,25},{17,1},{25,9},{2,18},{10... | collective-permute-start | bytes 350216 | tf_op jit(solution)/shard_map/ppermute | solution.py:145
  323.4 18.0 %collective-permute-start.11 = (bf16[1,24,2432]{2,1,0:T(8,128)(2,1)S(1)}, bf16[1,24,2432]{2,1,0:T(8,128)(2,1)}, u32[]{:S(2)}, u32[]{:S(2)}) collective-permute-start(bf16[1,24,2432]{2,1,0:T(8,128)(2,1)S(1)} %get-tuple-element.292), channel_id=1, source_target_pairs={{0,24},{8,0},{16,8},{24,16},{1,25},{9,1},{17,9},{25,17},{2,26},{10... | collective-permute-start | bytes 350216 | tf_op jit(solution)/shard_map/ppermute | solution.py:145
  324.8 16.6 %collective-permute-start.9 = (bf16[1,24,2432]{2,1,0:T(8,128)(2,1)S(1)}, bf16[1,24,2432]{2,1,0:T(8,128)(2,1)}, u32[]{:S(2)}, u32[]{:S(2)}) collective-permute-start(bf16[1,24,2432]{2,1,0:T(8,128)(2,1)S(1)} %get-tuple-element.294), channel_id=1, source_target_pairs={{0,8},{8,16},{16,24},{24,0},{1,9},{9,17},{17,25},{25,1},{2,10},{10... | collective-permute-start | bytes 350216 | tf_op jit(solution)/shard_map/ppermute | solution.py:145
  (19 other events, 77.8 us)
Sparse Core Ops, SparseCore 0:
  10.9 100.6 all-gather.1
  190.0 79.4 reduce-scatter.2
  288.6 25.0 reduce-scatter.4

commit v5 on v4

--- a/solution.py
+++ b/solution.py
@@ -169,18 +169,20 @@
 
 def add(left, right):
     parts, part, columns = left.shape
-    step = 4 if parts % 4 == 0 else 1
-    spec = pl.BlockSpec((step, part, columns), lambda i: (i, 0, 0))
-    return pl.pallas_call(
+    rows = parts * part
+    step = next(n for n in (96, 64, 48, 32, rows) if rows % n == 0)
+    spec = pl.BlockSpec((step, columns), lambda i: (i, 0))
+    total = pl.pallas_call(
         add_body,
-        grid=(parts // step,),
+        grid=(rows // step,),
         in_specs=[spec, spec],
         out_specs=spec,
-        out_shape=jax.ShapeDtypeStruct(left.shape, left.dtype),
+        out_shape=jax.ShapeDtypeStruct((rows, columns), left.dtype),
         compiler_params=params(),
         cost_estimate=cost(1e6, 1e5),
         name="add",
-    )(left, right)
+    )(left.reshape(rows, columns), right.reshape(rows, columns))
+    return total.reshape(left.shape)
 
 
 class Return:
@@ -490,10 +492,8 @@
     )
     small[...] = jnp.zeros_like(small)
     small[:pairs] = pooled[:pairs]
-    small[pairs : 2 * pairs] = grad_pre
-    small[2 * pairs : 3 * pairs] = dense[:pairs]
-    small[3 * pairs : 4 * pairs, :classes] = grad
-    at = 4 * pairs
+    small[pairs : 2 * pairs, :classes] = grad
+    at = 2 * pairs
     grad_pooled = right_inner(grad_pre, dense_weight[...], highest)
     grad_token = matmul(one_hot[:, :pairs], grad_pooled, highest)
     grad_score = []
@@ -507,20 +507,34 @@
     small[at + 1 : at + 2] = jnp.sum(widen(result), axis=0, keepdims=True)
 
 
-def head_sums_body(gathered, dense_weight_grad, class_weight_grad, rows, *, pairs):
+def head_sums_body(
+    gathered, dense_weight, dense_bias, class_weight, dense_weight_grad, class_weight_grad, rows, *, pairs
+):
     everyone = gathered[...]
     width = everyone.shape[2]
 
     def factor(i):
         return everyone[:, i * pairs : (i + 1) * pairs].reshape(-1, width)
 
-    pooled, grad_pre, dense, grad = (factor(i) for i in range(4))
-    dense_weight_grad[...] = left_inner(pooled, grad_pre, highest)
-    class_weight_grad[...] = left_inner(dense, grad, highest)
-    total = jnp.sum(everyone[:, 4 * pairs : 4 * pairs + 8], axis=0)
+    pooled, grad = factor(0), factor(1)
+    dense = jnp.tanh(matmul(pooled, dense_weight[...], highest) + dense_bias[...])
+    grad_pre = right_inner(grad[:, : class_weight.shape[1]], class_weight[...], highest) * (
+        1.0 - dense * dense
+    )
+    total = jnp.sum(everyone[:, 2 * pairs : 2 * pairs + 8], axis=0)
     row = lax.broadcasted_iota(jnp.int32, (8, width), 0)
     total = jnp.where(row == 2, jnp.sum(grad_pre, axis=0, keepdims=True), total)
-    rows[...] = jnp.where(row == 3, jnp.sum(grad, axis=0, keepdims=True), total)
+    total = jnp.where(row == 3, jnp.sum(grad, axis=0, keepdims=True), total)
+
+    @pl.when(pl.program_id(0) == 0)
+    def _():
+        dense_weight_grad[...] = jnp.zeros_like(dense_weight_grad)
+        class_weight_grad[...] = jnp.zeros_like(class_weight_grad)
+        rows[...] = jnp.zeros_like(rows)
+
+    dense_weight_grad[...] += left_inner(pooled, grad_pre, highest)
+    class_weight_grad[...] += left_inner(dense, grad, highest)
+    rows[...] += total
 
 
 def norm_grad(grad, pre, gain):
@@ -894,7 +908,7 @@
         out_shape=(
             array(*logits_grad.shape),
             array(token_count, SD, dtype=BF16),
-            array(4 * pairs + 8, SD),
+            array(2 * pairs + 8, SD),
         ),
         compiler_params=params(),
         cost_estimate=cost(1e6, 1e5),
@@ -1006,13 +1020,22 @@
         cost_estimate=cost(1e6, 1e5),
         name="token_grad",
     )(grads, entry, grad_first)
+    group = 32 if count % 32 == 0 else count
     dense_weight_grad, class_weight_grad, head_rows = pl.pallas_call(
         functools.partial(head_sums_body, pairs=pairs),
+        grid=(count // group,),
+        in_specs=[
+            pl.BlockSpec((group,) + small.shape[1:], lambda i: (i, 0, 0)),
+            fixed(dense_weight.shape),
+            fixed((1, SD)),
+            fixed(class_weight.shape),
+        ],
+        out_specs=(fixed((SD, SD)), fixed((SD, SD)), fixed((8, SD))),
         out_shape=(array(SD, SD), array(SD, SD), array(8, SD)),
         compiler_params=params(),
         cost_estimate=cost(1e6, 1e5),
         name="head_sums",
-    )(small)
+    )(small, dense_weight, dense_bias[None, :], class_weight)
     third_arrived, first_part, tokens_grad, dense_weight_grad = lax.optimization_barrier(
         (third_arrived, first_part, tokens_grad, dense_weight_grad)
     )
@@ -1036,6 +1059,7 @@
         functools.partial(second_end_body, hidden=hidden, ratio=ratio), "second_end", [second_arrived],
         (part, inner_dim), (part, hidden), (part, LANES),
     )
+    up_grad, down_grad, *third_arrived = lax.optimization_barrier((up_grad, down_grad, *third_arrived))
     qkv_grad, third_vectors = end(
         functools.partial(third_end_body, hidden=hidden), "third_end", third_arrived,
         (part, 3 * hidden), (part, LANES),

time: 367 us -> 362 us (0.986)
  waiting for transfers between devices: 55 us -> 48.6 us
    ppermute x6, waiting for transfers between devices: 10.7 us -> 1.39 us  [permutes(): parts.append(lax.ppermute(part, axes, pairs))]
    all_to_all x2, waiting for transfers between devices: 6.84 us -> 14 us  [exchange(): lax.all_to_all(value, self.stages[stage], split_axis=0, concat_axis=0, ti...]
    all_to_all x1, waiting for transfers between devices: 4.28 us -> 0.01 us  [local(): lax.all_to_all(jnp.broadcast_to(small, (count,) + small.shape), axes, spl...]
  transfers between devices with their start and end apart: 20 -> 20, of which waited for: 6 -> 6; matrix products, arithmetic and copies ran while one was open for 9% -> 9% of each run, Pallas kernels for 46% -> 47%
where the time goes in v5:
time: 362 us; the launch traced here: 356 us
  Pallas kernels  171 us (47%)
  starting transfers between devices  48.8 us (13%)
  waiting for transfers between devices  48.6 us (13%)
  local copies, waits for them, and re-layouts  33.7 us (9%)
  blocking collectives  31.8 us (9%)
  between operations  14.3 us (4%)
  other arithmetic  7.15 us (2%)
    all_to_all x2, blocking collectives, gather(): lax.all_to_all(copies, self.stages[stage], split_axis=0, concat_axis=0, t...  31.8 us
    pallas_call x1, Pallas kernels, local(): pl.pallas_call(functools.partial(up_grad_body, sums=sums, ratio=ratio), g...  30.7 us
    pallas_call x1, Pallas kernels, local(): pl.pallas_call(attention_grad_body, grid=(micro, blocks), in_specs=[pl.Bl...  25.8 us
    all_to_all x1, waiting for transfers between devices, gather(): lax.all_to_all(copies, self.stages[stage], split_axis=0, concat_axis=0, t...  24.8 us
    pallas_call x1, Pallas kernels, local(): pl.pallas_call(forward_body, grid=(ratio,), in_specs=[full_spec, full_spe...  24.5 us
    pallas_call x1, Pallas kernels, local(): pl.pallas_call(attention_body, grid=(micro, blocks), in_specs=[pl.BlockSp...  20.9 us
    pallas_call x1, Pallas kernels, local(): pl.pallas_call(functools.partial(down_grad_body, ratio=ratio, place=layou...  19.2 us
    all_to_all x2, waiting for transfers between devices, exchange(): lax.all_to_all(value, self.stages[stage], split_axis=0, concat_axis=0, ti...  14 us
  transfers between devices with their start and end apart: 20, of which 6 were waited for; matrix products, arithmetic and copies ran while one was open for 9% of the time, Pallas kernels for 47%

profile of v5, /device:TPU:0, one launch (start us, length us, event | category | flops | bytes accessed | tf_op | source)
XLA Modules:
  0.0 355.7 jit_solution(9427683820367524750)
XLA Ops:
  11.8 3.0 collective-permute-start
  15.9 24.9 %all_to_all.42 = bf16[4,24,2432]{2,1,0:T(8,128)(2,1)S(1)} all-to-all(bf16[4,24,2432]{2,1,0:T(8,128)(2,1)S(1)} %broadcast_in_dim.97), channel_id=1, replica_groups=mesh['z'=4,'x'=2,'y'=2,'core'=2] {'z'}, dimensions={0} | all-to-all | bytes 933888 | tf_op jit(solution)/shard_map/all_to_all | solution.py:119
  44.6 4.1 %all-to-all-start.1 = ((bf16[4,4,24,2432]{3,2,1,0:T(8,128)(2,1)}), bf16[4,4,24,2432]{3,2,1,0:T(8,128)(2,1)S(1)}, u32[]{:S(2)}, u32[]{:S(2)}) async-start(bf16[4,4,24,2432]{3,2,1,0:T(8,128)(2,1)} %broadcast_in_dim.98), calls=%async_computation.1 | async-start | bytes 3735552 | tf_op jit(solution)/shard_map/all_to_all | solution.py:119
  52.1 24.8 %all-to-all-done.1 = bf16[4,4,24,2432]{3,2,1,0:T(8,128)(2,1)S(1)} async-done(((bf16[4,4,24,2432]{3,2,1,0:T(8,128)(2,1)}), bf16[4,4,24,2432]{3,2,1,0:T(8,128)(2,1)S(1)}, u32[]{:S(2)}, u32[]{:S(2)}) %all-to-all-start.1) | async-done | bytes 1867808 | tf_op jit(solution)/shard_map/all_to_all | solution.py:119
  77.4 6.9 %all_to_all.43 = bf16[2,4,4,24,2432]{4,3,1,2,0:T(8,128)(2,1)S(1)} all-to-all(bf16[2,4,4,24,2432]{4,3,1,2,0:T(8,128)(2,1)S(1)} %broadcast_in_dim.99), channel_id=1, replica_groups=mesh['z'=4,'x'=2,'y'=2,'core'=2] {'core'}, dimensions={0} | all-to-all | bytes 7471104 | tf_op jit(solution)/shard_map/all_to_all | solution.py:119
  86.4 20.9 %attention.1 = (bf16[1024,768]{1,0:T(8,128)(2,1)}, bf16[1024,768]{1,0:T(8,128)(2,1)}, bf16[1024,768]{1,0:T(8,128)(2,1)}, bf16[1024,768]{1,0:T(8,128)(2,1)}, f32[6,8,512]{2,1,0:T(8,128)}) custom-call(bf16[1024,768]{1,0:T(8,128)(2,1)} %tokens.5, s32[2,512,1]{2,1,0:T(8,128)} %copy.127.seg_column, s32[2,1,512]{2,1,0:T(1,128)} %broadcast_in_dim.87.seg_row, ...), custom_call_target="tpu_custom_call" | custom-call | flops 1000000 | bytes 100000 | tf_op jit(solution)/shard_map/attention/pallas_call | solution.py:851
  119.1 24.5 %forward.1 = (f32[1024,768]{1,0:T(8,128)}, bf16[1024,768]{1,0:T(8,128)(2,1)}, bf16[1024,3072]{1,0:T(8,128)(2,1)}, bf16[1024,3072]{1,0:T(8,128)(2,1)}, f32[1024,7...) custom-call(bf16[1024,768]{1,0:T(8,128)(2,1)} %tokens.5, bf16[1024,768]{1,0:T(8,128)(2,1)} %get-tuple-element.100.context, ...), custom_call_target="tpu_custom_call" | custom-call | flops 1000000 | bytes 100000 | tf_op jit(solution)/shard_map/forward/pallas_call | solution.py:873
  143.6 5.8 %select.27 = bf16[1536,768]{1,0:T(8,128)(2,1)} custom-call(s32[1536,1]{1,0:T(8,128)} %select_n.98.index, bf16[1024,768]{1,0:T(8,128)(2,1)} %get-tuple-element.101.source.outputs), custom_call_target="tpu_custom_call" | custom-call | flops 1000000 | bytes 100000 | tf_op jit(solution)/shard_map/select/pallas_call | solution.py:894
  149.4 5.6 %student.3 = (f32[8,14]{1,0:T(8,128)}, bf16[1024,128]{1,0:T(8,128)(2,1)}, f32[24,128]{1,0:T(8,128)}) custom-call(f32[1024,128]{1,0:T(8,128)} %get-tuple-element.102.student_rows, s32[1024,1]{1,0:T(8,128)} %bitcast.92, f32[1,128]{1,0:T(1,128)} %bitcast.100, f32[128,128]{1,0:T(8,128)} %dense_weight.3, f32[1,128]{1,0:T(1,128)} %bitcast.98, ...), custom_call_target="tpu_custom_call" | custom-call | flops 1000000 | bytes 100000 | tf_op jit(solution)/shard_map/student/pallas_call | solution.py:906
  156.3 12.9 %all-to-all-start.3 = ((bf16[8,192,768]{2,1,0:T(8,128)(2,1)}), bf16[8,192,768]{2,1,0:T(8,128)(2,1)S(1)}, u32[]{:S(2)}, u32[]{:S(2)}) async-start(bf16[8,192,768]{2,1,0:T(8,128)(2,1)} %bitcast.85), calls=%async_computation.3 | async-start | bytes 4718592 | tf_op jit(solution)/shard_map/all_to_all | solution.py:921
  170.6 19.2 %down_grad.1 = (f32[1024,768]{1,0:T(8,128)}, bf16[1024,768]{1,0:T(8,128)(2,1)}, bf16[32,24,3328]{2,1,0:T(8,128)(2,1)}) custom-call(s32[1024,1]{1,0:T(8,128)} %compare_select_fusion.slot, bf16[1024,128]{1,0:T(8,128)(2,1)} %get-tuple-element.106.student_grad, bf16[768,7040]{1,0:T(8,128)(2,1)} %all-gather.2.cloned.1.call-done.out_weight.up.down.student, ...), custom_call_target="tpu_custom_call" | custom-call | flops 1000000 | bytes 100000 | tf_op jit(solution)/shard_map/down_grad/pallas_call | solution.py:925
  189.9 30.7 %up_grad.1 = (f32[1024,768]{1,0:T(8,128)}, bf16[1024,768]{1,0:T(8,128)(2,1)}, bf16[16,24,3968]{2,1,0:T(8,128)(2,1)}, bf16[16,24,3968]{2,1,0:T(8,128)(2,1)}) custom-call(s32[1]{0:T(128)} %bitcast.core, bf16[1024,768]{1,0:T(8,128)(2,1)} %get-tuple-element.113.grad_down, f32[1024,768]{1,0:T(8,128)} %get-tuple-element.114.grad_second, ...), custom_call_target="tpu_custom_call" | custom-call | flops 1000000 | bytes 100000 | tf_op jit(solution)/shard_map/up_grad/pallas_call | solution.py:950
  220.6 5.9 %collective-permute-done.4 = bf16[16,24,3968]{2,1,0:T(8,128)(2,1)} collective-permute-done((bf16[16,24,3968]{2,1,0:T(8,128)(2,1)}, bf16[16,24,3968]{2,1,0:T(8,128)(2,1)}, u32[]{:S(2)}, u32[]{:S(2)}) %collective-permute-start.4) | collective-permute-done | bytes 3047456 | tf_op jit(solution)/shard_map/ppermute | solution.py:261
  226.4 5.1 %add.224 = bf16[384,3968]{1,0:T(8,128)(2,1)} custom-call(bf16[384,3968]{1,0:T(8,128)(2,1)} %bitcast.89, bf16[384,3968]{1,0:T(8,128)(2,1)} %bitcast.29.right), custom_call_target="tpu_custom_call" | custom-call | flops 1000000 | bytes 100000 | tf_op jit(solution)/shard_map/add/pallas_call | solution.py:175
  232.9 4.3 %all-to-all-start.4 = ((bf16[4,4,24,3968]{3,2,1,0:T(8,128)(2,1)}), bf16[4,4,24,3968]{3,2,1,0:T(8,128)(2,1)S(1)}, u32[]{:S(2)}, u32[]{:S(2)}) async-start(bf16[4,4,24,3968]{3,2,1,0:T(8,128)(2,1)} %bitcast.83), calls=%async_computation.4 | async-start | bytes 6094848 | tf_op jit(solution)/shard_map/all_to_all | solution.py:112
  237.2 25.8 %attention_grad.1.grads = bf16[3,1024,768]{2,1,0:T(8,128)(2,1)} custom-call(bf16[1024,768]{1,0:T(8,128)(2,1)} %get-tuple-element.124.branch, s32[2,512,1]{2,1,0:T(8,128)} %copy.127.seg_column, s32[2,1,512]{2,1,0:T(1,128)} %broadcast_in_dim.87.seg_row, bf16[1024,768]{1,0:T(8,128)(2,1)} %get-tuple-element.125.query, bf16[1024,768]{1,0:T(8,128)(2,1)} %get-tuple-element.126.key, ...), custom_call_target="tpu_custom_call" | custom-call | flops 1000000 | bytes 100000 | tf_op jit(solution)/shard_map/attention_grad/pallas_call | solution.py:972
  263.1 8.6 %qkv_grad.1 = (bf16[16,24,2432]{2,1,0:T(8,128)(2,1)}, bf16[16,24,2432]{2,1,0:T(8,128)(2,1)}) custom-call(s32[1]{0:T(128)} %bitcast.core, bf16[1024,768]{1,0:T(8,128)(2,1)} %tokens.5, bf16[3,1024,768]{2,1,0:T(8,128)(2,1)} %attention_grad.1.grads), custom_call_target="tpu_custom_call" | custom-call | flops 1000000 | bytes 100000 | tf_op jit(solution)/shard_map/qkv_grad/pallas_call | solution.py:989
  271.7 6.8 %all-to-all-done.4 = bf16[4,4,24,3968]{3,2,1,0:T(8,128)(2,1)S(1)} async-done(((bf16[4,4,24,3968]{3,2,1,0:T(8,128)(2,1)}), bf16[4,4,24,3968]{3,2,1,0:T(8,128)(2,1)S(1)}, u32[]{:S(2)}, u32[]{:S(2)}) %all-to-all-start.4) | async-done | bytes 3047456 | tf_op jit(solution)/shard_map/all_to_all | solution.py:112
  279.3 4.7 %all-to-all-start.5 = ((f32[32,24,128]{2,1,0:T(8,128)}), f32[32,24,128]{2,1,0:T(8,128)S(1)}, u32[]{:S(2)}, u32[]{:S(2)}) async-start(f32[32,24,128]{2,1,0:T(8,128)} %broadcast_in_dim.104), calls=%async_computation.6 | async-start | bytes 786432 | tf_op jit(solution)/shard_map/all_to_all | solution.py:1001
  284.1 4.2 %add.225 = bf16[384,2432]{1,0:T(8,128)(2,1)} custom-call(bf16[384,2432]{1,0:T(8,128)(2,1)} %bitcast.93, bf16[384,2432]{1,0:T(8,128)(2,1)} %bitcast.35.right), custom_call_target="tpu_custom_call" | custom-call | flops 1000000 | bytes 100000 | tf_op jit(solution)/shard_map/add/pallas_call | solution.py:175
  295.7 9.3 %token_grad.1 = bf16[1024,768]{1,0:T(8,128)(2,1)} custom-call(bf16[3,1024,768]{2,1,0:T(8,128)(2,1)} %attention_grad.1.grads, bf16[768,2432]{1,0:T(8,128)(2,1)} %bitcast.81, f32[1024,768]{1,0:T(8,128)} %get-tuple-element.142.grad_first), custom_call_target="tpu_custom_call" | custom-call | flops 1000000 | bytes 100000 | tf_op jit(solution)/shard_map/token_grad/pallas_call | solution.py:1012
  307.9 4.3 %all-to-all-start.6 = ((bf16[4,1,24,3968]{3,2,1,0:T(8,128)(2,1)}), bf16[4,1,24,3968]{3,2,1,0:T(8,128)(2,1)S(1)}, u32[]{:S(2)}, u32[]{:S(2)}) async-start(bf16[4,1,24,3968]{3,2,1,0:T(8,128)(2,1)} %bitcast.90), calls=%async_computation.8 | async-start | bytes 1523712 | tf_op jit(solution)/shard_map/all_to_all | solution.py:112
  329.7 7.1 %all-to-all-done.6.refs_0_ = bf16[4,1,24,3968]{3,2,1,0:T(8,128)(2,1)S(1)} async-done(((bf16[4,1,24,3968]{3,2,1,0:T(8,128)(2,1)}), bf16[4,1,24,3968]{3,2,1,0:T(8,128)(2,1)S(1)}, u32[]{:S(2)}, u32[]{:S(2)}) %all-to-all-start.6) | async-done | bytes 761888 | tf_op jit(solution)/shard_map/all_to_all | solution.py:112
  337.7 3.0 second_end.1
  (140 shorter events, 68.9 us)
Async XLA Ops:
  7.2 111.9 %all-gather.2.cloned.1.call-start = ((), (), s32[]{:S(2)}) async-start(), calls=%async_computation.9 | async-start | bytes 11151360 | tf_op jit(solution)/shard_map/all_gather | solution.py:802
  11.8 31.5 %collective-permute-start = (bf16[4,192,768]{2,1,0:T(8,128)(2,1)S(1)}, bf16[4,192,768]{2,1,0:T(8,128)(2,1)}, u32[]{:S(2)}, u32[]{:S(2)}) collective-permute-start(bf16[4,192,768]{2,1,0:T(8,128)(2,1)S(1)} %get-tuple-element.298), channel_id=1, source_target_pairs={{0,4},{4,0},{1,5},{5,1},{2,6},{6,2},{3,7},{7,3},{8,12},{12,8},{9,1... | collective-permute-start | bytes 3538952 | tf_op jit(solution)/shard_map/ppermute | solution.py:202
  44.6 7.3 %copy-start.12 = (s32[2,4]{1,0:T(2,128)S(1)}, s32[2,4]{1,0:T(2,128)}, u32[]{:S(2)}) copy-start(s32[2,4]{1,0:T(2,128)} %param.28) | copy-start | bytes 100
  44.6 32.3 %all-to-all-start.1 = ((bf16[4,4,24,2432]{3,2,1,0:T(8,128)(2,1)}), bf16[4,4,24,2432]{3,2,1,0:T(8,128)(2,1)S(1)}, u32[]{:S(2)}, u32[]{:S(2)}) async-start(bf16[4,4,24,2432]{3,2,1,0:T(8,128)(2,1)} %broadcast_in_dim.98), calls=%async_computation.1 | async-start | bytes 3735552 | tf_op jit(solution)/shard_map/all_to_all | solution.py:119
  108.8 9.5 %copy-start.10 = (f32[128,14]{0,1:T(8,128)S(1)}, f32[128,14]{0,1:T(8,128)}, u32[]{:S(2)}) copy-start(f32[128,14]{0,1:T(8,128)} %param.50) | copy-start | bytes 21508
  110.0 45.0 %collective-permute-start.1 = (bf16[384,768]{1,0:T(8,128)(2,1)}, bf16[384,768]{1,0:T(8,128)(2,1)S(1)}, u32[]{:S(2)}, u32[]{:S(2)}) collective-permute-start(bf16[384,768]{1,0:T(8,128)(2,1)} %get-tuple-element.296), channel_id=1, source_target_pairs={{0,8},{8,16},{16,24},{24,0},{1,9},{9,17},{17,25},{25,1},{2,10},{10... | collective-permute-start | bytes 1769480 | tf_op jit(solution)/shard_map/ppermute | solution.py:216
  111.5 43.5 %collective-permute-start.2 = (bf16[384,768]{1,0:T(8,128)(2,1)S(1)}, bf16[384,768]{1,0:T(8,128)(2,1)S(1)}, u32[]{:S(2)}, u32[]{:S(2)}) collective-permute-start(bf16[384,768]{1,0:T(8,128)(2,1)S(1)} %get-tuple-element.295), channel_id=1, source_target_pairs={{0,16},{8,24},{16,0},{24,8},{1,17},{9,25},{17,1},{25,9},{2,18},{10... | collective-permute-start | bytes 1769480 | tf_op jit(solution)/shard_map/ppermute | solution.py:216
  113.9 41.1 %collective-permute-start.3 = (bf16[384,768]{1,0:T(8,128)(2,1)S(1)}, bf16[384,768]{1,0:T(8,128)(2,1)S(1)}, u32[]{:S(2)}, u32[]{:S(2)}) collective-permute-start(bf16[384,768]{1,0:T(8,128)(2,1)S(1)} %get-tuple-element.294), channel_id=1, source_target_pairs={{0,24},{8,0},{16,8},{24,16},{1,25},{9,1},{17,9},{25,17},{2,26},{10... | collective-permute-start | bytes 1769480 | tf_op jit(solution)/shard_map/ppermute | solution.py:216
  156.3 75.2 %all-to-all-start.3 = ((bf16[8,192,768]{2,1,0:T(8,128)(2,1)}), bf16[8,192,768]{2,1,0:T(8,128)(2,1)S(1)}, u32[]{:S(2)}, u32[]{:S(2)}) async-start(bf16[8,192,768]{2,1,0:T(8,128)(2,1)} %bitcast.85), calls=%async_computation.3 | async-start | bytes 4718592 | tf_op jit(solution)/shard_map/all_to_all | solution.py:921
  169.1 119.1 %reduce-scatter.3.cloned.1.call-start = ((), (), s32[]{:S(2)}) async-start(), calls=%async_computation.10 | async-start | bytes 5750784 | tf_op jit(solution)/shard_map/reduce_scatter | solution.py:132
  220.6 5.9 %collective-permute-start.4 = (bf16[16,24,3968]{2,1,0:T(8,128)(2,1)}, bf16[16,24,3968]{2,1,0:T(8,128)(2,1)}, u32[]{:S(2)}, u32[]{:S(2)}) collective-permute-start(bf16[16,24,3968]{2,1,0:T(8,128)(2,1)} %get-tuple-element.119), channel_id=1, source_target_pairs={{0,1},{1,0},{2,3},{3,2},{4,5},{5,4},{6,7},{7,6},{8,9},{9,8},{10,11... | collective-permute-start | bytes 9142280 | tf_op jit(solution)/shard_map/ppermute | solution.py:261
  232.9 45.6 %all-to-all-start.4 = ((bf16[4,4,24,3968]{3,2,1,0:T(8,128)(2,1)}), bf16[4,4,24,3968]{3,2,1,0:T(8,128)(2,1)S(1)}, u32[]{:S(2)}, u32[]{:S(2)}) async-start(bf16[4,4,24,3968]{3,2,1,0:T(8,128)(2,1)} %bitcast.83), calls=%async_computation.4 | async-start | bytes 6094848 | tf_op jit(solution)/shard_map/all_to_all | solution.py:112
  263.1 15.4 %copy-start.9 = (f32[24,128]{1,0:T(8,128)S(1)}, f32[24,128]{1,0:T(8,128)}, u32[]{:S(2)}) copy-start(f32[24,128]{1,0:T(8,128)} %get-tuple-element.139) | copy-start | bytes 36868
  278.5 5.6 %collective-permute-start.5 = (bf16[16,24,2432]{2,1,0:T(8,128)(2,1)}, bf16[16,24,2432]{2,1,0:T(8,128)(2,1)}, u32[]{:S(2)}, u32[]{:S(2)}) collective-permute-start(bf16[16,24,2432]{2,1,0:T(8,128)(2,1)} %get-tuple-element.134), channel_id=1, source_target_pairs={{0,1},{1,0},{2,3},{3,2},{4,5},{5,4},{6,7},{7,6},{8,9},{9,8},{10,11... | collective-permute-start | bytes 5603336 | tf_op jit(solution)/shard_map/ppermute | solution.py:261
  279.3 25.6 %all-to-all-start.5 = ((f32[32,24,128]{2,1,0:T(8,128)}), f32[32,24,128]{2,1,0:T(8,128)S(1)}, u32[]{:S(2)}, u32[]{:S(2)}) async-start(f32[32,24,128]{2,1,0:T(8,128)} %broadcast_in_dim.104), calls=%async_computation.6 | async-start | bytes 786432 | tf_op jit(solution)/shard_map/all_to_all | solution.py:1001
  284.0 34.7 %reduce-scatter.5.cloned.1.call-start = ((), (), s32[]{:S(2)}) async-start(), calls=%async_computation.11 | async-start | bytes 798720 | tf_op jit(solution)/shard_map/reduce_scatter | solution.py:135
  291.0 15.3 %collective-permute-start.6 = (bf16[4,24,2432]{2,1,0:T(8,128)(2,1)}, bf16[4,24,2432]{2,1,0:T(8,128)(2,1)}, u32[]{:S(2)}, u32[]{:S(2)}) collective-permute-start(bf16[4,24,2432]{2,1,0:T(8,128)(2,1)} %get-tuple-element.302), channel_id=1, source_target_pairs={{0,2},{2,4},{4,6},{6,0},{1,3},{3,5},{5,7},{7,1},{8,10},{10,12},{12... | collective-permute-start | bytes 1400840 | tf_op jit(solution)/shard_map/ppermute | solution.py:145
  292.8 25.9 %collective-permute-start.7 = (bf16[4,24,2432]{2,1,0:T(8,128)(2,1)}, bf16[4,24,2432]{2,1,0:T(8,128)(2,1)}, u32[]{:S(2)}, u32[]{:S(2)}) collective-permute-start(bf16[4,24,2432]{2,1,0:T(8,128)(2,1)} %get-tuple-element.301), channel_id=1, source_target_pairs={{0,4},{2,6},{4,0},{6,2},{1,5},{3,7},{5,1},{7,3},{8,12},{10,14},{12... | collective-permute-start | bytes 1400840 | tf_op jit(solution)/shard_map/ppermute | solution.py:145
  294.2 24.4 %collective-permute-start.8 = (bf16[4,24,2432]{2,1,0:T(8,128)(2,1)}, bf16[4,24,2432]{2,1,0:T(8,128)(2,1)}, u32[]{:S(2)}, u32[]{:S(2)}) collective-permute-start(bf16[4,24,2432]{2,1,0:T(8,128)(2,1)} %get-tuple-element.300), channel_id=1, source_target_pairs={{0,6},{2,0},{4,2},{6,4},{1,7},{3,1},{5,3},{7,5},{8,14},{10,8},{12,... | collective-permute-start | bytes 1400840 | tf_op jit(solution)/shard_map/ppermute | solution.py:145
  307.9 28.9 %all-to-all-start.6 = ((bf16[4,1,24,3968]{3,2,1,0:T(8,128)(2,1)}), bf16[4,1,24,3968]{3,2,1,0:T(8,128)(2,1)S(1)}, u32[]{:S(2)}, u32[]{:S(2)}) async-start(bf16[4,1,24,3968]{3,2,1,0:T(8,128)(2,1)} %bitcast.90), calls=%async_computation.8 | async-start | bytes 1523712 | tf_op jit(solution)/shard_map/all_to_all | solution.py:112
  318.7 28.9 %copy-start.1 = (bf16[8,192,768]{2,1,0:T(8,128)(2,1)S(1)}, bf16[8,192,768]{2,1,0:T(8,128)(2,1)}, u32[]{:S(2)}) copy-start(bf16[8,192,768]{2,1,0:T(8,128)(2,1)} %copy-done) | copy-start | bytes 7077892
  321.3 21.7 %collective-permute-start.10 = (bf16[1,24,2432]{2,1,0:T(8,128)(2,1)}, bf16[1,24,2432]{2,1,0:T(8,128)(2,1)S(1)}, u32[]{:S(2)}, u32[]{:S(2)}) collective-permute-start(bf16[1,24,2432]{2,1,0:T(8,128)(2,1)} %get-tuple-element.305), channel_id=1, source_target_pairs={{0,16},{8,24},{16,0},{24,8},{1,17},{9,25},{17,1},{25,9},{2,18},{10... | collective-permute-start | bytes 350216 | tf_op jit(solution)/shard_map/ppermute | solution.py:145
  324.2 18.8 %collective-permute-start.11 = (bf16[1,24,2432]{2,1,0:T(8,128)(2,1)S(1)}, bf16[1,24,2432]{2,1,0:T(8,128)(2,1)}, u32[]{:S(2)}, u32[]{:S(2)}) collective-permute-start(bf16[1,24,2432]{2,1,0:T(8,128)(2,1)S(1)} %get-tuple-element.304), channel_id=1, source_target_pairs={{0,24},{8,0},{16,8},{24,16},{1,25},{9,1},{17,9},{25,17},{2,26},{10... | collective-permute-start | bytes 350216 | tf_op jit(solution)/shard_map/ppermute | solution.py:145
  325.7 17.4 %collective-permute-start.9 = (bf16[1,24,2432]{2,1,0:T(8,128)(2,1)S(1)}, bf16[1,24,2432]{2,1,0:T(8,128)(2,1)}, u32[]{:S(2)}, u32[]{:S(2)}) collective-permute-start(bf16[1,24,2432]{2,1,0:T(8,128)(2,1)S(1)} %get-tuple-element.306), channel_id=1, source_target_pairs={{0,8},{8,16},{16,24},{24,0},{1,9},{9,17},{17,25},{25,1},{2,10},{10... | collective-permute-start | bytes 350216 | tf_op jit(solution)/shard_map/ppermute | solution.py:145
  (19 other events, 73.5 us)
Sparse Core Ops, SparseCore 0:
  10.9 100.6 all-gather.1
  190.0 79.4 reduce-scatter.2
  288.4 23.5 reduce-scatter.4
